TPU v7x, 32 devices: a whole 2x2x4 slice. The times are simulated.
32 devices in a mesh: row: 4 (over y, x), col: 8 (over z, core).
Axes of the slice: x: 2, y: 2, z: 4, core: 2. Of those that a mesh axis runs over, the one named last changes fastest.
Arguments:
- rhs: bfloat16 [1024, 2, 4096], P('col', None, 'row'), may hold values from -6 to 6
- solved: bfloat16 [1024, 49152], P(None, 'col'), may hold values from -6 to 6
- panel: bfloat16 [2, 4096, 49152], P(None, 'row', 'col'), may hold values from -0.02734375 to 0.02734375
- inverse: bfloat16 [2, 4096, 4096], P(None, 'row'), as said below
- link: bfloat16 [4096, 4096], P('row'), may hold values from -0.09375 to 0.09375
Outputs:
- solution: bfloat16 [1024, 2, 4096], P('col', None, 'row')
Inputs may be any that keep to these rules, and one draw needn't show every extreme that they name: Each inverse[b] is upper triangular with diagonal entries between 0.6 and 1.4.
All inputs are finite; a program needn't handle non-finite values.
Results may differ from a plain program's by a relative error of at most 0.0056.
Values may be sent and summed in bfloat16 or wider, within the bound.
No kernel may reach another device: no remote copies, remote signals or barrier semaphores. Data moves between devices by JAX's collectives and lax.ppermute only.
A program may use at most 128 MiB of HBM per device.

v0:
```python
import functools

import jax
import jax.numpy as jnp
from jax import lax
from jax.experimental import pallas as pl
from jax.experimental.pallas import tpu as pltpu
from jax.sharding import PartitionSpec as P


F32, BF16 = jnp.float32, jnp.bfloat16
AHEAD = 3
PIECES = 4
LIMIT = 8 << 20


def contract_last(a, b):
    return lax.dot_general(a, b, (((1,), (1,)), ((), ())), preferred_element_type=F32)


def tile_of(size, most):
    while size % most:
        most //= 2
    return most


def in_hbm(array):
    return pltpu.with_memory_space_constraint(array, pltpu.HBM)


def partial_kernel(cfg, *refs):
    block, half, tile, load_p, load_x, group, following, ordered, blocks, extras, chips = cfg
    refs = list(refs)
    place, solved = refs.pop(0)[0], refs.pop(0)
    x = None if load_x else refs.pop(0)
    held = [refs.pop(0) for _ in range(blocks)]
    panel = held[0]
    for _ in range(ordered):
        refs.pop(0)
    wanted = [refs.pop(0) for _ in extras]
    send, keep = refs.pop(0), refs.pop(0)
    if load_p:
        held = [refs.pop(0)]
    upcoming = refs.pop(0) if following else None
    fetched = [refs.pop(0) for _ in extras]
    if load_x:
        x = refs.pop(0)
    acc, sems = refs
    depth = solved.shape[1]
    piece = depth // PIECES
    per = held[0].shape[0] // tile
    tiles = per * len(held)
    count = len(group)
    chip, core = lax.rem(place, 2 * chips) // 2, lax.rem(place, 2)
    used = [0]

    def copy(source, target):
        used[0] += 1
        return pltpu.make_async_copy(source, target, sems.at[used[0] - 1])

    def rows_copy(offsets, target, at, columns):
        parity = 1 - core if at < len(offsets) else core
        start = ((chip ^ offsets[at % len(offsets)]) * 2 + parity) * half
        return copy(
            solved.at[pl.ds(pl.multiple_of(start, half), half), columns],
            target.at[pl.ds(at * half, half), columns],
        )

    def panel_copy(n, columns):
        rows = pl.ds(n * tile, tile)
        return copy(panel.at[block, rows, columns], held[0].at[rows, columns])

    units = []
    if load_x or load_p:
        for j in range(PIECES):
            columns = pl.ds(j * piece, piece)
            unit = [rows_copy(group, x, s, columns) for s in range(2 * count)] if load_x else []
            units.append(unit + ([panel_copy(0, columns)] if load_p else []))
    if load_p:
        units += [[panel_copy(n, slice(None))] for n in range(1, tiles)]
    units += [[rows_copy(following, upcoming, s, slice(None))] for s in range(2 * len(following))]
    for (layer, low), source, target in zip(extras, wanted, fetched):
        step = target.shape[0] // PIECES
        for j in range(PIECES):
            rows = pl.ds(low + j * step, step)
            part = source.at[rows] if layer is None else source.at[layer, rows]
            units.append([copy(part, target.at[pl.ds(j * step, step)])])
    ahead = AHEAD if load_p else len(units)
    begun, ended = [0], [0]

    def begin():
        while begun[0] < min(ended[0] + ahead, len(units)):
            for c in units[begun[0]]:
                c.start()
            begun[0] += 1

    def arrive():
        begin()
        for c in units[ended[0]]:
            c.wait()
        ended[0] += 1
        begin()

    begin()

    def put(d, n):
        at = pl.ds(n * tile, tile)
        for c in range(count):
            send[c, :, at] = d[c * half : (c + 1) * half].astype(send.dtype)
            keep[c, :, at] = d[(count + c) * half : (count + c + 1) * half]

    def step(n):
        put(contract_last(x[...], held[n // per][pl.ds(n % per * tile, tile), :]), n)

    first = 0
    if load_x or load_p:
        for j in range(PIECES):
            arrive()

            @pl.when(place >= 0)
            def _(j=j):
                columns = pl.ds(j * piece, piece)
                d = contract_last(x[:, columns], held[0][pl.ds(0, tile), columns])
                if j > 0:
                    d = acc[...] + d
                if j < PIECES - 1:
                    acc[...] = d
                else:
                    put(d, 0)

        first = 1
    for n in range(first, tiles):
        if load_p:
            arrive()

        @pl.when(place >= 0)
        def _(n=n):
            step(n)

    while ended[0] < len(units):
        arrive()


def partial_sums(solved, x, panel, block, orders, place, group, following, half, chips, extras):
    load_x, load_p = x is None, not isinstance(panel, list)
    panels = [in_hbm(panel)] if load_p else panel
    depth = solved.shape[1]
    width = panel.shape[1] if load_p else sum(part.shape[0] for part in panel)
    count = len(group)
    rows = 2 * count * half
    tile = tile_of(width // 2, 256)
    hbm, vmem = pl.BlockSpec(memory_space=pltpu.HBM), pl.BlockSpec(memory_space=pltpu.VMEM)
    operands = [place, in_hbm(solved)]
    in_specs = [pl.BlockSpec(memory_space=pltpu.SMEM), hbm]
    if not load_x:
        operands.append(x)
        in_specs.append(vmem)
    operands += panels
    in_specs += [hbm if load_p else vmem] * len(panels)
    operands += orders
    in_specs += [pl.BlockSpec(memory_space=pl.ANY)] * len(orders)
    operands += [in_hbm(array) for array, *_ in extras]
    in_specs += [hbm] * len(extras)
    shapes = [
        jax.ShapeDtypeStruct((count, half, width), BF16),
        jax.ShapeDtypeStruct((count, half, width), F32),
    ]
    if load_p:
        shapes.append(jax.ShapeDtypeStruct((width, depth), panel.dtype))
    if following:
        shapes.append(jax.ShapeDtypeStruct((2 * len(following) * half, depth), solved.dtype))
    shapes += [
        jax.ShapeDtypeStruct((size, array.shape[-1]), array.dtype) for array, _, _, size in extras
    ]
    scratch = [pltpu.VMEM((rows, depth), solved.dtype)] if load_x else []
    scratch.append(pltpu.VMEM((rows, tile), F32))
    copies = PIECES * (2 * count + 1) + width // tile + 2 * len(following) + PIECES * len(extras)
    scratch.append(pltpu.SemaphoreType.DMA((copies,)))
    cfg = (
        block, half, tile, load_p, load_x, tuple(group), tuple(following), len(orders),
        len(panels), tuple((layer, low) for _, layer, low, _ in extras), chips,
    )
    out = pl.pallas_call(
        functools.partial(partial_kernel, cfg),
        in_specs=in_specs,
        out_specs=[vmem] * len(shapes),
        out_shape=shapes,
        scratch_shapes=scratch,
        compiler_params=pltpu.CompilerParams(vmem_limit_bytes=LIMIT),
        cost_estimate=pl.CostEstimate(
            flops=2 * rows * width * depth,
            bytes_accessed=2 * depth * (rows + width),
            transcendentals=0,
        ),
    )(*operands)
    out = list(out)
    send, keep = out.pop(0), out.pop(0)
    held = [out.pop(0)] if load_p else panel
    return send, keep, held, out.pop(0) if following else None, out


def residual(b, rhs_ref, parts):
    total = parts[0][...].astype(F32)
    for part in parts[1:]:
        total += part[...].astype(F32)
    return rhs_ref[:, b, :].astype(F32) - total


def blocks_of(mine, members, width):
    return [
        pl.ds(pl.multiple_of((mine ^ offset) * width, width), width)
        for offset in range(members)
    ]


def solve_first_kernel(count, cols, place, rhs, *refs):
    parts, inverse, outs = refs[:count], refs[count], refs[count + 1 :]
    members, width = len(outs), rhs.shape[2]
    at = blocks_of(place[0] // cols, members, width)
    res = residual(0, rhs, parts).astype(BF16)
    for offset in range(members - 1, -1, -1):
        d = jnp.dot(res, inverse[:, at[offset]], preferred_element_type=F32)
        outs[offset][...] = d.astype(outs[offset].dtype)


def carry(firsts, link, at, offsets):
    total = None
    for first, offset in zip(firsts, offsets):
        d = contract_last(first[...], link[:, at[offset]])
        total = d if total is None else total + d
    return total


def carry_kernel(members, offsets, cols, place, *refs):
    firsts, link, out = refs[:-2], refs[-2], refs[-1]
    at = blocks_of(place[0] // cols, members, out.shape[1])
    out[...] = carry(firsts, link, at, offsets)


def solve_second_kernel(count, members, offsets, cols, place, rhs, *refs):
    parts, refs = refs[:count], refs[count:]
    early, refs = refs[0], refs[1:]
    firsts, refs = refs[: len(offsets)], refs[len(offsets) :]
    link, inverse, outs = refs[0], refs[1], refs[2:]
    at = blocks_of(place[0] // cols, members, rhs.shape[2])
    carried = early[...]
    if offsets:
        carried += carry(firsts, link, at, offsets)
    res = (residual(1, rhs, parts) - carried).astype(BF16)
    for offset in range(members - 1, -1, -1):
        d = jnp.dot(res, inverse[:, at[offset]], preferred_element_type=F32)
        outs[offset][...] = d.astype(outs[offset].dtype)


def solve(kernel, flops, place, rhs, parts, rest, members):
    half, _, width = rhs.shape
    vmem = pl.BlockSpec(memory_space=pltpu.VMEM)
    shapes = [
        jax.ShapeDtypeStruct((half, width), BF16 if offset else F32) for offset in range(members)
    ]
    return pl.pallas_call(
        kernel,
        in_specs=[pl.BlockSpec(memory_space=pltpu.SMEM)] + [vmem] * (1 + len(parts) + len(rest)),
        out_specs=[vmem] * members,
        out_shape=shapes,
        compiler_params=pltpu.CompilerParams(vmem_limit_bytes=LIMIT),
        cost_estimate=pl.CostEstimate(flops=flops, bytes_accessed=flops // half, transcendentals=0),
    )(place, rhs, *parts, *rest)


def result_kernel(first, *refs):
    parts, out = refs[:-1], refs[-1]
    total = parts[0][...].astype(F32)
    for part in parts[1:]:
        total += part[...].astype(F32)
    out[:, 0, :] = first[...]
    out[:, 1, :] = total.astype(BF16)


def plan_of(chips):
    plan = [(0, [o]) for o in range(chips - 1, -1, -1)]
    return plan + [(1, [o + 1, o] if chips > 1 else [o]) for o in range(max(chips - 2, 0), -1, -2)]


def local(members, chips, rhs, solved, panel, inverse, link):
    half, _, width = rhs.shape
    cols = 2 * chips
    place = lax.axis_index(("row", "col")).astype(jnp.int32)[None]

    def across_row(value, offset):
        return lax.ppermute(value, "row", [(i, i ^ offset) for i in range(members)])

    def across_col(value, offset):
        return lax.ppermute(value, "col", [(i, i ^ offset) for i in range(cols)])

    plan = plan_of(chips)
    last = len(plan) - 1

    extras = [[] for _ in plan]
    extras[chips].append(("inverse", inverse, 0, 0, width))
    piece = width // 2
    extras[max(0, chips - 2)].append(("low", panel, 1, 0, piece))
    extras[chips - 1].append(("high", panel, 1, piece, piece))
    extras[last].append(("link", link, None, 0, width))
    extras[last].append(("second", inverse, 1, 0, width))

    flops = 2 * half * width * width * members
    sums, sent, kept = [[], []], [], {}
    x, held = None, panel
    for n, (b, group) in enumerate(plan):
        if b == 1 and plan[n - 1][0] == 0:
            held = [kept["low"], kept["high"]]
        following = plan[n + 1][1] if n < last else []
        orders = sent[n - 2] if n >= 2 else []
        if n == last:
            parts = solve(
                functools.partial(solve_first_kernel, len(sums[0]), cols),
                flops, place, rhs, sums[0], [kept["inverse"]], members,
            )
            orders = sent[n - 1] + [parts[members > 1]]
        send, keep, held, x, got = partial_sums(
            solved, x, held, b, orders, place,
            group, following, half, chips, [e[1:] for e in extras[n]],
        )
        kept.update(zip([e[0] for e in extras[n]], got))
        other = across_col(send, 1)
        outgoing = []
        for at, offset in enumerate(group):
            if offset == 0:
                sums[b] += [keep[at], other[at]]
            else:
                outgoing.append((keep[at] + other[at].astype(F32)).astype(BF16))
                sums[b].append(across_col(outgoing[-1], 2 * offset))
        sent.append(outgoing)

    total = parts[0]
    for offset in range(1, members):
        total += across_row(parts[offset], offset).astype(F32)
    first = total.astype(BF16)
    firsts = [first] + [across_row(first, o) for o in range(1, members)]
    early = sorted({0, members // 2 if members > 2 else 0})
    late = [o for o in range(members) if o not in early]
    vmem = pl.BlockSpec(memory_space=pltpu.VMEM)
    carried = pl.pallas_call(
        functools.partial(carry_kernel, members, early, cols),
        in_specs=[pl.BlockSpec(memory_space=pltpu.SMEM)] + [vmem] * (1 + len(early)),
        out_specs=vmem,
        out_shape=jax.ShapeDtypeStruct((half, width), F32),
        name="carry",
        compiler_params=pltpu.CompilerParams(vmem_limit_bytes=LIMIT),
        cost_estimate=pl.CostEstimate(
            flops=2 * half * width * width, bytes_accessed=width * width, transcendentals=0
        ),
    )(place, *[firsts[o] for o in early], kept["link"])
    parts = solve(
        functools.partial(solve_second_kernel, len(sums[1]), members, late, cols),
        2 * flops, place, rhs, sums[1],
        [carried] + [firsts[o] for o in late] + [kept["link"], kept["second"]], members,
    )
    arrived = [across_row(parts[offset], offset) for offset in range(1, members)]
    return pl.pallas_call(
        result_kernel,
        out_shape=jax.ShapeDtypeStruct(rhs.shape, rhs.dtype),
        name="result",
        compiler_params=pltpu.CompilerParams(vmem_limit_bytes=LIMIT),
    )(first, parts[0], *arrived)


def solution(mesh):
    members, chips = mesh.shape["row"], mesh.shape["col"] // 2

    def body(*arrays):
        return local(members, chips, *arrays)

    return jax.shard_map(
        body,
        mesh=mesh,
        in_specs=(
            P("col", None, "row"),
            P(None, "col"),
            P(None, "row", "col"),
            P(None, "row", None),
            P("row", None),
        ),
        out_specs=P("col", None, "row"),
        check_vma=False,
    )
```

profile of v0, /device:TPU:0, one launch (start us, length us, event | category | flops | bytes accessed | tf_op | source)
XLA Modules:
  0.0 111.9 jit_solution(12787732621313952201)
XLA Ops:
  0.0 7.2 %shard_map.55 = (bf16[1,128,1024]{2,1,0:T(8,128)(2,1)S(1)}, f32[1,128,1024]{2,1,0:T(8,128)S(1)}, bf16[1024,6144]{1,0:T(8,128)(2,1)S(1)}, bf16[256,6144]{1,0:T(8,128)(2,1)S(1)}) custom-call(s32[1]{0:T(128)} %bitcast.refs_0_.place, bf16[1024,6144]{1,0:T(8,128)(2,1)} %refs_1_.11, bf16[2,1024,6144]{2,1,0:T(8,128)(2,1)} %refs_5_.3), custom_call_target="tpu_custom_call" | custom-call | flops 3221225472 | bytes 15728640 | tf_op jit(solution)/shard_map/pallas_call | solution.py:183
  7.2 0.6 collective-permute-start
  7.7 3.6 %shard_map.56 = (bf16[1,128,1024]{2,1,0:T(8,128)(2,1)S(1)}, f32[1,128,1024]{2,1,0:T(8,128)S(1)}, bf16[256,6144]{1,0:T(8,128)(2,1)S(1)}) custom-call(s32[1]{0:T(128)} %bitcast.refs_0_.place, bf16[1024,6144]{1,0:T(8,128)(2,1)} %refs_1_.11, bf16[256,6144]{1,0:T(8,128)(2,1)S(1)} %get-tuple-element.38.refs_2_, bf16[1024,6144]{1,0:T(8,128)(2,1)S(1)} %get-tuple-element.39.refs_3_), custom_call_target="tpu_custom_call" | custom-call | flops 3221225472 | bytes 15728640 | tf_op jit(solution)/shard_map/pallas_call | solution.py:183
  11.5 3.9 %shard_map.57 = (bf16[1,128,1024]{2,1,0:T(8,128)(2,1)S(1)}, f32[1,128,1024]{2,1,0:T(8,128)S(1)}, bf16[256,6144]{1,0:T(8,128)(2,1)S(1)}, bf16[512,6144]{1,0:T(8,128)(2,1)S(1)}) custom-call(s32[1]{0:T(128)} %bitcast.refs_0_.place, bf16[1024,6144]{1,0:T(8,128)(2,1)} %refs_1_.11, bf16[256,6144]{1,0:T(8,128)(2,1)S(1)} %get-tuple-element.42.refs_2_, ...), custom_call_target="tpu_custom_call" | custom-call | flops 3221225472 | bytes 15728640 | tf_op jit(solution)/shard_map/pallas_call | solution.py:183
  15.5 0.6 collective-permute-start.4
  16.1 4.9 %shard_map.58 = (bf16[1,128,1024]{2,1,0:T(8,128)(2,1)S(1)}, f32[1,128,1024]{2,1,0:T(8,128)S(1)}, bf16[512,6144]{1,0:T(8,128)(2,1)S(1)}, bf16[512,6144]{1,0:T(8,128)(2,1)S(1)}) custom-call(s32[1]{0:T(128)} %bitcast.refs_0_.place, bf16[1024,6144]{1,0:T(8,128)(2,1)} %refs_1_.11, bf16[256,6144]{1,0:T(8,128)(2,1)S(1)} %get-tuple-element.45.refs_2_, ...), custom_call_target="tpu_custom_call" | custom-call | flops 3221225472 | bytes 15728640 | tf_op jit(solution)/shard_map/pallas_call | solution.py:183
  21.0 7.2 %shard_map.59 = (bf16[2,128,1024]{2,1,0:T(8,128)(2,1)S(1)}, f32[2,128,1024]{2,1,0:T(8,128)S(1)}, bf16[512,6144]{1,0:T(8,128)(2,1)S(1)}, bf16[1024,4096]{1,0:T(8,128)(2,1)S(1)}) custom-call(s32[1]{0:T(128)} %bitcast.refs_0_.place, bf16[1024,6144]{1,0:T(8,128)(2,1)} %refs_1_.11, bf16[512,6144]{1,0:T(8,128)(2,1)S(1)} %get-tuple-element.48.refs_2_, ...), custom_call_target="tpu_custom_call" | custom-call | flops 6442450944 | bytes 18874368 | tf_op jit(solution)/shard_map/pallas_call | solution.py:183
  28.3 5.1 %collective-permute-start.1 = (bf16[128,1024]{1,0:T(8,128)(2,1)S(1)}, bf16[128,1024]{1,0:T(8,128)(2,1)S(1)}, u32[]{:S(2)}, u32[]{:S(2)}) collective-permute-start(bf16[128,1024]{1,0:T(8,128)(2,1)S(1)} %fusion.refs_4_), channel_id=1, source_target_pairs={{0,6},{1,7},{2,4},{3,5},{4,2},{5,3},{6,0},{7,1},{8,14},{9,15},{10,... | collective-permute-start | bytes 786440 | tf_op jit(solution)/shard_map/ppermute | solution.py:294
  33.4 0.6 collective-permute-start.5
  33.9 6.7 %collective-permute-done.1.refs_0_ = bf16[128,1024]{1,0:T(8,128)(2,1)S(1)} collective-permute-done((bf16[128,1024]{1,0:T(8,128)(2,1)S(1)}, bf16[128,1024]{1,0:T(8,128)(2,1)S(1)}, u32[]{:S(2)}, u32[]{:S(2)}) %collective-permute-start.1) | collective-permute-done | bytes 262176 | tf_op jit(solution)/shard_map/ppermute | solution.py:294
  40.7 15.3 %collective-permute-done.3.refs_1_ = bf16[128,1024]{1,0:T(8,128)(2,1)S(1)} collective-permute-done((bf16[128,1024]{1,0:T(8,128)(2,1)S(1)}, bf16[128,1024]{1,0:T(8,128)(2,1)S(1)}, u32[]{:S(2)}, u32[]{:S(2)}) %collective-permute-start.3) | collective-permute-done | bytes 262176 | tf_op jit(solution)/shard_map/ppermute | solution.py:294
  55.9 1.5 %shard_map.60 = (f32[128,1024]{1,0:T(8,128)S(1)}, bf16[128,1024]{1,0:T(8,128)(2,1)S(1)}, bf16[128,1024]{1,0:T(8,128)(2,1)S(1)}, bf16[128,1024]{1,0:T(8,128)(2,1)S(1)}) custom-call(s32[1]{0:T(128)} %bitcast.refs_0_.place, bf16[128,2,1024]{2,1,0:T(2,128)(2,1)S(1)} %copy-done, bf16[128,1024]{1,0:T(8,128)(2,1)S(1)} %collective-permute-done.1.refs_0_, ...), custom_call_target="tpu_custom_call" | custom-call | flops 1073741824 | bytes 8388608 | tf_op jit(solution)/shard_map/pallas_call | solution.py:261
  57.4 2.5 %collective-permute-start.9 = (bf16[128,1024]{1,0:T(8,128)(2,1)S(1)}, bf16[128,1024]{1,0:T(8,128)(2,1)S(1)}, u32[]{:S(2)}, u32[]{:S(2)}) collective-permute-start(bf16[128,1024]{1,0:T(8,128)(2,1)S(1)} %get-tuple-element.55), channel_id=1, source_target_pairs={{0,24},{8,16},{16,8},{24,0},{1,25},{9,17},{17,9},{25,1},{2,26},{10... | collective-permute-start | bytes 786440 | tf_op jit(solution)/shard_map/ppermute | solution.py:291
  59.9 0.5 collective-permute-start.8
  60.4 0.5 collective-permute-start.7
  61.1 7.2 %shard_map.61 = (bf16[2,128,1024]{2,1,0:T(8,128)(2,1)S(1)}, f32[2,128,1024]{2,1,0:T(8,128)S(1)}, bf16[1024,4096]{1,0:T(8,128)(2,1)S(1)}, bf16[1024,4096]{1,0:T(8,128)(2,1)S(1)}) custom-call(s32[1]{0:T(128)} %bitcast.refs_0_.place, bf16[1024,6144]{1,0:T(8,128)(2,1)} %refs_1_.11, bf16[512,6144]{1,0:T(8,128)(2,1)S(1)} %get-tuple-element.58.refs_2_, ...), custom_call_target="tpu_custom_call" | custom-call | flops 6442450944 | bytes 18874368 | tf_op jit(solution)/shard_map/pallas_call | solution.py:183
  68.4 2.5 %collective-permute-start.11 = (bf16[128,1024]{1,0:T(8,128)(2,1)S(1)}, bf16[128,1024]{1,0:T(8,128)(2,1)S(1)}, u32[]{:S(2)}, u32[]{:S(2)}) collective-permute-start(bf16[128,1024]{1,0:T(8,128)(2,1)S(1)} %get-tuple-element.68.refs_5_), channel_id=1, source_target_pairs={{0,6},{1,7},{2,4},{3,5},{4,2},{5,3},{6,0},{7,1},{8,14},{9,15},{10,... | collective-permute-start | bytes 786440 | tf_op jit(solution)/shard_map/ppermute | solution.py:294
  71.0 0.5 collective-permute-done.8
  71.7 1.5 %collective-permute-start.15 = (bf16[128,1024]{1,0:T(8,128)(2,1)S(1)}, bf16[128,1024]{1,0:T(8,128)(2,1)S(1)}, u32[]{:S(2)}, u32[]{:S(2)}) collective-permute-start(bf16[128,1024]{1,0:T(8,128)(2,1)S(1)} %add_convert_fusion.3.refs_0_.first), channel_id=1, source_target_pairs={{0,16},{8,24},{16,0},{24,8},{1,17},{9,25},{17,1},{25,9},{2,18},{10... | collective-permute-start | bytes 786440 | tf_op jit(solution)/shard_map/ppermute | solution.py:291
  73.2 1.0 collective-permute-start.16
  74.2 1.0 collective-permute-start.17
  75.4 4.7 %collective-permute-done.15.refs_1_ = bf16[128,1024]{1,0:T(8,128)(2,1)S(1)} collective-permute-done((bf16[128,1024]{1,0:T(8,128)(2,1)S(1)}, bf16[128,1024]{1,0:T(8,128)(2,1)S(1)}, u32[]{:S(2)}, u32[]{:S(2)}) %collective-permute-start.15) | collective-permute-done | bytes 262176 | tf_op jit(solution)/shard_map/ppermute | solution.py:291
  80.1 1.3 %collective-permute-start.14 = (bf16[128,1024]{1,0:T(8,128)(2,1)S(1)}, bf16[128,1024]{1,0:T(8,128)(2,1)S(1)}, u32[]{:S(2)}, u32[]{:S(2)}) collective-permute-start(bf16[128,1024]{1,0:T(8,128)(2,1)S(1)} %get-tuple-element.70), channel_id=1, source_target_pairs={{0,2},{1,3},{2,0},{3,1},{4,6},{5,7},{6,4},{7,5},{8,10},{9,11},{10,... | collective-permute-start | bytes 786440 | tf_op jit(solution)/shard_map/ppermute | solution.py:294
  81.4 1.5 %carry.1.refs_5_ = f32[128,1024]{1,0:T(8,128)S(1)} custom-call(s32[1]{0:T(128)} %bitcast.refs_0_.place, bf16[128,1024]{1,0:T(8,128)(2,1)S(1)} %add_convert_fusion.3.refs_0_.first, bf16[128,1024]{1,0:T(8,128)(2,1)S(1)} %collective-permute-done.15.refs_1_, bf16[1024,4096]{1,0:T(8,128)(2,1)S(1)} %get-tuple-element.61.refs_2_.refs_8_), custom_call_target="tpu_custom_call" | custom-call | flops 268435456 | bytes 1048576 | tf_op jit(solution)/shard_map/carry/pallas_call | solution.py:344
  82.9 10.1 %collective-permute-done.12.refs_1_ = bf16[128,1024]{1,0:T(8,128)(2,1)S(1)} collective-permute-done((bf16[128,1024]{1,0:T(8,128)(2,1)S(1)}, bf16[128,1024]{1,0:T(8,128)(2,1)S(1)}, u32[]{:S(2)}, u32[]{:S(2)}) %collective-permute-start.12) | collective-permute-done | bytes 262176 | tf_op jit(solution)/shard_map/ppermute | solution.py:294
  93.1 2.9 %shard_map.62 = (f32[128,1024]{1,0:T(8,128)S(1)}, bf16[128,1024]{1,0:T(8,128)(2,1)S(1)}, bf16[128,1024]{1,0:T(8,128)(2,1)S(1)}, bf16[128,1024]{1,0:T(8,128)(2,1)S(1)}) custom-call(s32[1]{0:T(128)} %bitcast.refs_0_.place, bf16[128,2,1024]{2,1,0:T(2,128)(2,1)S(1)} %copy-done, bf16[128,1024]{1,0:T(8,128)(2,1)S(1)} %collective-permute-done.11.refs_0_, ...), custom_call_target="tpu_custom_call" | custom-call | flops 2147483648 | bytes 16777216 | tf_op jit(solution)/shard_map/pallas_call | solution.py:261
  96.0 1.6 %collective-permute-start.18 = (bf16[128,1024]{1,0:T(8,128)(2,1)S(1)}, bf16[128,1024]{1,0:T(8,128)(2,1)S(1)}, u32[]{:S(2)}, u32[]{:S(2)}) collective-permute-start(bf16[128,1024]{1,0:T(8,128)(2,1)S(1)} %get-tuple-element.64), channel_id=1, source_target_pairs={{0,8},{8,0},{16,24},{24,16},{1,9},{9,1},{17,25},{25,17},{2,10},{10... | collective-permute-start | bytes 786440 | tf_op jit(solution)/shard_map/ppermute | solution.py:291
  97.5 1.5 %collective-permute-start.19 = (bf16[128,1024]{1,0:T(8,128)(2,1)S(1)}, bf16[128,1024]{1,0:T(8,128)(2,1)S(1)}, u32[]{:S(2)}, u32[]{:S(2)}) collective-permute-start(bf16[128,1024]{1,0:T(8,128)(2,1)S(1)} %get-tuple-element.65), channel_id=1, source_target_pairs={{0,16},{8,24},{16,0},{24,8},{1,17},{9,25},{17,1},{25,9},{2,18},{10... | collective-permute-start | bytes 786440 | tf_op jit(solution)/shard_map/ppermute | solution.py:291
  99.1 0.5 collective-permute-start.20
  99.5 5.7 %collective-permute-done.18.refs_1_ = bf16[128,1024]{1,0:T(8,128)(2,1)S(1)} collective-permute-done((bf16[128,1024]{1,0:T(8,128)(2,1)S(1)}, bf16[128,1024]{1,0:T(8,128)(2,1)S(1)}, u32[]{:S(2)}, u32[]{:S(2)}) %collective-permute-start.18) | collective-permute-done | bytes 262176 | tf_op jit(solution)/shard_map/ppermute | solution.py:291
  105.2 5.4 %collective-permute-done.19.refs_2_ = bf16[128,1024]{1,0:T(8,128)(2,1)S(1)} collective-permute-done((bf16[128,1024]{1,0:T(8,128)(2,1)S(1)}, bf16[128,1024]{1,0:T(8,128)(2,1)S(1)}, u32[]{:S(2)}, u32[]{:S(2)}) %collective-permute-start.19) | collective-permute-done | bytes 262176 | tf_op jit(solution)/shard_map/ppermute | solution.py:291
  110.7 1.2 %result.1 = bf16[128,2,1024]{2,1,0:T(2,128)(2,1)} custom-call(bf16[128,1024]{1,0:T(8,128)(2,1)S(1)} %add_convert_fusion.3.refs_0_.first, f32[128,1024]{1,0:T(8,128)S(1)} %get-tuple-element.63.refs_0_, bf16[128,1024]{1,0:T(8,128)(2,1)S(1)} %collective-permute-done.18.refs_1_, bf16[128,1024]{1,0:T(8,128)(2,1)S(1)} %collective-permute-done.19.refs_2_, ...), custom_call_target="tpu_custom_call" | custom-call | tf_op jit(solution)/shard_map/result/pallas_call | solution.py:361
  (29 shorter events, 1.0 us)
Async XLA Ops:
  7.2 4.3 %collective-permute-start = (bf16[1,128,1024]{2,1,0:T(8,128)(2,1)S(1)}, bf16[1,128,1024]{2,1,0:T(8,128)(2,1)S(1)}, u32[]{:S(2)}, u32[]{:S(2)}) collective-permute-start(bf16[1,128,1024]{2,1,0:T(8,128)(2,1)S(1)} %get-tuple-element.37), channel_id=1, source_target_pairs={{0,1},{1,0},{2,3},{3,2},{4,5},{5,4},{6,7},{7,6},{8,9},{9,8},{10,11... | collective-permute-start | bytes 786440 | tf_op jit(solution)/shard_map/ppermute | solution.py:294
  11.3 4.7 %collective-permute-start.2 = (bf16[1,128,1024]{2,1,0:T(8,128)(2,1)S(1)}, bf16[1,128,1024]{2,1,0:T(8,128)(2,1)S(1)}, u32[]{:S(2)}, u32[]{:S(2)}) collective-permute-start(bf16[1,128,1024]{2,1,0:T(8,128)(2,1)S(1)} %get-tuple-element.41), channel_id=1, source_target_pairs={{0,1},{1,0},{2,3},{3,2},{4,5},{5,4},{6,7},{7,6},{8,9},{9,8},{10,11... | collective-permute-start | bytes 786440 | tf_op jit(solution)/shard_map/ppermute | solution.py:294
  15.5 5.5 %collective-permute-start.4 = (bf16[1,128,1024]{2,1,0:T(8,128)(2,1)S(1)}, bf16[1,128,1024]{2,1,0:T(8,128)(2,1)S(1)}, u32[]{:S(2)}, u32[]{:S(2)}) collective-permute-start(bf16[1,128,1024]{2,1,0:T(8,128)(2,1)S(1)} %get-tuple-element.44), channel_id=1, source_target_pairs={{0,1},{1,0},{2,3},{3,2},{4,5},{5,4},{6,7},{7,6},{8,9},{9,8},{10,11... | collective-permute-start | bytes 786440 | tf_op jit(solution)/shard_map/ppermute | solution.py:294
  21.0 34.9 %copy-start = (bf16[128,2,1024]{2,1,0:T(2,128)(2,1)S(1)}, bf16[128,2,1024]{2,1,0:T(2,128)(2,1)}, u32[]{:S(2)}) copy-start(bf16[128,2,1024]{2,1,0:T(2,128)(2,1)} %rhs.3) | copy-start | bytes 1572868
  28.2 32.8 %collective-permute-start.10 = (bf16[2,128,1024]{2,1,0:T(8,128)(2,1)S(1)}, bf16[2,128,1024]{2,1,0:T(8,128)(2,1)S(1)}, u32[]{:S(2)}, u32[]{:S(2)}) collective-permute-start(bf16[2,128,1024]{2,1,0:T(8,128)(2,1)S(1)} %get-tuple-element.57), channel_id=1, source_target_pairs={{0,1},{1,0},{2,3},{3,2},{4,5},{5,4},{6,7},{7,6},{8,9},{9,8},{10,11... | collective-permute-start | bytes 1572872 | tf_op jit(solution)/shard_map/ppermute | solution.py:294
  28.3 12.4 %collective-permute-start.1 = (bf16[128,1024]{1,0:T(8,128)(2,1)S(1)}, bf16[128,1024]{1,0:T(8,128)(2,1)S(1)}, u32[]{:S(2)}, u32[]{:S(2)}) collective-permute-start(bf16[128,1024]{1,0:T(8,128)(2,1)S(1)} %fusion.refs_4_), channel_id=1, source_target_pairs={{0,6},{1,7},{2,4},{3,5},{4,2},{5,3},{6,0},{7,1},{8,14},{9,15},{10,... | collective-permute-start | bytes 786440 | tf_op jit(solution)/shard_map/ppermute | solution.py:294
  33.4 22.6 %collective-permute-start.3 = (bf16[128,1024]{1,0:T(8,128)(2,1)S(1)}, bf16[128,1024]{1,0:T(8,128)(2,1)S(1)}, u32[]{:S(2)}, u32[]{:S(2)}) collective-permute-start(bf16[128,1024]{1,0:T(8,128)(2,1)S(1)} %fusion.1.refs_4_), channel_id=1, source_target_pairs={{0,4},{1,5},{2,6},{3,7},{4,0},{5,1},{6,2},{7,3},{8,12},{9,13},{10,... | collective-permute-start | bytes 786440 | tf_op jit(solution)/shard_map/ppermute | solution.py:294
  33.4 22.6 %collective-permute-start.6 = (bf16[1,128,1024]{2,1,0:T(8,128)(2,1)S(1)}, bf16[1,128,1024]{2,1,0:T(8,128)(2,1)S(1)}, u32[]{:S(2)}, u32[]{:S(2)}) collective-permute-start(bf16[1,128,1024]{2,1,0:T(8,128)(2,1)S(1)} %get-tuple-element.47), channel_id=1, source_target_pairs={{0,1},{1,0},{2,3},{3,2},{4,5},{5,4},{6,7},{7,6},{8,9},{9,8},{10,11... | collective-permute-start | bytes 786440 | tf_op jit(solution)/shard_map/ppermute | solution.py:294
  33.4 22.6 %collective-permute-start.5 = (bf16[128,1024]{1,0:T(8,128)(2,1)S(1)}, bf16[128,1024]{1,0:T(8,128)(2,1)S(1)}, u32[]{:S(2)}, u32[]{:S(2)}) collective-permute-start(bf16[128,1024]{1,0:T(8,128)(2,1)S(1)} %fusion.2.refs_5_), channel_id=1, source_target_pairs={{0,2},{1,3},{2,0},{3,1},{4,6},{5,7},{6,4},{7,5},{8,10},{9,11},{10,... | collective-permute-start | bytes 786440 | tf_op jit(solution)/shard_map/ppermute | solution.py:294
  57.4 13.5 %collective-permute-start.9 = (bf16[128,1024]{1,0:T(8,128)(2,1)S(1)}, bf16[128,1024]{1,0:T(8,128)(2,1)S(1)}, u32[]{:S(2)}, u32[]{:S(2)}) collective-permute-start(bf16[128,1024]{1,0:T(8,128)(2,1)S(1)} %get-tuple-element.55), channel_id=1, source_target_pairs={{0,24},{8,16},{16,8},{24,0},{1,25},{9,17},{17,9},{25,1},{2,26},{10... | collective-permute-start | bytes 786440 | tf_op jit(solution)/shard_map/ppermute | solution.py:291
  59.9 11.5 %collective-permute-start.8 = (bf16[128,1024]{1,0:T(8,128)(2,1)S(1)}, bf16[128,1024]{1,0:T(8,128)(2,1)S(1)}, u32[]{:S(2)}, u32[]{:S(2)}) collective-permute-start(bf16[128,1024]{1,0:T(8,128)(2,1)S(1)} %get-tuple-element.54), channel_id=1, source_target_pairs={{0,16},{8,24},{16,0},{24,8},{1,17},{9,25},{17,1},{25,9},{2,18},{10... | collective-permute-start | bytes 786440 | tf_op jit(solution)/shard_map/ppermute | solution.py:291
  60.4 11.1 %collective-permute-start.7 = (bf16[128,1024]{1,0:T(8,128)(2,1)S(1)}, bf16[128,1024]{1,0:T(8,128)(2,1)S(1)}, u32[]{:S(2)}, u32[]{:S(2)}) collective-permute-start(bf16[128,1024]{1,0:T(8,128)(2,1)S(1)} %get-tuple-element.53.refs_7_), channel_id=1, source_target_pairs={{0,8},{8,0},{16,24},{24,16},{1,9},{9,1},{17,25},{25,17},{2,10},{10... | collective-permute-start | bytes 786440 | tf_op jit(solution)/shard_map/ppermute | solution.py:291
  68.4 5.9 %collective-permute-start.13 = (bf16[2,128,1024]{2,1,0:T(8,128)(2,1)S(1)}, bf16[2,128,1024]{2,1,0:T(8,128)(2,1)S(1)}, u32[]{:S(2)}, u32[]{:S(2)}) collective-permute-start(bf16[2,128,1024]{2,1,0:T(8,128)(2,1)S(1)} %get-tuple-element.60), channel_id=1, source_target_pairs={{0,1},{1,0},{2,3},{3,2},{4,5},{5,4},{6,7},{7,6},{8,9},{9,8},{10,11... | collective-permute-start | bytes 1572872 | tf_op jit(solution)/shard_map/ppermute | solution.py:294
  68.4 14.5 %collective-permute-start.11 = (bf16[128,1024]{1,0:T(8,128)(2,1)S(1)}, bf16[128,1024]{1,0:T(8,128)(2,1)S(1)}, u32[]{:S(2)}, u32[]{:S(2)}) collective-permute-start(bf16[128,1024]{1,0:T(8,128)(2,1)S(1)} %get-tuple-element.68.refs_5_), channel_id=1, source_target_pairs={{0,6},{1,7},{2,4},{3,5},{4,2},{5,3},{6,0},{7,1},{8,14},{9,15},{10,... | collective-permute-start | bytes 786440 | tf_op jit(solution)/shard_map/ppermute | solution.py:294
  71.0 22.1 %collective-permute-start.12 = (bf16[128,1024]{1,0:T(8,128)(2,1)S(1)}, bf16[128,1024]{1,0:T(8,128)(2,1)S(1)}, u32[]{:S(2)}, u32[]{:S(2)}) collective-permute-start(bf16[128,1024]{1,0:T(8,128)(2,1)S(1)} %get-tuple-element.67.refs_6_), channel_id=1, source_target_pairs={{0,4},{1,5},{2,6},{3,7},{4,0},{5,1},{6,2},{7,3},{8,12},{9,13},{10,... | collective-permute-start | bytes 786440 | tf_op jit(solution)/shard_map/ppermute | solution.py:294
  71.7 8.3 %collective-permute-start.15 = (bf16[128,1024]{1,0:T(8,128)(2,1)S(1)}, bf16[128,1024]{1,0:T(8,128)(2,1)S(1)}, u32[]{:S(2)}, u32[]{:S(2)}) collective-permute-start(bf16[128,1024]{1,0:T(8,128)(2,1)S(1)} %add_convert_fusion.3.refs_0_.first), channel_id=1, source_target_pairs={{0,16},{8,24},{16,0},{24,8},{1,17},{9,25},{17,1},{25,9},{2,18},{10... | collective-permute-start | bytes 786440 | tf_op jit(solution)/shard_map/ppermute | solution.py:291
  73.2 19.9 %collective-permute-start.16 = (bf16[128,1024]{1,0:T(8,128)(2,1)S(1)}, bf16[128,1024]{1,0:T(8,128)(2,1)S(1)}, u32[]{:S(2)}, u32[]{:S(2)}) collective-permute-start(bf16[128,1024]{1,0:T(8,128)(2,1)S(1)} %add_convert_fusion.3.refs_0_.first), channel_id=1, source_target_pairs={{0,8},{8,0},{16,24},{24,16},{1,9},{9,1},{17,25},{25,17},{2,10},{10... | collective-permute-start | bytes 786440 | tf_op jit(solution)/shard_map/ppermute | solution.py:291
  74.2 18.9 %collective-permute-start.17 = (bf16[128,1024]{1,0:T(8,128)(2,1)S(1)}, bf16[128,1024]{1,0:T(8,128)(2,1)S(1)}, u32[]{:S(2)}, u32[]{:S(2)}) collective-permute-start(bf16[128,1024]{1,0:T(8,128)(2,1)S(1)} %add_convert_fusion.3.refs_0_.first), channel_id=1, source_target_pairs={{0,24},{8,16},{16,8},{24,0},{1,25},{9,17},{17,9},{25,1},{2,26},{10... | collective-permute-start | bytes 786440 | tf_op jit(solution)/shard_map/ppermute | solution.py:291
  80.1 13.1 %collective-permute-start.14 = (bf16[128,1024]{1,0:T(8,128)(2,1)S(1)}, bf16[128,1024]{1,0:T(8,128)(2,1)S(1)}, u32[]{:S(2)}, u32[]{:S(2)}) collective-permute-start(bf16[128,1024]{1,0:T(8,128)(2,1)S(1)} %get-tuple-element.70), channel_id=1, source_target_pairs={{0,2},{1,3},{2,0},{3,1},{4,6},{5,7},{6,4},{7,5},{8,10},{9,11},{10,... | collective-permute-start | bytes 786440 | tf_op jit(solution)/shard_map/ppermute | solution.py:294
  96.0 9.2 %collective-permute-start.18 = (bf16[128,1024]{1,0:T(8,128)(2,1)S(1)}, bf16[128,1024]{1,0:T(8,128)(2,1)S(1)}, u32[]{:S(2)}, u32[]{:S(2)}) collective-permute-start(bf16[128,1024]{1,0:T(8,128)(2,1)S(1)} %get-tuple-element.64), channel_id=1, source_target_pairs={{0,8},{8,0},{16,24},{24,16},{1,9},{9,1},{17,25},{25,17},{2,10},{10... | collective-permute-start | bytes 786440 | tf_op jit(solution)/shard_map/ppermute | solution.py:291
  97.5 13.1 %collective-permute-start.19 = (bf16[128,1024]{1,0:T(8,128)(2,1)S(1)}, bf16[128,1024]{1,0:T(8,128)(2,1)S(1)}, u32[]{:S(2)}, u32[]{:S(2)}) collective-permute-start(bf16[128,1024]{1,0:T(8,128)(2,1)S(1)} %get-tuple-element.65), channel_id=1, source_target_pairs={{0,16},{8,24},{16,0},{24,8},{1,17},{9,25},{17,1},{25,9},{2,18},{10... | collective-permute-start | bytes 786440 | tf_op jit(solution)/shard_map/ppermute | solution.py:291
  99.1 11.6 %collective-permute-start.20 = (bf16[128,1024]{1,0:T(8,128)(2,1)S(1)}, bf16[128,1024]{1,0:T(8,128)(2,1)S(1)}, u32[]{:S(2)}, u32[]{:S(2)}) collective-permute-start(bf16[128,1024]{1,0:T(8,128)(2,1)S(1)} %get-tuple-element.66), channel_id=1, source_target_pairs={{0,24},{8,16},{16,8},{24,0},{1,25},{9,17},{17,9},{25,1},{2,26},{10... | collective-permute-start | bytes 786440 | tf_op jit(solution)/shard_map/ppermute | solution.py:291
where the time goes:
time: 112 us
  waiting for transfers between devices  48.5 us (43%)
  Pallas kernels  41 us (37%)
  starting transfers between devices  21.5 us (19%)
    pallas_call x6, Pallas kernels, partial_sums(): pl.pallas_call(functools.partial(partial_kernel, cfg), in_specs=in_specs,...  34 us
    ppermute x12, waiting for transfers between devices, across_col(): return lax.ppermute(value, 'col', [(i, i ^ offset) for i in range(cols)])  32.2 us
    ppermute x9, waiting for transfers between devices, across_row(): return lax.ppermute(value, 'row', [(i, i ^ offset) for i in range(members)])  16.4 us
    ppermute x12, starting transfers between devices, across_col(): return lax.ppermute(value, 'col', [(i, i ^ offset) for i in range(cols)])  10.9 us
    ppermute x9, starting transfers between devices, across_row(): return lax.ppermute(value, 'row', [(i, i ^ offset) for i in range(members)])  10.7 us
    pallas_call x2, Pallas kernels, solve(): pl.pallas_call(kernel, in_specs=[pl.BlockSpec(memory_space=pltpu.SMEM)] +...  4.38 us
  transfers between devices with their start and end apart: 21, of which 8 were waited for; matrix products, arithmetic and copies ran while one was open for 0% of the time, Pallas kernels for 20%

commit v1 on v0

--- a/solution.py
+++ b/solution.py
@@ -305,33 +305,41 @@
     extras[last].append(("second", inverse, 1, 0, width))
 
     flops = 2 * half * width * width * members
-    sums, sent, kept = [[], []], [], {}
+    sums, kept, passing = [[], []], {}, {}
+    due = [[] for _ in plan]
     x, held = None, panel
     for n, (b, group) in enumerate(plan):
         if b == 1 and plan[n - 1][0] == 0:
             held = [kept["low"], kept["high"]]
         following = plan[n + 1][1] if n < last else []
-        orders = sent[n - 2] if n >= 2 else []
+        orders = due[n]
         if n == last:
             parts = solve(
                 functools.partial(solve_first_kernel, len(sums[0]), cols),
                 flops, place, rhs, sums[0], [kept["inverse"]], members,
             )
-            orders = sent[n - 1] + [parts[members > 1]]
+            orders = due[n] + [parts[members > 1]]
         send, keep, held, x, got = partial_sums(
             solved, x, held, b, orders, place,
             group, following, half, chips, [e[1:] for e in extras[n]],
         )
         kept.update(zip([e[0] for e in extras[n]], got))
         other = across_col(send, 1)
-        outgoing = []
         for at, offset in enumerate(group):
+            pair = keep[at], other[at]
             if offset == 0:
-                sums[b] += [keep[at], other[at]]
+                sums[b] += pair
+                continue
+            value = pair[0] + pair[1].astype(F32)
+            if offset % 2 == 0:
+                value += passing.pop((b, offset)).astype(F32)
+            value = value.astype(BF16)
+            due[min(last, n + (2 if offset % 2 else 3))].append(value)
+            arrived = across_col(value, 2 if offset % 2 else 2 * offset)
+            if offset > 1 and offset % 2:
+                passing[b, offset - 1] = arrived
             else:
-                outgoing.append((keep[at] + other[at].astype(F32)).astype(BF16))
-                sums[b].append(across_col(outgoing[-1], 2 * offset))
-        sent.append(outgoing)
+                sums[b].append(arrived)
 
     total = parts[0]
     for offset in range(1, members):

time: 112 us -> 100 us (0.89)
  waiting for transfers between devices: 48.5 us -> 36.4 us
    ppermute x12, waiting for transfers between devices: 32.2 us -> 14.9 us  [across_col(): return lax.ppermute(value, 'col', [(i, i ^ offset) for i in range(cols)])]
    ppermute x9, waiting for transfers between devices: 16.4 us -> 21.5 us  [across_row(): return lax.ppermute(value, 'row', [(i, i ^ offset) for i in range(members)])]
  transfers between devices with their start and end apart: 21 -> 21, of which waited for: 8 -> 10; matrix products, arithmetic and copies ran while one was open for 0% -> 1% of each run, Pallas kernels for 20% -> 23%
where the time goes in v1:
time: 100 us
  Pallas kernels  41 us (41%)
  waiting for transfers between devices  36.4 us (36%)
  starting transfers between devices  22 us (22%)
    pallas_call x6, Pallas kernels, partial_sums(): pl.pallas_call(functools.partial(partial_kernel, cfg), in_specs=in_specs,...  33.9 us
    ppermute x9, waiting for transfers between devices, across_row(): return lax.ppermute(value, 'row', [(i, i ^ offset) for i in range(members)])  21.5 us
    ppermute x12, waiting for transfers between devices, across_col(): return lax.ppermute(value, 'col', [(i, i ^ offset) for i in range(cols)])  14.9 us
    ppermute x12, starting transfers between devices, across_col(): return lax.ppermute(value, 'col', [(i, i ^ offset) for i in range(cols)])  11.4 us
    ppermute x9, starting transfers between devices, across_row(): return lax.ppermute(value, 'row', [(i, i ^ offset) for i in range(members)])  10.7 us
    pallas_call x2, Pallas kernels, solve(): pl.pallas_call(kernel, in_specs=[pl.BlockSpec(memory_space=pltpu.SMEM)] +...  4.33 us
  transfers between devices with their start and end apart: 21, of which 10 were waited for; matrix products, arithmetic and copies ran while one was open for 1% of the time, Pallas kernels for 23%

profile of v1, /device:TPU:0, one launch (start us, length us, event | category | flops | bytes accessed | tf_op | source)
XLA Modules:
  0.0 100.2 jit_solution(7923300959249830662)
XLA Ops:
  0.0 7.2 %shard_map.55 = (bf16[1,128,1024]{2,1,0:T(8,128)(2,1)S(1)}, f32[1,128,1024]{2,1,0:T(8,128)S(1)}, bf16[1024,6144]{1,0:T(8,128)(2,1)S(1)}, bf16[256,6144]{1,0:T(8,128)(2,1)S(1)}) custom-call(s32[1]{0:T(128)} %bitcast.refs_0_.place, bf16[1024,6144]{1,0:T(8,128)(2,1)} %refs_1_.11, bf16[2,1024,6144]{2,1,0:T(8,128)(2,1)} %refs_4_.1), custom_call_target="tpu_custom_call" | custom-call | flops 3221225472 | bytes 15728640 | tf_op jit(solution)/shard_map/pallas_call | solution.py:183
  7.2 0.6 collective-permute-start.1
  7.7 3.6 %shard_map.56 = (bf16[1,128,1024]{2,1,0:T(8,128)(2,1)S(1)}, f32[1,128,1024]{2,1,0:T(8,128)S(1)}, bf16[256,6144]{1,0:T(8,128)(2,1)S(1)}) custom-call(s32[1]{0:T(128)} %bitcast.refs_0_.place, bf16[1024,6144]{1,0:T(8,128)(2,1)} %refs_1_.11, bf16[256,6144]{1,0:T(8,128)(2,1)S(1)} %get-tuple-element.36.refs_2_, bf16[1024,6144]{1,0:T(8,128)(2,1)S(1)} %get-tuple-element.37.refs_3_), custom_call_target="tpu_custom_call" | custom-call | flops 3221225472 | bytes 15728640 | tf_op jit(solution)/shard_map/pallas_call | solution.py:183
  11.5 3.1 %collective-permute-start.2 = (bf16[128,1024]{1,0:T(8,128)(2,1)S(1)}, bf16[128,1024]{1,0:T(8,128)(2,1)S(1)}, u32[]{:S(2)}, u32[]{:S(2)}) collective-permute-start(bf16[128,1024]{1,0:T(8,128)(2,1)S(1)} %fusion.2.refs_4_), channel_id=1, source_target_pairs={{0,2},{1,3},{2,0},{3,1},{4,6},{5,7},{6,4},{7,5},{8,10},{9,11},{10,... | collective-permute-start | bytes 786440 | tf_op jit(solution)/shard_map/ppermute | solution.py:294
  14.6 3.9 %shard_map.57 = (bf16[1,128,1024]{2,1,0:T(8,128)(2,1)S(1)}, f32[1,128,1024]{2,1,0:T(8,128)S(1)}, bf16[256,6144]{1,0:T(8,128)(2,1)S(1)}, bf16[512,6144]{1,0:T(8,128)(2,1)S(1)}) custom-call(s32[1]{0:T(128)} %bitcast.refs_0_.place, bf16[1024,6144]{1,0:T(8,128)(2,1)} %refs_1_.11, bf16[256,6144]{1,0:T(8,128)(2,1)S(1)} %get-tuple-element.42.refs_2_, ...), custom_call_target="tpu_custom_call" | custom-call | flops 3221225472 | bytes 15728640 | tf_op jit(solution)/shard_map/pallas_call | solution.py:183
  18.6 4.9 %shard_map.58 = (bf16[1,128,1024]{2,1,0:T(8,128)(2,1)S(1)}, f32[1,128,1024]{2,1,0:T(8,128)S(1)}, bf16[512,6144]{1,0:T(8,128)(2,1)S(1)}, bf16[512,6144]{1,0:T(8,128)(2,1)S(1)}) custom-call(s32[1]{0:T(128)} %bitcast.refs_0_.place, bf16[1024,6144]{1,0:T(8,128)(2,1)} %refs_1_.11, bf16[256,6144]{1,0:T(8,128)(2,1)S(1)} %get-tuple-element.45.refs_2_, ...), custom_call_target="tpu_custom_call" | custom-call | flops 3221225472 | bytes 15728640 | tf_op jit(solution)/shard_map/pallas_call | solution.py:183
  23.7 7.2 %shard_map.59 = (bf16[2,128,1024]{2,1,0:T(8,128)(2,1)S(1)}, f32[2,128,1024]{2,1,0:T(8,128)S(1)}, bf16[512,6144]{1,0:T(8,128)(2,1)S(1)}, bf16[1024,4096]{1,0:T(8,128)(2,1)S(1)}) custom-call(s32[1]{0:T(128)} %bitcast.refs_0_.place, bf16[1024,6144]{1,0:T(8,128)(2,1)} %refs_1_.11, bf16[512,6144]{1,0:T(8,128)(2,1)S(1)} %get-tuple-element.48.refs_2_, ...), custom_call_target="tpu_custom_call" | custom-call | flops 6442450944 | bytes 18874368 | tf_op jit(solution)/shard_map/pallas_call | solution.py:183
  30.9 0.6 collective-permute-start.10
  31.5 2.6 %collective-permute-start.3 = (bf16[128,1024]{1,0:T(8,128)(2,1)S(1)}, bf16[128,1024]{1,0:T(8,128)(2,1)S(1)}, u32[]{:S(2)}, u32[]{:S(2)}) collective-permute-start(bf16[128,1024]{1,0:T(8,128)(2,1)S(1)} %fusion.1.refs_5_), channel_id=1, source_target_pairs={{0,4},{1,5},{2,6},{3,7},{4,0},{5,1},{6,2},{7,3},{8,12},{9,13},{10,... | collective-permute-start | bytes 786440 | tf_op jit(solution)/shard_map/ppermute | solution.py:294
  34.6 1.6 %collective-permute-start.11 = (bf16[128,1024]{1,0:T(8,128)(2,1)S(1)}, bf16[128,1024]{1,0:T(8,128)(2,1)S(1)}, u32[]{:S(2)}, u32[]{:S(2)}) collective-permute-start(bf16[128,1024]{1,0:T(8,128)(2,1)S(1)} %fusion.4.refs_5_), channel_id=1, source_target_pairs={{0,2},{1,3},{2,0},{3,1},{4,6},{5,7},{6,4},{7,5},{8,10},{9,11},{10,... | collective-permute-start | bytes 786440 | tf_op jit(solution)/shard_map/ppermute | solution.py:294
  36.3 10.3 %collective-permute-done.3.refs_0_ = bf16[128,1024]{1,0:T(8,128)(2,1)S(1)} collective-permute-done((bf16[128,1024]{1,0:T(8,128)(2,1)S(1)}, bf16[128,1024]{1,0:T(8,128)(2,1)S(1)}, u32[]{:S(2)}, u32[]{:S(2)}) %collective-permute-start.3) | collective-permute-done | bytes 262176 | tf_op jit(solution)/shard_map/ppermute | solution.py:294
  46.6 2.2 %collective-permute-done.5.refs_1_ = bf16[128,1024]{1,0:T(8,128)(2,1)S(1)} collective-permute-done((bf16[128,1024]{1,0:T(8,128)(2,1)S(1)}, bf16[128,1024]{1,0:T(8,128)(2,1)S(1)}, u32[]{:S(2)}, u32[]{:S(2)}) %collective-permute-start.5) | collective-permute-done | bytes 262176 | tf_op jit(solution)/shard_map/ppermute | solution.py:294
  48.8 1.5 %shard_map.60 = (f32[128,1024]{1,0:T(8,128)S(1)}, bf16[128,1024]{1,0:T(8,128)(2,1)S(1)}, bf16[128,1024]{1,0:T(8,128)(2,1)S(1)}, bf16[128,1024]{1,0:T(8,128)(2,1)S(1)}) custom-call(s32[1]{0:T(128)} %bitcast.refs_0_.place, bf16[128,2,1024]{2,1,0:T(2,128)(2,1)S(1)} %copy-done, bf16[128,1024]{1,0:T(8,128)(2,1)S(1)} %collective-permute-done.3.refs_0_, ...), custom_call_target="tpu_custom_call" | custom-call | flops 1073741824 | bytes 8388608 | tf_op jit(solution)/shard_map/pallas_call | solution.py:261
  50.3 2.5 %collective-permute-start.9 = (bf16[128,1024]{1,0:T(8,128)(2,1)S(1)}, bf16[128,1024]{1,0:T(8,128)(2,1)S(1)}, u32[]{:S(2)}, u32[]{:S(2)}) collective-permute-start(bf16[128,1024]{1,0:T(8,128)(2,1)S(1)} %get-tuple-element.55), channel_id=1, source_target_pairs={{0,24},{8,16},{16,8},{24,0},{1,25},{9,17},{17,9},{25,1},{2,26},{10... | collective-permute-start | bytes 786440 | tf_op jit(solution)/shard_map/ppermute | solution.py:291
  53.3 0.5 collective-permute-start.7
  54.0 7.2 %shard_map.61 = (bf16[2,128,1024]{2,1,0:T(8,128)(2,1)S(1)}, f32[2,128,1024]{2,1,0:T(8,128)S(1)}, bf16[1024,4096]{1,0:T(8,128)(2,1)S(1)}, bf16[1024,4096]{1,0:T(8,128)(2,1)S(1)}) custom-call(s32[1]{0:T(128)} %bitcast.refs_0_.place, bf16[1024,6144]{1,0:T(8,128)(2,1)} %refs_1_.11, bf16[512,6144]{1,0:T(8,128)(2,1)S(1)} %get-tuple-element.58.refs_2_, ...), custom_call_target="tpu_custom_call" | custom-call | flops 6442450944 | bytes 18874368 | tf_op jit(solution)/shard_map/pallas_call | solution.py:183
  61.3 2.3 %collective-permute-done.8 = bf16[128,1024]{1,0:T(8,128)(2,1)S(1)} collective-permute-done((bf16[128,1024]{1,0:T(8,128)(2,1)S(1)}, bf16[128,1024]{1,0:T(8,128)(2,1)S(1)}, u32[]{:S(2)}, u32[]{:S(2)}) %collective-permute-start.8) | collective-permute-done | bytes 262176 | tf_op jit(solution)/shard_map/ppermute | solution.py:291
  63.8 1.5 %collective-permute-start.15 = (bf16[128,1024]{1,0:T(8,128)(2,1)S(1)}, bf16[128,1024]{1,0:T(8,128)(2,1)S(1)}, u32[]{:S(2)}, u32[]{:S(2)}) collective-permute-start(bf16[128,1024]{1,0:T(8,128)(2,1)S(1)} %add_convert_fusion.2.refs_0_.first), channel_id=1, source_target_pairs={{0,16},{8,24},{16,0},{24,8},{1,17},{9,25},{17,1},{25,9},{2,18},{10... | collective-permute-start | bytes 786440 | tf_op jit(solution)/shard_map/ppermute | solution.py:291
  65.3 0.8 collective-permute-start.16
  66.1 1.3 %collective-permute-start.17 = (bf16[128,1024]{1,0:T(8,128)(2,1)S(1)}, bf16[128,1024]{1,0:T(8,128)(2,1)S(1)}, u32[]{:S(2)}, u32[]{:S(2)}) collective-permute-start(bf16[128,1024]{1,0:T(8,128)(2,1)S(1)} %add_convert_fusion.2.refs_0_.first), channel_id=1, source_target_pairs={{0,24},{8,16},{16,8},{24,0},{1,25},{9,17},{17,9},{25,1},{2,26},{10... | collective-permute-start | bytes 786440 | tf_op jit(solution)/shard_map/ppermute | solution.py:291
  67.5 2.2 %collective-permute-start.14 = (bf16[128,1024]{1,0:T(8,128)(2,1)S(1)}, bf16[128,1024]{1,0:T(8,128)(2,1)S(1)}, u32[]{:S(2)}, u32[]{:S(2)}) collective-permute-start(bf16[128,1024]{1,0:T(8,128)(2,1)S(1)} %get-tuple-element.68), channel_id=1, source_target_pairs={{0,2},{1,3},{2,0},{3,1},{4,6},{5,7},{6,4},{7,5},{8,10},{9,11},{10,... | collective-permute-start | bytes 786440 | tf_op jit(solution)/shard_map/ppermute | solution.py:294
  69.6 2.4 %collective-permute-done.15.refs_1_ = bf16[128,1024]{1,0:T(8,128)(2,1)S(1)} collective-permute-done((bf16[128,1024]{1,0:T(8,128)(2,1)S(1)}, bf16[128,1024]{1,0:T(8,128)(2,1)S(1)}, u32[]{:S(2)}, u32[]{:S(2)}) %collective-permute-start.15) | collective-permute-done | bytes 262176 | tf_op jit(solution)/shard_map/ppermute | solution.py:291
  72.0 1.5 %carry.1.refs_4_ = f32[128,1024]{1,0:T(8,128)S(1)} custom-call(s32[1]{0:T(128)} %bitcast.refs_0_.place, bf16[128,1024]{1,0:T(8,128)(2,1)S(1)} %add_convert_fusion.2.refs_0_.first, bf16[128,1024]{1,0:T(8,128)(2,1)S(1)} %collective-permute-done.15.refs_1_, bf16[1024,4096]{1,0:T(8,128)(2,1)S(1)} %get-tuple-element.61.refs_2_.refs_7_), custom_call_target="tpu_custom_call" | custom-call | flops 268435456 | bytes 1048576 | tf_op jit(solution)/shard_map/carry/pallas_call | solution.py:352
  73.5 0.9 collective-permute-done.16.refs_5_
  74.5 4.2 %collective-permute-done.17.refs_6_ = bf16[128,1024]{1,0:T(8,128)(2,1)S(1)} collective-permute-done((bf16[128,1024]{1,0:T(8,128)(2,1)S(1)}, bf16[128,1024]{1,0:T(8,128)(2,1)S(1)}, u32[]{:S(2)}, u32[]{:S(2)}) %collective-permute-start.17) | collective-permute-done | bytes 262176 | tf_op jit(solution)/shard_map/ppermute | solution.py:291
  78.7 2.4 %collective-permute-done.12.refs_0_ = bf16[128,1024]{1,0:T(8,128)(2,1)S(1)} collective-permute-done((bf16[128,1024]{1,0:T(8,128)(2,1)S(1)}, bf16[128,1024]{1,0:T(8,128)(2,1)S(1)}, u32[]{:S(2)}, u32[]{:S(2)}) %collective-permute-start.12) | collective-permute-done | bytes 262176 | tf_op jit(solution)/shard_map/ppermute | solution.py:294
  81.0 2.9 %shard_map.62 = (f32[128,1024]{1,0:T(8,128)S(1)}, bf16[128,1024]{1,0:T(8,128)(2,1)S(1)}, bf16[128,1024]{1,0:T(8,128)(2,1)S(1)}, bf16[128,1024]{1,0:T(8,128)(2,1)S(1)}) custom-call(s32[1]{0:T(128)} %bitcast.refs_0_.place, bf16[128,2,1024]{2,1,0:T(2,128)(2,1)S(1)} %copy-done, bf16[128,1024]{1,0:T(8,128)(2,1)S(1)} %collective-permute-done.12.refs_0_, ...), custom_call_target="tpu_custom_call" | custom-call | flops 2147483648 | bytes 16777216 | tf_op jit(solution)/shard_map/pallas_call | solution.py:261
  83.9 1.7 %collective-permute-start.18 = (bf16[128,1024]{1,0:T(8,128)(2,1)S(1)}, bf16[128,1024]{1,0:T(8,128)(2,1)S(1)}, u32[]{:S(2)}, u32[]{:S(2)}) collective-permute-start(bf16[128,1024]{1,0:T(8,128)(2,1)S(1)} %get-tuple-element.64), channel_id=1, source_target_pairs={{0,8},{8,0},{16,24},{24,16},{1,9},{9,1},{17,25},{25,17},{2,10},{10... | collective-permute-start | bytes 786440 | tf_op jit(solution)/shard_map/ppermute | solution.py:291
  86.0 1.5 %collective-permute-start.20 = (bf16[128,1024]{1,0:T(8,128)(2,1)S(1)}, bf16[128,1024]{1,0:T(8,128)(2,1)S(1)}, u32[]{:S(2)}, u32[]{:S(2)}) collective-permute-start(bf16[128,1024]{1,0:T(8,128)(2,1)S(1)} %get-tuple-element.66), channel_id=1, source_target_pairs={{0,24},{8,16},{16,8},{24,0},{1,25},{9,17},{17,9},{25,1},{2,26},{10... | collective-permute-start | bytes 786440 | tf_op jit(solution)/shard_map/ppermute | solution.py:291
  87.5 5.7 %collective-permute-done.18.refs_1_ = bf16[128,1024]{1,0:T(8,128)(2,1)S(1)} collective-permute-done((bf16[128,1024]{1,0:T(8,128)(2,1)S(1)}, bf16[128,1024]{1,0:T(8,128)(2,1)S(1)}, u32[]{:S(2)}, u32[]{:S(2)}) %collective-permute-start.18) | collective-permute-done | bytes 262176 | tf_op jit(solution)/shard_map/ppermute | solution.py:291
  93.1 5.9 %collective-permute-done.19.refs_2_ = bf16[128,1024]{1,0:T(8,128)(2,1)S(1)} collective-permute-done((bf16[128,1024]{1,0:T(8,128)(2,1)S(1)}, bf16[128,1024]{1,0:T(8,128)(2,1)S(1)}, u32[]{:S(2)}, u32[]{:S(2)}) %collective-permute-start.19) | collective-permute-done | bytes 262176 | tf_op jit(solution)/shard_map/ppermute | solution.py:291
  99.0 1.2 %result.1 = bf16[128,2,1024]{2,1,0:T(2,128)(2,1)} custom-call(bf16[128,1024]{1,0:T(8,128)(2,1)S(1)} %add_convert_fusion.2.refs_0_.first, f32[128,1024]{1,0:T(8,128)S(1)} %get-tuple-element.63.refs_0_, bf16[128,1024]{1,0:T(8,128)(2,1)S(1)} %collective-permute-done.18.refs_1_, bf16[128,1024]{1,0:T(8,128)(2,1)S(1)} %collective-permute-done.19.refs_2_, ...), custom_call_target="tpu_custom_call" | custom-call | tf_op jit(solution)/shard_map/result/pallas_call | solution.py:369
  (30 shorter events, 2.4 us)
Async XLA Ops:
  7.2 4.3 %collective-permute-start.1 = (bf16[1,128,1024]{2,1,0:T(8,128)(2,1)S(1)}, bf16[1,128,1024]{2,1,0:T(8,128)(2,1)S(1)}, u32[]{:S(2)}, u32[]{:S(2)}) collective-permute-start(bf16[1,128,1024]{2,1,0:T(8,128)(2,1)S(1)} %get-tuple-element.41), channel_id=1, source_target_pairs={{0,1},{1,0},{2,3},{3,2},{4,5},{5,4},{6,7},{7,6},{8,9},{9,8},{10,11... | collective-permute-start | bytes 786440 | tf_op jit(solution)/shard_map/ppermute | solution.py:294
  11.3 12.2 %collective-permute-start = (bf16[1,128,1024]{2,1,0:T(8,128)(2,1)S(1)}, bf16[1,128,1024]{2,1,0:T(8,128)(2,1)S(1)}, u32[]{:S(2)}, u32[]{:S(2)}) collective-permute-start(bf16[1,128,1024]{2,1,0:T(8,128)(2,1)S(1)} %get-tuple-element.39), channel_id=1, source_target_pairs={{0,1},{1,0},{2,3},{3,2},{4,5},{5,4},{6,7},{7,6},{8,9},{9,8},{10,11... | collective-permute-start | bytes 786440 | tf_op jit(solution)/shard_map/ppermute | solution.py:294
  11.5 12.1 %collective-permute-start.2 = (bf16[128,1024]{1,0:T(8,128)(2,1)S(1)}, bf16[128,1024]{1,0:T(8,128)(2,1)S(1)}, u32[]{:S(2)}, u32[]{:S(2)}) collective-permute-start(bf16[128,1024]{1,0:T(8,128)(2,1)S(1)} %fusion.2.refs_4_), channel_id=1, source_target_pairs={{0,2},{1,3},{2,0},{3,1},{4,6},{5,7},{6,4},{7,5},{8,10},{9,11},{10,... | collective-permute-start | bytes 786440 | tf_op jit(solution)/shard_map/ppermute | solution.py:294
  18.6 5.0 %collective-permute-start.4 = (bf16[1,128,1024]{2,1,0:T(8,128)(2,1)S(1)}, bf16[1,128,1024]{2,1,0:T(8,128)(2,1)S(1)}, u32[]{:S(2)}, u32[]{:S(2)}) collective-permute-start(bf16[1,128,1024]{2,1,0:T(8,128)(2,1)S(1)} %get-tuple-element.44), channel_id=1, source_target_pairs={{0,1},{1,0},{2,3},{3,2},{4,5},{5,4},{6,7},{7,6},{8,9},{9,8},{10,11... | collective-permute-start | bytes 786440 | tf_op jit(solution)/shard_map/ppermute | solution.py:294
  23.7 25.1 %copy-start = (bf16[128,2,1024]{2,1,0:T(2,128)(2,1)S(1)}, bf16[128,2,1024]{2,1,0:T(2,128)(2,1)}, u32[]{:S(2)}) copy-start(bf16[128,2,1024]{2,1,0:T(2,128)(2,1)} %rhs.3) | copy-start | bytes 1572868
  30.9 3.7 %collective-permute-start.10 = (bf16[2,128,1024]{2,1,0:T(8,128)(2,1)S(1)}, bf16[2,128,1024]{2,1,0:T(8,128)(2,1)S(1)}, u32[]{:S(2)}, u32[]{:S(2)}) collective-permute-start(bf16[2,128,1024]{2,1,0:T(8,128)(2,1)S(1)} %get-tuple-element.57), channel_id=1, source_target_pairs={{0,1},{1,0},{2,3},{3,2},{4,5},{5,4},{6,7},{7,6},{8,9},{9,8},{10,11... | collective-permute-start | bytes 1572872 | tf_op jit(solution)/shard_map/ppermute | solution.py:294
  31.4 4.8 %collective-permute-start.6 = (bf16[1,128,1024]{2,1,0:T(8,128)(2,1)S(1)}, bf16[1,128,1024]{2,1,0:T(8,128)(2,1)S(1)}, u32[]{:S(2)}, u32[]{:S(2)}) collective-permute-start(bf16[1,128,1024]{2,1,0:T(8,128)(2,1)S(1)} %get-tuple-element.47), channel_id=1, source_target_pairs={{0,1},{1,0},{2,3},{3,2},{4,5},{5,4},{6,7},{7,6},{8,9},{9,8},{10,11... | collective-permute-start | bytes 786440 | tf_op jit(solution)/shard_map/ppermute | solution.py:294
  31.5 15.1 %collective-permute-start.3 = (bf16[128,1024]{1,0:T(8,128)(2,1)S(1)}, bf16[128,1024]{1,0:T(8,128)(2,1)S(1)}, u32[]{:S(2)}, u32[]{:S(2)}) collective-permute-start(bf16[128,1024]{1,0:T(8,128)(2,1)S(1)} %fusion.1.refs_5_), channel_id=1, source_target_pairs={{0,4},{1,5},{2,6},{3,7},{4,0},{5,1},{6,2},{7,3},{8,12},{9,13},{10,... | collective-permute-start | bytes 786440 | tf_op jit(solution)/shard_map/ppermute | solution.py:294
  34.1 14.7 %collective-permute-start.5 = (bf16[128,1024]{1,0:T(8,128)(2,1)S(1)}, bf16[128,1024]{1,0:T(8,128)(2,1)S(1)}, u32[]{:S(2)}, u32[]{:S(2)}) collective-permute-start(bf16[128,1024]{1,0:T(8,128)(2,1)S(1)} %fusion.3.refs_6_), channel_id=1, source_target_pairs={{0,2},{1,3},{2,0},{3,1},{4,6},{5,7},{6,4},{7,5},{8,10},{9,11},{10,... | collective-permute-start | bytes 786440 | tf_op jit(solution)/shard_map/ppermute | solution.py:294
  34.6 19.2 %collective-permute-start.11 = (bf16[128,1024]{1,0:T(8,128)(2,1)S(1)}, bf16[128,1024]{1,0:T(8,128)(2,1)S(1)}, u32[]{:S(2)}, u32[]{:S(2)}) collective-permute-start(bf16[128,1024]{1,0:T(8,128)(2,1)S(1)} %fusion.4.refs_5_), channel_id=1, source_target_pairs={{0,2},{1,3},{2,0},{3,1},{4,6},{5,7},{6,4},{7,5},{8,10},{9,11},{10,... | collective-permute-start | bytes 786440 | tf_op jit(solution)/shard_map/ppermute | solution.py:294
  50.3 11.0 %collective-permute-start.9 = (bf16[128,1024]{1,0:T(8,128)(2,1)S(1)}, bf16[128,1024]{1,0:T(8,128)(2,1)S(1)}, u32[]{:S(2)}, u32[]{:S(2)}) collective-permute-start(bf16[128,1024]{1,0:T(8,128)(2,1)S(1)} %get-tuple-element.55), channel_id=1, source_target_pairs={{0,24},{8,16},{16,8},{24,0},{1,25},{9,17},{17,9},{25,1},{2,26},{10... | collective-permute-start | bytes 786440 | tf_op jit(solution)/shard_map/ppermute | solution.py:291
  52.8 10.8 %collective-permute-start.8 = (bf16[128,1024]{1,0:T(8,128)(2,1)S(1)}, bf16[128,1024]{1,0:T(8,128)(2,1)S(1)}, u32[]{:S(2)}, u32[]{:S(2)}) collective-permute-start(bf16[128,1024]{1,0:T(8,128)(2,1)S(1)} %get-tuple-element.54), channel_id=1, source_target_pairs={{0,16},{8,24},{16,0},{24,8},{1,17},{9,25},{17,1},{25,9},{2,18},{10... | collective-permute-start | bytes 786440 | tf_op jit(solution)/shard_map/ppermute | solution.py:291
  53.3 10.4 %collective-permute-start.7 = (bf16[128,1024]{1,0:T(8,128)(2,1)S(1)}, bf16[128,1024]{1,0:T(8,128)(2,1)S(1)}, u32[]{:S(2)}, u32[]{:S(2)}) collective-permute-start(bf16[128,1024]{1,0:T(8,128)(2,1)S(1)} %get-tuple-element.53.refs_7_), channel_id=1, source_target_pairs={{0,8},{8,0},{16,24},{24,16},{1,9},{9,1},{17,25},{25,17},{2,10},{10... | collective-permute-start | bytes 786440 | tf_op jit(solution)/shard_map/ppermute | solution.py:291
  61.2 6.2 %collective-permute-start.13 = (bf16[2,128,1024]{2,1,0:T(8,128)(2,1)S(1)}, bf16[2,128,1024]{2,1,0:T(8,128)(2,1)S(1)}, u32[]{:S(2)}, u32[]{:S(2)}) collective-permute-start(bf16[2,128,1024]{2,1,0:T(8,128)(2,1)S(1)} %get-tuple-element.60), channel_id=1, source_target_pairs={{0,1},{1,0},{2,3},{3,2},{4,5},{5,4},{6,7},{7,6},{8,9},{9,8},{10,11... | collective-permute-start | bytes 1572872 | tf_op jit(solution)/shard_map/ppermute | solution.py:294
  63.8 8.2 %collective-permute-start.15 = (bf16[128,1024]{1,0:T(8,128)(2,1)S(1)}, bf16[128,1024]{1,0:T(8,128)(2,1)S(1)}, u32[]{:S(2)}, u32[]{:S(2)}) collective-permute-start(bf16[128,1024]{1,0:T(8,128)(2,1)S(1)} %add_convert_fusion.2.refs_0_.first), channel_id=1, source_target_pairs={{0,16},{8,24},{16,0},{24,8},{1,17},{9,25},{17,1},{25,9},{2,18},{10... | collective-permute-start | bytes 786440 | tf_op jit(solution)/shard_map/ppermute | solution.py:291
  65.3 9.2 %collective-permute-start.16 = (bf16[128,1024]{1,0:T(8,128)(2,1)S(1)}, bf16[128,1024]{1,0:T(8,128)(2,1)S(1)}, u32[]{:S(2)}, u32[]{:S(2)}) collective-permute-start(bf16[128,1024]{1,0:T(8,128)(2,1)S(1)} %add_convert_fusion.2.refs_0_.first), channel_id=1, source_target_pairs={{0,8},{8,0},{16,24},{24,16},{1,9},{9,1},{17,25},{25,17},{2,10},{10... | collective-permute-start | bytes 786440 | tf_op jit(solution)/shard_map/ppermute | solution.py:291
  66.1 12.6 %collective-permute-start.17 = (bf16[128,1024]{1,0:T(8,128)(2,1)S(1)}, bf16[128,1024]{1,0:T(8,128)(2,1)S(1)}, u32[]{:S(2)}, u32[]{:S(2)}) collective-permute-start(bf16[128,1024]{1,0:T(8,128)(2,1)S(1)} %add_convert_fusion.2.refs_0_.first), channel_id=1, source_target_pairs={{0,24},{8,16},{16,8},{24,0},{1,25},{9,17},{17,9},{25,1},{2,26},{10... | collective-permute-start | bytes 786440 | tf_op jit(solution)/shard_map/ppermute | solution.py:291
  67.4 13.7 %collective-permute-start.12 = (bf16[128,1024]{1,0:T(8,128)(2,1)S(1)}, bf16[128,1024]{1,0:T(8,128)(2,1)S(1)}, u32[]{:S(2)}, u32[]{:S(2)}) collective-permute-start(bf16[128,1024]{1,0:T(8,128)(2,1)S(1)} %fusion.refs_6_), channel_id=1, source_target_pairs={{0,4},{1,5},{2,6},{3,7},{4,0},{5,1},{6,2},{7,3},{8,12},{9,13},{10,... | collective-permute-start | bytes 786440 | tf_op jit(solution)/shard_map/ppermute | solution.py:294
  67.5 13.5 %collective-permute-start.14 = (bf16[128,1024]{1,0:T(8,128)(2,1)S(1)}, bf16[128,1024]{1,0:T(8,128)(2,1)S(1)}, u32[]{:S(2)}, u32[]{:S(2)}) collective-permute-start(bf16[128,1024]{1,0:T(8,128)(2,1)S(1)} %get-tuple-element.68), channel_id=1, source_target_pairs={{0,2},{1,3},{2,0},{3,1},{4,6},{5,7},{6,4},{7,5},{8,10},{9,11},{10,... | collective-permute-start | bytes 786440 | tf_op jit(solution)/shard_map/ppermute | solution.py:294
  83.9 9.2 %collective-permute-start.18 = (bf16[128,1024]{1,0:T(8,128)(2,1)S(1)}, bf16[128,1024]{1,0:T(8,128)(2,1)S(1)}, u32[]{:S(2)}, u32[]{:S(2)}) collective-permute-start(bf16[128,1024]{1,0:T(8,128)(2,1)S(1)} %get-tuple-element.64), channel_id=1, source_target_pairs={{0,8},{8,0},{16,24},{24,16},{1,9},{9,1},{17,25},{25,17},{2,10},{10... | collective-permute-start | bytes 786440 | tf_op jit(solution)/shard_map/ppermute | solution.py:291
  85.6 13.4 %collective-permute-start.19 = (bf16[128,1024]{1,0:T(8,128)(2,1)S(1)}, bf16[128,1024]{1,0:T(8,128)(2,1)S(1)}, u32[]{:S(2)}, u32[]{:S(2)}) collective-permute-start(bf16[128,1024]{1,0:T(8,128)(2,1)S(1)} %get-tuple-element.65), channel_id=1, source_target_pairs={{0,16},{8,24},{16,0},{24,8},{1,17},{9,25},{17,1},{25,9},{2,18},{10... | collective-permute-start | bytes 786440 | tf_op jit(solution)/shard_map/ppermute | solution.py:291
  86.0 13.1 %collective-permute-start.20 = (bf16[128,1024]{1,0:T(8,128)(2,1)S(1)}, bf16[128,1024]{1,0:T(8,128)(2,1)S(1)}, u32[]{:S(2)}, u32[]{:S(2)}) collective-permute-start(bf16[128,1024]{1,0:T(8,128)(2,1)S(1)} %get-tuple-element.66), channel_id=1, source_target_pairs={{0,24},{8,16},{16,8},{24,0},{1,25},{9,17},{17,9},{25,1},{2,26},{10... | collective-permute-start | bytes 786440 | tf_op jit(solution)/shard_map/ppermute | solution.py:291

commit v2 on v1

--- a/solution.py
+++ b/solution.py
@@ -29,7 +29,7 @@
 
 
 def partial_kernel(cfg, *refs):
-    block, half, tile, load_p, load_x, group, following, ordered, blocks, extras, chips = cfg
+    block, low_row, half, tile, load_p, load_x, group, following, ordered, blocks, extras, chips = cfg
     refs = list(refs)
     place, solved = refs.pop(0)[0], refs.pop(0)
     x = None if load_x else refs.pop(0)
@@ -41,10 +41,10 @@
     send, keep = refs.pop(0), refs.pop(0)
     if load_p:
         held = [refs.pop(0)]
+    if load_x:
+        x = refs.pop(0)
     upcoming = refs.pop(0) if following else None
     fetched = [refs.pop(0) for _ in extras]
-    if load_x:
-        x = refs.pop(0)
     acc, sems = refs
     depth = solved.shape[1]
     piece = depth // PIECES
@@ -68,7 +68,7 @@
 
     def panel_copy(n, columns):
         rows = pl.ds(n * tile, tile)
-        return copy(panel.at[block, rows, columns], held[0].at[rows, columns])
+        return copy(panel.at[block, pl.ds(low_row + n * tile, tile), columns], held[0].at[rows, columns])
 
     units = []
     if load_x or load_p:
@@ -141,14 +141,14 @@
         arrive()
 
 
-def partial_sums(solved, x, panel, block, orders, place, group, following, half, chips, extras):
+def partial_sums(solved, x, panel, span, orders, place, group, following, half, chips, extras):
     load_x, load_p = x is None, not isinstance(panel, list)
     panels = [in_hbm(panel)] if load_p else panel
     depth = solved.shape[1]
-    width = panel.shape[1] if load_p else sum(part.shape[0] for part in panel)
+    block, low_row, width = span if load_p else (0, 0, sum(part.shape[0] for part in panel))
     count = len(group)
     rows = 2 * count * half
-    tile = tile_of(width // 2, 256)
+    tile = tile_of(width if load_p else panels[0].shape[0], 256)
     hbm, vmem = pl.BlockSpec(memory_space=pltpu.HBM), pl.BlockSpec(memory_space=pltpu.VMEM)
     operands = [place, in_hbm(solved)]
     in_specs = [pl.BlockSpec(memory_space=pltpu.SMEM), hbm]
@@ -167,17 +167,18 @@
     ]
     if load_p:
         shapes.append(jax.ShapeDtypeStruct((width, depth), panel.dtype))
+    if load_x:
+        shapes.append(jax.ShapeDtypeStruct((rows, depth), solved.dtype))
     if following:
         shapes.append(jax.ShapeDtypeStruct((2 * len(following) * half, depth), solved.dtype))
     shapes += [
         jax.ShapeDtypeStruct((size, array.shape[-1]), array.dtype) for array, _, _, size in extras
     ]
-    scratch = [pltpu.VMEM((rows, depth), solved.dtype)] if load_x else []
-    scratch.append(pltpu.VMEM((rows, tile), F32))
+    scratch = [pltpu.VMEM((rows, tile), F32)]
     copies = PIECES * (2 * count + 1) + width // tile + 2 * len(following) + PIECES * len(extras)
     scratch.append(pltpu.SemaphoreType.DMA((copies,)))
     cfg = (
-        block, half, tile, load_p, load_x, tuple(group), tuple(following), len(orders),
+        block, low_row, half, tile, load_p, load_x, tuple(group), tuple(following), len(orders),
         len(panels), tuple((layer, low) for _, layer, low, _ in extras), chips,
     )
     out = pl.pallas_call(
@@ -195,15 +196,18 @@
     )(*operands)
     out = list(out)
     send, keep = out.pop(0), out.pop(0)
-    held = [out.pop(0)] if load_p else panel
-    return send, keep, held, out.pop(0) if following else None, out
-
-
-def residual(b, rhs_ref, parts):
-    total = parts[0][...].astype(F32)
-    for part in parts[1:]:
-        total += part[...].astype(F32)
-    return rhs_ref[:, b, :].astype(F32) - total
+    held = [out.pop(0)] if load_p else []
+    if load_x:
+        x = out.pop(0)
+    return send, keep, held, out.pop(0) if following else x, out
+
+
+def residual(b, rhs_ref, parts, counts):
+    total, parts = rhs_ref[:, b, :].astype(F32), list(parts)
+    for count in counts:
+        pieces = [parts.pop(0)[...].astype(F32) for _ in range(count)]
+        total -= pieces[0] if count == 1 else jnp.concatenate(pieces, axis=1)
+    return total
 
 
 def blocks_of(mine, members, width):
@@ -213,11 +217,12 @@
     ]
 
 
-def solve_first_kernel(count, cols, place, rhs, *refs):
+def solve_first_kernel(counts, cols, place, rhs, *refs):
+    count = sum(counts)
     parts, inverse, outs = refs[:count], refs[count], refs[count + 1 :]
     members, width = len(outs), rhs.shape[2]
     at = blocks_of(place[0] // cols, members, width)
-    res = residual(0, rhs, parts).astype(BF16)
+    res = residual(0, rhs, parts, counts).astype(BF16)
     for offset in range(members - 1, -1, -1):
         d = jnp.dot(res, inverse[:, at[offset]], preferred_element_type=F32)
         outs[offset][...] = d.astype(outs[offset].dtype)
@@ -237,7 +242,8 @@
     out[...] = carry(firsts, link, at, offsets)
 
 
-def solve_second_kernel(count, members, offsets, cols, place, rhs, *refs):
+def solve_second_kernel(counts, members, offsets, cols, place, rhs, *refs):
+    count = sum(counts)
     parts, refs = refs[:count], refs[count:]
     early, refs = refs[0], refs[1:]
     firsts, refs = refs[: len(offsets)], refs[len(offsets) :]
@@ -246,7 +252,7 @@
     carried = early[...]
     if offsets:
         carried += carry(firsts, link, at, offsets)
-    res = (residual(1, rhs, parts) - carried).astype(BF16)
+    res = (residual(1, rhs, parts, counts) - carried).astype(BF16)
     for offset in range(members - 1, -1, -1):
         d = jnp.dot(res, inverse[:, at[offset]], preferred_element_type=F32)
         outs[offset][...] = d.astype(outs[offset].dtype)
@@ -278,8 +284,11 @@
 
 
 def plan_of(chips):
-    plan = [(0, [o]) for o in range(chips - 1, -1, -1)]
-    return plan + [(1, [o + 1, o] if chips > 1 else [o]) for o in range(max(chips - 2, 0), -1, -2)]
+    far = list(range(chips - 1, max(chips - 3, -1), -1))
+    plan = [(0, far, 0), (0, far, 1)]
+    plan += [(0, [o], None) for o in range(far[-1] - 1, -1, -1)]
+    pairs = [[o + 1, o] if chips > 1 else [o] for o in range(max(chips - 2, 0), -1, -2)]
+    return plan + [(1, pair, None) for pair in pairs]
 
 
 def local(members, chips, rhs, solved, panel, inverse, link):
@@ -297,49 +306,64 @@
     last = len(plan) - 1
 
     extras = [[] for _ in plan]
-    extras[chips].append(("inverse", inverse, 0, 0, width))
+    ahead = [n for n, (b, _, _) in enumerate(plan) if b == 0]
+    extras[min(len(ahead), last - 1)].append(("inverse", inverse, 0, 0, width))
     piece = width // 2
-    extras[max(0, chips - 2)].append(("low", panel, 1, 0, piece))
-    extras[chips - 1].append(("high", panel, 1, piece, piece))
+    extras[ahead[-2]].append(("low", panel, 1, 0, piece))
+    extras[ahead[-1]].append(("high", panel, 1, piece, piece))
     extras[last].append(("link", link, None, 0, width))
     extras[last].append(("second", inverse, 1, 0, width))
 
     flops = 2 * half * width * width * members
-    sums, kept, passing = [[], []], {}, {}
+    kept, passing = {}, {}
+    sums = [{}, {}]
     due = [[] for _ in plan]
-    x, held = None, panel
-    for n, (b, group) in enumerate(plan):
-        if b == 1 and plan[n - 1][0] == 0:
-            held = [kept["low"], kept["high"]]
-        following = plan[n + 1][1] if n < last else []
+
+    def term(b, key, value):
+        sums[b].setdefault(key, []).append(value)
+
+    def counts(b):
+        return tuple(len(pieces) for pieces in sums[b].values())
+
+    def flat(b):
+        return [value for pieces in sums[b].values() for value in pieces]
+
+    x, blocks = None, []
+    for n, (b, group, part) in enumerate(plan):
+        if n == len(ahead):
+            blocks = [kept["low"], kept["high"]]
+        follows = n < last and plan[n + 1][1] != group
+        following = plan[n + 1][1] if follows else []
         orders = due[n]
         if n == last:
             parts = solve(
-                functools.partial(solve_first_kernel, len(sums[0]), cols),
-                flops, place, rhs, sums[0], [kept["inverse"]], members,
+                functools.partial(solve_first_kernel, counts(0), cols),
+                flops, place, rhs, flat(0), [kept["inverse"]], members,
             )
             orders = due[n] + [parts[members > 1]]
+        span = None if part is None else (b, part * piece, piece)
         send, keep, held, x, got = partial_sums(
-            solved, x, held, b, orders, place,
+            solved, x, blocks if part is None else panel, span, orders, place,
             group, following, half, chips, [e[1:] for e in extras[n]],
         )
+        blocks = blocks + held
         kept.update(zip([e[0] for e in extras[n]], got))
         other = across_col(send, 1)
         for at, offset in enumerate(group):
-            pair = keep[at], other[at]
             if offset == 0:
-                sums[b] += pair
+                term(b, "own", keep[at])
+                term(b, "swap", other[at])
                 continue
-            value = pair[0] + pair[1].astype(F32)
+            value = keep[at] + other[at].astype(F32)
             if offset % 2 == 0:
-                value += passing.pop((b, offset)).astype(F32)
+                value += passing.pop((b, offset, part)).astype(F32)
             value = value.astype(BF16)
             due[min(last, n + (2 if offset % 2 else 3))].append(value)
             arrived = across_col(value, 2 if offset % 2 else 2 * offset)
             if offset > 1 and offset % 2:
-                passing[b, offset - 1] = arrived
+                passing[b, offset - 1, part] = arrived
             else:
-                sums[b].append(arrived)
+                term(b, offset, arrived)
 
     total = parts[0]
     for offset in range(1, members):
@@ -361,8 +385,8 @@
         ),
     )(place, *[firsts[o] for o in early], kept["link"])
     parts = solve(
-        functools.partial(solve_second_kernel, len(sums[1]), members, late, cols),
-        2 * flops, place, rhs, sums[1],
+        functools.partial(solve_second_kernel, counts(1), members, late, cols),
+        2 * flops, place, rhs, flat(1),
         [carried] + [firsts[o] for o in late] + [kept["link"], kept["second"]], members,
     )
     arrived = [across_row(parts[offset], offset) for offset in range(1, members)]

time: 100 us -> 104 us (1.040)
  starting transfers between devices: 22 us -> 25.8 us
  Pallas kernels: 41 us -> 42.7 us
  waiting for transfers between devices: 36.4 us -> 34.7 us
    ppermute x12 -> x14, starting transfers between devices: 11.4 us -> 15.1 us  [across_col(): return lax.ppermute(value, 'col', [(i, i ^ offset) for i in range(cols)])]
    ppermute x9, waiting for transfers between devices: 21.5 us -> 18.4 us  [across_row(): return lax.ppermute(value, 'row', [(i, i ^ offset) for i in range(members)])]
    pallas_call x6, Pallas kernels: 33.9 us -> 35.6 us  [partial_sums(): pl.pallas_call(functools.partial(partial_kernel, cfg), in_specs=in_specs,...]
    ppermute x12 -> x14, waiting for transfers between devices: 14.9 us -> 16.3 us  [across_col(): return lax.ppermute(value, 'col', [(i, i ^ offset) for i in range(cols)])]
  transfers between devices with their start and end apart: 21 -> 23, of which waited for: 10 -> 11; matrix products, arithmetic and copies ran while one was open for 1% -> 1% of each run, Pallas kernels for 23% -> 24%
where the time goes in v2:
time: 104 us
  Pallas kernels  42.7 us (41%)
  waiting for transfers between devices  34.7 us (33%)
  starting transfers between devices  25.8 us (25%)
    pallas_call x6, Pallas kernels, partial_sums(): pl.pallas_call(functools.partial(partial_kernel, cfg), in_specs=in_specs,...  35.6 us
    ppermute x9, waiting for transfers between devices, across_row(): return lax.ppermute(value, 'row', [(i, i ^ offset) for i in range(members)])  18.4 us
    ppermute x14, waiting for transfers between devices, across_col(): return lax.ppermute(value, 'col', [(i, i ^ offset) for i in range(cols)])  16.3 us
    ppermute x14, starting transfers between devices, across_col(): return lax.ppermute(value, 'col', [(i, i ^ offset) for i in range(cols)])  15.1 us
    ppermute x9, starting transfers between devices, across_row(): return lax.ppermute(value, 'row', [(i, i ^ offset) for i in range(members)])  10.7 us
    pallas_call x2, Pallas kernels, solve(): pl.pallas_call(kernel, in_specs=[pl.BlockSpec(memory_space=pltpu.SMEM)] +...  4.36 us
  transfers between devices with their start and end apart: 23, of which 11 were waited for; matrix products, arithmetic and copies ran while one was open for 1% of the time, Pallas kernels for 24%

profile of v2, /device:TPU:0, one launch (start us, length us, event | category | flops | bytes accessed | tf_op | source)
XLA Modules:
  0.0 104.0 jit_solution(5345676867094329291)
XLA Ops:
  0.0 6.9 %shard_map.55 = (bf16[2,128,512]{2,1,0:T(8,128)(2,1)S(1)}, f32[2,128,512]{2,1,0:T(8,128)S(1)}, bf16[512,6144]{1,0:T(8,128)(2,1)S(1)}, bf16[512,6144]{1,0:T(8,128)(2,1)S(1)}) custom-call(s32[1]{0:T(128)} %bitcast.refs_0_.place, bf16[1024,6144]{1,0:T(8,128)(2,1)} %refs_1_.11, bf16[2,1024,6144]{2,1,0:T(8,128)(2,1)} %refs_7_.2), custom_call_target="tpu_custom_call" | custom-call | flops 3221225472 | bytes 12582912 | tf_op jit(solution)/shard_map/pallas_call | solution.py:184
  6.9 0.6 collective-permute-start
  7.5 5.7 %shard_map.56 = (bf16[2,128,512]{2,1,0:T(8,128)(2,1)S(1)}, f32[2,128,512]{2,1,0:T(8,128)S(1)}, bf16[512,6144]{1,0:T(8,128)(2,1)S(1)}, bf16[256,6144]{1,0:T(8,128)(2,1)S(1)}) custom-call(s32[1]{0:T(128)} %bitcast.refs_0_.place, bf16[1024,6144]{1,0:T(8,128)(2,1)} %refs_1_.11, bf16[512,6144]{1,0:T(8,128)(2,1)S(1)} %get-tuple-element.39.refs_2_, ...), custom_call_target="tpu_custom_call" | custom-call | flops 3221225472 | bytes 12582912 | tf_op jit(solution)/shard_map/pallas_call | solution.py:184
  13.3 3.1 %collective-permute-start.1 = (bf16[128,512]{1,0:T(8,128)(2,1)S(1)}, bf16[128,512]{1,0:T(8,128)(2,1)S(1)}, u32[]{:S(2)}, u32[]{:S(2)}) collective-permute-start(bf16[128,512]{1,0:T(8,128)(2,1)S(1)} %fusion.6.refs_5_), channel_id=1, source_target_pairs={{0,2},{1,3},{2,0},{3,1},{4,6},{5,7},{6,4},{7,5},{8,10},{9,11},{10,... | collective-permute-start | bytes 393224 | tf_op jit(solution)/shard_map/ppermute | solution.py:303
  16.5 1.1 %collective-permute-start.4 = (bf16[128,512]{1,0:T(8,128)(2,1)S(1)}, bf16[128,512]{1,0:T(8,128)(2,1)S(1)}, u32[]{:S(2)}, u32[]{:S(2)}) collective-permute-start(bf16[128,512]{1,0:T(8,128)(2,1)S(1)} %fusion.7.refs_6_), channel_id=1, source_target_pairs={{0,2},{1,3},{2,0},{3,1},{4,6},{5,7},{6,4},{7,5},{8,10},{9,11},{10,... | collective-permute-start | bytes 393224 | tf_op jit(solution)/shard_map/ppermute | solution.py:303
  17.6 3.9 %shard_map.57 = (bf16[1,128,1024]{2,1,0:T(8,128)(2,1)S(1)}, f32[1,128,1024]{2,1,0:T(8,128)S(1)}, bf16[256,6144]{1,0:T(8,128)(2,1)S(1)}, bf16[512,6144]{1,0:T(8,128)(2,1)S(1)}) custom-call(s32[1]{0:T(128)} %bitcast.refs_0_.place, bf16[1024,6144]{1,0:T(8,128)(2,1)} %refs_1_.11, bf16[256,6144]{1,0:T(8,128)(2,1)S(1)} %get-tuple-element.42.refs_2_, ...), custom_call_target="tpu_custom_call" | custom-call | flops 3221225472 | bytes 15728640 | tf_op jit(solution)/shard_map/pallas_call | solution.py:184
  21.8 4.9 %shard_map.58 = (bf16[1,128,1024]{2,1,0:T(8,128)(2,1)S(1)}, f32[1,128,1024]{2,1,0:T(8,128)S(1)}, bf16[512,6144]{1,0:T(8,128)(2,1)S(1)}, bf16[512,6144]{1,0:T(8,128)(2,1)S(1)}) custom-call(s32[1]{0:T(128)} %bitcast.refs_0_.place, bf16[1024,6144]{1,0:T(8,128)(2,1)} %refs_1_.11, bf16[256,6144]{1,0:T(8,128)(2,1)S(1)} %get-tuple-element.47.refs_2_, ...), custom_call_target="tpu_custom_call" | custom-call | flops 3221225472 | bytes 15728640 | tf_op jit(solution)/shard_map/pallas_call | solution.py:184
  26.8 7.0 %shard_map.59 = (bf16[2,128,1024]{2,1,0:T(8,128)(2,1)S(1)}, f32[2,128,1024]{2,1,0:T(8,128)S(1)}, bf16[512,6144]{1,0:T(8,128)(2,1)S(1)}, bf16[1024,4096]{1,0:T(8,128)(2,1)S(1)}) custom-call(s32[1]{0:T(128)} %bitcast.refs_0_.place, bf16[1024,6144]{1,0:T(8,128)(2,1)} %refs_1_.11, bf16[512,6144]{1,0:T(8,128)(2,1)S(1)} %get-tuple-element.50.refs_2_, ...), custom_call_target="tpu_custom_call" | custom-call | flops 6442450944 | bytes 18874368 | tf_op jit(solution)/shard_map/pallas_call | solution.py:184
  34.4 1.1 %collective-permute-start.7 = (bf16[128,1024]{1,0:T(8,128)(2,1)S(1)}, bf16[128,1024]{1,0:T(8,128)(2,1)S(1)}, u32[]{:S(2)}, u32[]{:S(2)}) collective-permute-start(bf16[128,1024]{1,0:T(8,128)(2,1)S(1)} %fusion.1.refs_6_), channel_id=1, source_target_pairs={{0,2},{1,3},{2,0},{3,1},{4,6},{5,7},{6,4},{7,5},{8,10},{9,11},{10,... | collective-permute-start | bytes 786440 | tf_op jit(solution)/shard_map/ppermute | solution.py:303
  35.9 1.1 %collective-permute-start.13 = (bf16[128,1024]{1,0:T(8,128)(2,1)S(1)}, bf16[128,1024]{1,0:T(8,128)(2,1)S(1)}, u32[]{:S(2)}, u32[]{:S(2)}) collective-permute-start(bf16[128,1024]{1,0:T(8,128)(2,1)S(1)} %fusion.2.refs_5_), channel_id=1, source_target_pairs={{0,2},{1,3},{2,0},{3,1},{4,6},{5,7},{6,4},{7,5},{8,10},{9,11},{10,... | collective-permute-start | bytes 786440 | tf_op jit(solution)/shard_map/ppermute | solution.py:303
  37.0 2.6 %collective-permute-start.2 = (bf16[128,512]{1,0:T(8,128)(2,1)S(1)}, bf16[128,512]{1,0:T(8,128)(2,1)S(1)}, u32[]{:S(2)}, u32[]{:S(2)}) collective-permute-start(bf16[128,512]{1,0:T(8,128)(2,1)S(1)} %fusion.5.refs_5_), channel_id=1, source_target_pairs={{0,4},{1,5},{2,6},{3,7},{4,0},{5,1},{6,2},{7,3},{8,12},{9,13},{10,... | collective-permute-start | bytes 393224 | tf_op jit(solution)/shard_map/ppermute | solution.py:303
  39.9 10.7 %collective-permute-done.2.refs_0_ = bf16[128,512]{1,0:T(8,128)(2,1)S(1)} collective-permute-done((bf16[128,512]{1,0:T(8,128)(2,1)S(1)}, bf16[128,512]{1,0:T(8,128)(2,1)S(1)}, u32[]{:S(2)}, u32[]{:S(2)}) %collective-permute-start.2) | collective-permute-done | bytes 131104 | tf_op jit(solution)/shard_map/ppermute | solution.py:303
  50.6 2.1 %collective-permute-done.5.refs_1_ = bf16[128,512]{1,0:T(8,128)(2,1)S(1)} collective-permute-done((bf16[128,512]{1,0:T(8,128)(2,1)S(1)}, bf16[128,512]{1,0:T(8,128)(2,1)S(1)}, u32[]{:S(2)}, u32[]{:S(2)}) %collective-permute-start.5) | collective-permute-done | bytes 131104 | tf_op jit(solution)/shard_map/ppermute | solution.py:303
  52.7 1.5 %shard_map.60 = (f32[128,1024]{1,0:T(8,128)S(1)}, bf16[128,1024]{1,0:T(8,128)(2,1)S(1)}, bf16[128,1024]{1,0:T(8,128)(2,1)S(1)}, bf16[128,1024]{1,0:T(8,128)(2,1)S(1)}) custom-call(s32[1]{0:T(128)} %bitcast.refs_0_.place, bf16[128,2,1024]{2,1,0:T(2,128)(2,1)S(1)} %copy-done, bf16[128,512]{1,0:T(8,128)(2,1)S(1)} %collective-permute-done.2.refs_0_, ...), custom_call_target="tpu_custom_call" | custom-call | flops 1073741824 | bytes 8388608 | tf_op jit(solution)/shard_map/pallas_call | solution.py:267
  54.2 2.5 %collective-permute-start.11 = (bf16[128,1024]{1,0:T(8,128)(2,1)S(1)}, bf16[128,1024]{1,0:T(8,128)(2,1)S(1)}, u32[]{:S(2)}, u32[]{:S(2)}) collective-permute-start(bf16[128,1024]{1,0:T(8,128)(2,1)S(1)} %get-tuple-element.57), channel_id=1, source_target_pairs={{0,24},{8,16},{16,8},{24,0},{1,25},{9,17},{17,9},{25,1},{2,26},{10... | collective-permute-start | bytes 786440 | tf_op jit(solution)/shard_map/ppermute | solution.py:300
  57.9 7.2 %shard_map.61 = (bf16[2,128,1024]{2,1,0:T(8,128)(2,1)S(1)}, f32[2,128,1024]{2,1,0:T(8,128)S(1)}, bf16[1024,4096]{1,0:T(8,128)(2,1)S(1)}, bf16[1024,4096]{1,0:T(8,128)(2,1)S(1)}) custom-call(s32[1]{0:T(128)} %bitcast.refs_0_.place, bf16[1024,6144]{1,0:T(8,128)(2,1)} %refs_1_.11, bf16[512,6144]{1,0:T(8,128)(2,1)S(1)} %get-tuple-element.60.refs_2_, ...), custom_call_target="tpu_custom_call" | custom-call | flops 6442450944 | bytes 18874368 | tf_op jit(solution)/shard_map/pallas_call | solution.py:184
  65.2 3.3 %collective-permute-done.10 = bf16[128,1024]{1,0:T(8,128)(2,1)S(1)} collective-permute-done((bf16[128,1024]{1,0:T(8,128)(2,1)S(1)}, bf16[128,1024]{1,0:T(8,128)(2,1)S(1)}, u32[]{:S(2)}, u32[]{:S(2)}) %collective-permute-start.10) | collective-permute-done | bytes 262176 | tf_op jit(solution)/shard_map/ppermute | solution.py:300
  68.7 1.5 %collective-permute-start.17 = (bf16[128,1024]{1,0:T(8,128)(2,1)S(1)}, bf16[128,1024]{1,0:T(8,128)(2,1)S(1)}, u32[]{:S(2)}, u32[]{:S(2)}) collective-permute-start(bf16[128,1024]{1,0:T(8,128)(2,1)S(1)} %add_convert_fusion.2.refs_0_.first), channel_id=1, source_target_pairs={{0,16},{8,24},{16,0},{24,8},{1,17},{9,25},{17,1},{25,9},{2,18},{10... | collective-permute-start | bytes 786440 | tf_op jit(solution)/shard_map/ppermute | solution.py:300
  70.2 0.8 collective-permute-start.18
  71.0 1.3 %collective-permute-start.19 = (bf16[128,1024]{1,0:T(8,128)(2,1)S(1)}, bf16[128,1024]{1,0:T(8,128)(2,1)S(1)}, u32[]{:S(2)}, u32[]{:S(2)}) collective-permute-start(bf16[128,1024]{1,0:T(8,128)(2,1)S(1)} %add_convert_fusion.2.refs_0_.first), channel_id=1, source_target_pairs={{0,24},{8,16},{16,8},{24,0},{1,25},{9,17},{17,9},{25,1},{2,26},{10... | collective-permute-start | bytes 786440 | tf_op jit(solution)/shard_map/ppermute | solution.py:300
  72.2 3.4 %collective-permute-start.14 = (bf16[128,1024]{1,0:T(8,128)(2,1)S(1)}, bf16[128,1024]{1,0:T(8,128)(2,1)S(1)}, u32[]{:S(2)}, u32[]{:S(2)}) collective-permute-start(bf16[128,1024]{1,0:T(8,128)(2,1)S(1)} %fusion.refs_6_), channel_id=1, source_target_pairs={{0,4},{1,5},{2,6},{3,7},{4,0},{5,1},{6,2},{7,3},{8,12},{9,13},{10,... | collective-permute-start | bytes 786440 | tf_op jit(solution)/shard_map/ppermute | solution.py:303
  75.7 0.9 collective-permute-start.16
  77.0 1.5 %carry.1.refs_4_ = f32[128,1024]{1,0:T(8,128)S(1)} custom-call(s32[1]{0:T(128)} %bitcast.refs_0_.place, bf16[128,1024]{1,0:T(8,128)(2,1)S(1)} %add_convert_fusion.2.refs_0_.first, bf16[128,1024]{1,0:T(8,128)(2,1)S(1)} %collective-permute-done.17.refs_1_, bf16[1024,4096]{1,0:T(8,128)(2,1)S(1)} %get-tuple-element.63.refs_2_.refs_7_), custom_call_target="tpu_custom_call" | custom-call | flops 268435456 | bytes 1048576 | tf_op jit(solution)/shard_map/carry/pallas_call | solution.py:376
  78.6 0.8 collective-permute-done.18.refs_5_
  79.3 4.3 %collective-permute-done.19.refs_6_ = bf16[128,1024]{1,0:T(8,128)(2,1)S(1)} collective-permute-done((bf16[128,1024]{1,0:T(8,128)(2,1)S(1)}, bf16[128,1024]{1,0:T(8,128)(2,1)S(1)}, u32[]{:S(2)}, u32[]{:S(2)}) %collective-permute-start.19) | collective-permute-done | bytes 262176 | tf_op jit(solution)/shard_map/ppermute | solution.py:300
  83.7 3.1 %collective-permute-done.14.refs_0_ = bf16[128,1024]{1,0:T(8,128)(2,1)S(1)} collective-permute-done((bf16[128,1024]{1,0:T(8,128)(2,1)S(1)}, bf16[128,1024]{1,0:T(8,128)(2,1)S(1)}, u32[]{:S(2)}, u32[]{:S(2)}) %collective-permute-start.14) | collective-permute-done | bytes 262176 | tf_op jit(solution)/shard_map/ppermute | solution.py:303
  86.8 2.9 %shard_map.62 = (f32[128,1024]{1,0:T(8,128)S(1)}, bf16[128,1024]{1,0:T(8,128)(2,1)S(1)}, bf16[128,1024]{1,0:T(8,128)(2,1)S(1)}, bf16[128,1024]{1,0:T(8,128)(2,1)S(1)}) custom-call(s32[1]{0:T(128)} %bitcast.refs_0_.place, bf16[128,2,1024]{2,1,0:T(2,128)(2,1)S(1)} %copy-done, bf16[128,1024]{1,0:T(8,128)(2,1)S(1)} %collective-permute-done.14.refs_0_, ...), custom_call_target="tpu_custom_call" | custom-call | flops 2147483648 | bytes 16777216 | tf_op jit(solution)/shard_map/pallas_call | solution.py:267
  89.7 1.6 %collective-permute-start.20 = (bf16[128,1024]{1,0:T(8,128)(2,1)S(1)}, bf16[128,1024]{1,0:T(8,128)(2,1)S(1)}, u32[]{:S(2)}, u32[]{:S(2)}) collective-permute-start(bf16[128,1024]{1,0:T(8,128)(2,1)S(1)} %get-tuple-element.66), channel_id=1, source_target_pairs={{0,8},{8,0},{16,24},{24,16},{1,9},{9,1},{17,25},{25,17},{2,10},{10... | collective-permute-start | bytes 786440 | tf_op jit(solution)/shard_map/ppermute | solution.py:300
  91.6 1.6 %collective-permute-start.22 = (bf16[128,1024]{1,0:T(8,128)(2,1)S(1)}, bf16[128,1024]{1,0:T(8,128)(2,1)S(1)}, u32[]{:S(2)}, u32[]{:S(2)}) collective-permute-start(bf16[128,1024]{1,0:T(8,128)(2,1)S(1)} %get-tuple-element.68), channel_id=1, source_target_pairs={{0,24},{8,16},{16,8},{24,0},{1,25},{9,17},{17,9},{25,1},{2,26},{10... | collective-permute-start | bytes 786440 | tf_op jit(solution)/shard_map/ppermute | solution.py:300
  93.2 5.3 %collective-permute-done.20.refs_1_ = bf16[128,1024]{1,0:T(8,128)(2,1)S(1)} collective-permute-done((bf16[128,1024]{1,0:T(8,128)(2,1)S(1)}, bf16[128,1024]{1,0:T(8,128)(2,1)S(1)}, u32[]{:S(2)}, u32[]{:S(2)}) %collective-permute-start.20) | collective-permute-done | bytes 262176 | tf_op jit(solution)/shard_map/ppermute | solution.py:300
  98.5 4.3 %collective-permute-done.21.refs_2_ = bf16[128,1024]{1,0:T(8,128)(2,1)S(1)} collective-permute-done((bf16[128,1024]{1,0:T(8,128)(2,1)S(1)}, bf16[128,1024]{1,0:T(8,128)(2,1)S(1)}, u32[]{:S(2)}, u32[]{:S(2)}) %collective-permute-start.21) | collective-permute-done | bytes 262176 | tf_op jit(solution)/shard_map/ppermute | solution.py:300
  102.8 1.2 %result.1 = bf16[128,2,1024]{2,1,0:T(2,128)(2,1)} custom-call(bf16[128,1024]{1,0:T(8,128)(2,1)S(1)} %add_convert_fusion.2.refs_0_.first, f32[128,1024]{1,0:T(8,128)S(1)} %get-tuple-element.65.refs_0_, bf16[128,1024]{1,0:T(8,128)(2,1)S(1)} %collective-permute-done.20.refs_1_, bf16[128,1024]{1,0:T(8,128)(2,1)S(1)} %collective-permute-done.21.refs_2_, ...), custom_call_target="tpu_custom_call" | custom-call | tf_op jit(solution)/shard_map/result/pallas_call | solution.py:393
  (36 shorter events, 4.1 us)
Async XLA Ops:
  6.9 6.4 %collective-permute-start = (bf16[2,128,512]{2,1,0:T(8,128)(2,1)S(1)}, bf16[2,128,512]{2,1,0:T(8,128)(2,1)S(1)}, u32[]{:S(2)}, u32[]{:S(2)}) collective-permute-start(bf16[2,128,512]{2,1,0:T(8,128)(2,1)S(1)} %get-tuple-element.38), channel_id=1, source_target_pairs={{0,1},{1,0},{2,3},{3,2},{4,5},{5,4},{6,7},{7,6},{8,9},{9,8},{10,11... | collective-permute-start | bytes 786440 | tf_op jit(solution)/shard_map/ppermute | solution.py:303
  13.2 3.2 %collective-permute-start.3 = (bf16[2,128,512]{2,1,0:T(8,128)(2,1)S(1)}, bf16[2,128,512]{2,1,0:T(8,128)(2,1)S(1)}, u32[]{:S(2)}, u32[]{:S(2)}) collective-permute-start(bf16[2,128,512]{2,1,0:T(8,128)(2,1)S(1)} %get-tuple-element.41), channel_id=1, source_target_pairs={{0,1},{1,0},{2,3},{3,2},{4,5},{5,4},{6,7},{7,6},{8,9},{9,8},{10,11... | collective-permute-start | bytes 786440 | tf_op jit(solution)/shard_map/ppermute | solution.py:303
  13.3 8.4 %collective-permute-start.1 = (bf16[128,512]{1,0:T(8,128)(2,1)S(1)}, bf16[128,512]{1,0:T(8,128)(2,1)S(1)}, u32[]{:S(2)}, u32[]{:S(2)}) collective-permute-start(bf16[128,512]{1,0:T(8,128)(2,1)S(1)} %fusion.6.refs_5_), channel_id=1, source_target_pairs={{0,2},{1,3},{2,0},{3,1},{4,6},{5,7},{6,4},{7,5},{8,10},{9,11},{10,... | collective-permute-start | bytes 393224 | tf_op jit(solution)/shard_map/ppermute | solution.py:303
  16.5 10.2 %collective-permute-start.4 = (bf16[128,512]{1,0:T(8,128)(2,1)S(1)}, bf16[128,512]{1,0:T(8,128)(2,1)S(1)}, u32[]{:S(2)}, u32[]{:S(2)}) collective-permute-start(bf16[128,512]{1,0:T(8,128)(2,1)S(1)} %fusion.7.refs_6_), channel_id=1, source_target_pairs={{0,2},{1,3},{2,0},{3,1},{4,6},{5,7},{6,4},{7,5},{8,10},{9,11},{10,... | collective-permute-start | bytes 393224 | tf_op jit(solution)/shard_map/ppermute | solution.py:303
  21.6 5.2 %collective-permute-start.6 = (bf16[1,128,1024]{2,1,0:T(8,128)(2,1)S(1)}, bf16[1,128,1024]{2,1,0:T(8,128)(2,1)S(1)}, u32[]{:S(2)}, u32[]{:S(2)}) collective-permute-start(bf16[1,128,1024]{2,1,0:T(8,128)(2,1)S(1)} %get-tuple-element.46), channel_id=1, source_target_pairs={{0,1},{1,0},{2,3},{3,2},{4,5},{5,4},{6,7},{7,6},{8,9},{9,8},{10,11... | collective-permute-start | bytes 786440 | tf_op jit(solution)/shard_map/ppermute | solution.py:303
  26.8 25.9 %copy-start = (bf16[128,2,1024]{2,1,0:T(2,128)(2,1)S(1)}, bf16[128,2,1024]{2,1,0:T(2,128)(2,1)}, u32[]{:S(2)}) copy-start(bf16[128,2,1024]{2,1,0:T(2,128)(2,1)} %rhs.3) | copy-start | bytes 1572868
  33.8 2.0 %collective-permute-start.12 = (bf16[2,128,1024]{2,1,0:T(8,128)(2,1)S(1)}, bf16[2,128,1024]{2,1,0:T(8,128)(2,1)S(1)}, u32[]{:S(2)}, u32[]{:S(2)}) collective-permute-start(bf16[2,128,1024]{2,1,0:T(8,128)(2,1)S(1)} %get-tuple-element.59), channel_id=1, source_target_pairs={{0,1},{1,0},{2,3},{3,2},{4,5},{5,4},{6,7},{7,6},{8,9},{9,8},{10,11... | collective-permute-start | bytes 1572872 | tf_op jit(solution)/shard_map/ppermute | solution.py:303
  34.3 18.4 %collective-permute-start.8 = (bf16[1,128,1024]{2,1,0:T(8,128)(2,1)S(1)}, bf16[1,128,1024]{2,1,0:T(8,128)(2,1)S(1)}, u32[]{:S(2)}, u32[]{:S(2)}) collective-permute-start(bf16[1,128,1024]{2,1,0:T(8,128)(2,1)S(1)} %get-tuple-element.49), channel_id=1, source_target_pairs={{0,1},{1,0},{2,3},{3,2},{4,5},{5,4},{6,7},{7,6},{8,9},{9,8},{10,11... | collective-permute-start | bytes 786440 | tf_op jit(solution)/shard_map/ppermute | solution.py:303
  34.4 18.4 %collective-permute-start.7 = (bf16[128,1024]{1,0:T(8,128)(2,1)S(1)}, bf16[128,1024]{1,0:T(8,128)(2,1)S(1)}, u32[]{:S(2)}, u32[]{:S(2)}) collective-permute-start(bf16[128,1024]{1,0:T(8,128)(2,1)S(1)} %fusion.1.refs_6_), channel_id=1, source_target_pairs={{0,2},{1,3},{2,0},{3,1},{4,6},{5,7},{6,4},{7,5},{8,10},{9,11},{10,... | collective-permute-start | bytes 786440 | tf_op jit(solution)/shard_map/ppermute | solution.py:303
  35.9 21.9 %collective-permute-start.13 = (bf16[128,1024]{1,0:T(8,128)(2,1)S(1)}, bf16[128,1024]{1,0:T(8,128)(2,1)S(1)}, u32[]{:S(2)}, u32[]{:S(2)}) collective-permute-start(bf16[128,1024]{1,0:T(8,128)(2,1)S(1)} %fusion.2.refs_5_), channel_id=1, source_target_pairs={{0,2},{1,3},{2,0},{3,1},{4,6},{5,7},{6,4},{7,5},{8,10},{9,11},{10,... | collective-permute-start | bytes 786440 | tf_op jit(solution)/shard_map/ppermute | solution.py:303
  37.0 13.6 %collective-permute-start.2 = (bf16[128,512]{1,0:T(8,128)(2,1)S(1)}, bf16[128,512]{1,0:T(8,128)(2,1)S(1)}, u32[]{:S(2)}, u32[]{:S(2)}) collective-permute-start(bf16[128,512]{1,0:T(8,128)(2,1)S(1)} %fusion.5.refs_5_), channel_id=1, source_target_pairs={{0,4},{1,5},{2,6},{3,7},{4,0},{5,1},{6,2},{7,3},{8,12},{9,13},{10,... | collective-permute-start | bytes 393224 | tf_op jit(solution)/shard_map/ppermute | solution.py:303
  39.6 13.1 %collective-permute-start.5 = (bf16[128,512]{1,0:T(8,128)(2,1)S(1)}, bf16[128,512]{1,0:T(8,128)(2,1)S(1)}, u32[]{:S(2)}, u32[]{:S(2)}) collective-permute-start(bf16[128,512]{1,0:T(8,128)(2,1)S(1)} %fusion.4.refs_5_), channel_id=1, source_target_pairs={{0,4},{1,5},{2,6},{3,7},{4,0},{5,1},{6,2},{7,3},{8,12},{9,13},{10,... | collective-permute-start | bytes 393224 | tf_op jit(solution)/shard_map/ppermute | solution.py:303
  54.2 11.0 %collective-permute-start.11 = (bf16[128,1024]{1,0:T(8,128)(2,1)S(1)}, bf16[128,1024]{1,0:T(8,128)(2,1)S(1)}, u32[]{:S(2)}, u32[]{:S(2)}) collective-permute-start(bf16[128,1024]{1,0:T(8,128)(2,1)S(1)} %get-tuple-element.57), channel_id=1, source_target_pairs={{0,24},{8,16},{16,8},{24,0},{1,25},{9,17},{17,9},{25,1},{2,26},{10... | collective-permute-start | bytes 786440 | tf_op jit(solution)/shard_map/ppermute | solution.py:300
  56.7 11.7 %collective-permute-start.10 = (bf16[128,1024]{1,0:T(8,128)(2,1)S(1)}, bf16[128,1024]{1,0:T(8,128)(2,1)S(1)}, u32[]{:S(2)}, u32[]{:S(2)}) collective-permute-start(bf16[128,1024]{1,0:T(8,128)(2,1)S(1)} %get-tuple-element.56), channel_id=1, source_target_pairs={{0,16},{8,24},{16,0},{24,8},{1,17},{9,25},{17,1},{25,9},{2,18},{10... | collective-permute-start | bytes 786440 | tf_op jit(solution)/shard_map/ppermute | solution.py:300
  57.2 11.3 %collective-permute-start.9 = (bf16[128,1024]{1,0:T(8,128)(2,1)S(1)}, bf16[128,1024]{1,0:T(8,128)(2,1)S(1)}, u32[]{:S(2)}, u32[]{:S(2)}) collective-permute-start(bf16[128,1024]{1,0:T(8,128)(2,1)S(1)} %get-tuple-element.55.refs_7_), channel_id=1, source_target_pairs={{0,8},{8,0},{16,24},{24,16},{1,9},{9,1},{17,25},{25,17},{2,10},{10... | collective-permute-start | bytes 786440 | tf_op jit(solution)/shard_map/ppermute | solution.py:300
  65.1 10.5 %collective-permute-start.15 = (bf16[2,128,1024]{2,1,0:T(8,128)(2,1)S(1)}, bf16[2,128,1024]{2,1,0:T(8,128)(2,1)S(1)}, u32[]{:S(2)}, u32[]{:S(2)}) collective-permute-start(bf16[2,128,1024]{2,1,0:T(8,128)(2,1)S(1)} %get-tuple-element.62), channel_id=1, source_target_pairs={{0,1},{1,0},{2,3},{3,2},{4,5},{5,4},{6,7},{7,6},{8,9},{9,8},{10,11... | collective-permute-start | bytes 1572872 | tf_op jit(solution)/shard_map/ppermute | solution.py:303
  68.7 8.3 %collective-permute-start.17 = (bf16[128,1024]{1,0:T(8,128)(2,1)S(1)}, bf16[128,1024]{1,0:T(8,128)(2,1)S(1)}, u32[]{:S(2)}, u32[]{:S(2)}) collective-permute-start(bf16[128,1024]{1,0:T(8,128)(2,1)S(1)} %add_convert_fusion.2.refs_0_.first), channel_id=1, source_target_pairs={{0,16},{8,24},{16,0},{24,8},{1,17},{9,25},{17,1},{25,9},{2,18},{10... | collective-permute-start | bytes 786440 | tf_op jit(solution)/shard_map/ppermute | solution.py:300
  70.2 9.2 %collective-permute-start.18 = (bf16[128,1024]{1,0:T(8,128)(2,1)S(1)}, bf16[128,1024]{1,0:T(8,128)(2,1)S(1)}, u32[]{:S(2)}, u32[]{:S(2)}) collective-permute-start(bf16[128,1024]{1,0:T(8,128)(2,1)S(1)} %add_convert_fusion.2.refs_0_.first), channel_id=1, source_target_pairs={{0,8},{8,0},{16,24},{24,16},{1,9},{9,1},{17,25},{25,17},{2,10},{10... | collective-permute-start | bytes 786440 | tf_op jit(solution)/shard_map/ppermute | solution.py:300
  71.0 12.7 %collective-permute-start.19 = (bf16[128,1024]{1,0:T(8,128)(2,1)S(1)}, bf16[128,1024]{1,0:T(8,128)(2,1)S(1)}, u32[]{:S(2)}, u32[]{:S(2)}) collective-permute-start(bf16[128,1024]{1,0:T(8,128)(2,1)S(1)} %add_convert_fusion.2.refs_0_.first), channel_id=1, source_target_pairs={{0,24},{8,16},{16,8},{24,0},{1,25},{9,17},{17,9},{25,1},{2,26},{10... | collective-permute-start | bytes 786440 | tf_op jit(solution)/shard_map/ppermute | solution.py:300
  72.2 14.5 %collective-permute-start.14 = (bf16[128,1024]{1,0:T(8,128)(2,1)S(1)}, bf16[128,1024]{1,0:T(8,128)(2,1)S(1)}, u32[]{:S(2)}, u32[]{:S(2)}) collective-permute-start(bf16[128,1024]{1,0:T(8,128)(2,1)S(1)} %fusion.refs_6_), channel_id=1, source_target_pairs={{0,4},{1,5},{2,6},{3,7},{4,0},{5,1},{6,2},{7,3},{8,12},{9,13},{10,... | collective-permute-start | bytes 786440 | tf_op jit(solution)/shard_map/ppermute | solution.py:303
  75.7 11.1 %collective-permute-start.16 = (bf16[128,1024]{1,0:T(8,128)(2,1)S(1)}, bf16[128,1024]{1,0:T(8,128)(2,1)S(1)}, u32[]{:S(2)}, u32[]{:S(2)}) collective-permute-start(bf16[128,1024]{1,0:T(8,128)(2,1)S(1)} %get-tuple-element.70), channel_id=1, source_target_pairs={{0,2},{1,3},{2,0},{3,1},{4,6},{5,7},{6,4},{7,5},{8,10},{9,11},{10,... | collective-permute-start | bytes 786440 | tf_op jit(solution)/shard_map/ppermute | solution.py:303
  89.7 8.8 %collective-permute-start.20 = (bf16[128,1024]{1,0:T(8,128)(2,1)S(1)}, bf16[128,1024]{1,0:T(8,128)(2,1)S(1)}, u32[]{:S(2)}, u32[]{:S(2)}) collective-permute-start(bf16[128,1024]{1,0:T(8,128)(2,1)S(1)} %get-tuple-element.66), channel_id=1, source_target_pairs={{0,8},{8,0},{16,24},{24,16},{1,9},{9,1},{17,25},{25,17},{2,10},{10... | collective-permute-start | bytes 786440 | tf_op jit(solution)/shard_map/ppermute | solution.py:300
  91.2 11.5 %collective-permute-start.21 = (bf16[128,1024]{1,0:T(8,128)(2,1)S(1)}, bf16[128,1024]{1,0:T(8,128)(2,1)S(1)}, u32[]{:S(2)}, u32[]{:S(2)}) collective-permute-start(bf16[128,1024]{1,0:T(8,128)(2,1)S(1)} %get-tuple-element.67), channel_id=1, source_target_pairs={{0,16},{8,24},{16,0},{24,8},{1,17},{9,25},{17,1},{25,9},{2,18},{10... | collective-permute-start | bytes 786440 | tf_op jit(solution)/shard_map/ppermute | solution.py:300
  91.6 11.2 %collective-permute-start.22 = (bf16[128,1024]{1,0:T(8,128)(2,1)S(1)}, bf16[128,1024]{1,0:T(8,128)(2,1)S(1)}, u32[]{:S(2)}, u32[]{:S(2)}) collective-permute-start(bf16[128,1024]{1,0:T(8,128)(2,1)S(1)} %get-tuple-element.68), channel_id=1, source_target_pairs={{0,24},{8,16},{16,8},{24,0},{1,25},{9,17},{17,9},{25,1},{2,26},{10... | collective-permute-start | bytes 786440 | tf_op jit(solution)/shard_map/ppermute | solution.py:300

commit v3 on v2

--- a/solution.py
+++ b/solution.py
@@ -11,7 +11,7 @@
 F32, BF16 = jnp.float32, jnp.bfloat16
 AHEAD = 3
 PIECES = 4
-LIMIT = 8 << 20
+LIMIT = 6 << 20
 
 
 def contract_last(a, b):
@@ -29,7 +29,7 @@
 
 
 def partial_kernel(cfg, *refs):
-    block, low_row, half, tile, load_p, load_x, group, following, ordered, blocks, extras, chips = cfg
+    block, low_row, half, tile, load_p, load_x, group, following, ordered, blocks, within, extras, chips = cfg
     refs = list(refs)
     place, solved = refs.pop(0)[0], refs.pop(0)
     x = None if load_x else refs.pop(0)
@@ -50,6 +50,7 @@
     piece = depth // PIECES
     per = held[0].shape[0] // tile
     tiles = per * len(held)
+    begin_tile, end_tile = [tiles * edge // within[1] for edge in (within[0], within[0] + 1)]
     count = len(group)
     chip, core = lax.rem(place, 2 * chips) // 2, lax.rem(place, 2)
     used = [0]
@@ -104,7 +105,7 @@
     begin()
 
     def put(d, n):
-        at = pl.ds(n * tile, tile)
+        at = pl.ds((n - begin_tile) * tile, tile)
         for c in range(count):
             send[c, :, at] = d[c * half : (c + 1) * half].astype(send.dtype)
             keep[c, :, at] = d[(count + c) * half : (count + c + 1) * half]
@@ -112,7 +113,7 @@
     def step(n):
         put(contract_last(x[...], held[n // per][pl.ds(n % per * tile, tile), :]), n)
 
-    first = 0
+    first = begin_tile
     if load_x or load_p:
         for j in range(PIECES):
             arrive()
@@ -129,7 +130,7 @@
                     put(d, 0)
 
         first = 1
-    for n in range(first, tiles):
+    for n in range(first, end_tile):
         if load_p:
             arrive()
 
@@ -141,7 +142,7 @@
         arrive()
 
 
-def partial_sums(solved, x, panel, span, orders, place, group, following, half, chips, extras):
+def partial_sums(solved, x, panel, span, orders, place, group, following, half, chips, within, extras):
     load_x, load_p = x is None, not isinstance(panel, list)
     panels = [in_hbm(panel)] if load_p else panel
     depth = solved.shape[1]
@@ -149,6 +150,7 @@
     count = len(group)
     rows = 2 * count * half
     tile = tile_of(width if load_p else panels[0].shape[0], 256)
+    width = width // within[1]
     hbm, vmem = pl.BlockSpec(memory_space=pltpu.HBM), pl.BlockSpec(memory_space=pltpu.VMEM)
     operands = [place, in_hbm(solved)]
     in_specs = [pl.BlockSpec(memory_space=pltpu.SMEM), hbm]
@@ -166,7 +168,7 @@
         jax.ShapeDtypeStruct((count, half, width), F32),
     ]
     if load_p:
-        shapes.append(jax.ShapeDtypeStruct((width, depth), panel.dtype))
+        shapes.append(jax.ShapeDtypeStruct((span[2], depth), panel.dtype))
     if load_x:
         shapes.append(jax.ShapeDtypeStruct((rows, depth), solved.dtype))
     if following:
@@ -175,11 +177,11 @@
         jax.ShapeDtypeStruct((size, array.shape[-1]), array.dtype) for array, _, _, size in extras
     ]
     scratch = [pltpu.VMEM((rows, tile), F32)]
-    copies = PIECES * (2 * count + 1) + width // tile + 2 * len(following) + PIECES * len(extras)
+    copies = PIECES * (2 * count + 1) + panels[0].shape[-2] // tile + 2 * len(following) + PIECES * len(extras)
     scratch.append(pltpu.SemaphoreType.DMA((copies,)))
     cfg = (
         block, low_row, half, tile, load_p, load_x, tuple(group), tuple(following), len(orders),
-        len(panels), tuple((layer, low) for _, layer, low, _ in extras), chips,
+        len(panels), within, tuple((layer, low) for _, layer, low, _ in extras), chips,
     )
     out = pl.pallas_call(
         functools.partial(partial_kernel, cfg),
@@ -237,7 +239,7 @@
 
 
 def carry_kernel(members, offsets, cols, place, *refs):
-    firsts, link, out = refs[:-2], refs[-2], refs[-1]
+    firsts, link, out = refs[:-3], refs[-3], refs[-1]
     at = blocks_of(place[0] // cols, members, out.shape[1])
     out[...] = carry(firsts, link, at, offsets)
 
@@ -252,26 +254,32 @@
     carried = early[...]
     if offsets:
         carried += carry(firsts, link, at, offsets)
-    res = (residual(1, rhs, parts, counts) - carried).astype(BF16)
-    for offset in range(members - 1, -1, -1):
-        d = jnp.dot(res, inverse[:, at[offset]], preferred_element_type=F32)
+    out, res = outs
+    value = (residual(1, rhs, parts, counts) - carried).astype(BF16)
+    res[...] = value
+    d = jnp.dot(value, inverse[:, at[members - 1]], preferred_element_type=F32)
+    out[...] = d.astype(out.dtype)
+
+
+def second_rest_kernel(members, cols, place, res, inverse, *outs):
+    at = blocks_of(place[0] // cols, members, res.shape[1])
+    for offset in range(members - 2, -1, -1):
+        d = jnp.dot(res[...], inverse[:, at[offset]], preferred_element_type=F32)
         outs[offset][...] = d.astype(outs[offset].dtype)
 
 
-def solve(kernel, flops, place, rhs, parts, rest, members):
-    half, _, width = rhs.shape
+def solve(kernel, flops, place, operands, shape, types):
     vmem = pl.BlockSpec(memory_space=pltpu.VMEM)
-    shapes = [
-        jax.ShapeDtypeStruct((half, width), BF16 if offset else F32) for offset in range(members)
-    ]
     return pl.pallas_call(
         kernel,
-        in_specs=[pl.BlockSpec(memory_space=pltpu.SMEM)] + [vmem] * (1 + len(parts) + len(rest)),
-        out_specs=[vmem] * members,
-        out_shape=shapes,
+        in_specs=[pl.BlockSpec(memory_space=pltpu.SMEM)] + [vmem] * len(operands),
+        out_specs=[vmem] * len(types),
+        out_shape=[jax.ShapeDtypeStruct(shape, kind) for kind in types],
         compiler_params=pltpu.CompilerParams(vmem_limit_bytes=LIMIT),
-        cost_estimate=pl.CostEstimate(flops=flops, bytes_accessed=flops // half, transcendentals=0),
-    )(place, rhs, *parts, *rest)
+        cost_estimate=pl.CostEstimate(
+            flops=flops, bytes_accessed=flops // shape[0], transcendentals=0
+        ),
+    )(place, *operands)
 
 
 def result_kernel(first, *refs):
@@ -284,11 +292,15 @@
 
 
 def plan_of(chips):
-    far = list(range(chips - 1, max(chips - 3, -1), -1))
-    plan = [(0, far, 0), (0, far, 1)]
-    plan += [(0, [o], None) for o in range(far[-1] - 1, -1, -1)]
-    pairs = [[o + 1, o] if chips > 1 else [o] for o in range(max(chips - 2, 0), -1, -2)]
-    return plan + [(1, pair, None) for pair in pairs]
+    plan = [(0, [o], (0, 1)) for o in range(chips - 1, 0, -1)]
+    plan += [(0, [0], (0, 2)), (0, [0], (1, 2))] if plan else [(0, [0], (0, 1))]
+    plan += [(1, [o + 1, o], (0, 1)) for o in range(chips - 2, 0, -2)]
+    return plan + [(1, [o], (0, 1)) for o in ([1, 0] if chips > 1 else [0])]
+
+
+def deadline(plan, n, offset):
+    odd, last = offset % 2, len(plan) - 1
+    return min(last, n + (1 if plan[n][0] else 2 if odd else 3))
 
 
 def local(members, chips, rhs, solved, panel, inverse, link):
@@ -307,11 +319,11 @@
 
     extras = [[] for _ in plan]
     ahead = [n for n, (b, _, _) in enumerate(plan) if b == 0]
-    extras[min(len(ahead), last - 1)].append(("inverse", inverse, 0, 0, width))
+    extras[len(ahead) if last > len(ahead) + 1 else 0].append(("inverse", inverse, 0, 0, width))
     piece = width // 2
-    extras[ahead[-2]].append(("low", panel, 1, 0, piece))
-    extras[ahead[-1]].append(("high", panel, 1, piece, piece))
-    extras[last].append(("link", link, None, 0, width))
+    extras[max(0, ahead[-1] - 3)].append(("low", panel, 1, 0, piece))
+    extras[max(0, ahead[-1] - 2)].append(("high", panel, 1, piece, piece))
+    extras[last - 1].append(("link", link, None, 0, width))
     extras[last].append(("second", inverse, 1, 0, width))
 
     flops = 2 * half * width * width * members
@@ -335,16 +347,22 @@
         follows = n < last and plan[n + 1][1] != group
         following = plan[n + 1][1] if follows else []
         orders = due[n]
-        if n == last:
+        if n == last - 1:
             parts = solve(
                 functools.partial(solve_first_kernel, counts(0), cols),
-                flops, place, rhs, flat(0), [kept["inverse"]], members,
+                flops, place, [rhs, *flat(0), kept["inverse"]],
+                (half, width), [F32] + [BF16] * (members - 1),
             )
             orders = due[n] + [parts[members > 1]]
-        span = None if part is None else (b, part * piece, piece)
+        if n == last:
+            total = parts[0]
+            for offset in range(1, members):
+                total += across_row(parts[offset], offset).astype(F32)
+            first = total.astype(BF16)
+            orders = due[n] + [first]
         send, keep, held, x, got = partial_sums(
-            solved, x, blocks if part is None else panel, span, orders, place,
-            group, following, half, chips, [e[1:] for e in extras[n]],
+            solved, x, blocks if n else panel, (0, 0, width), orders, place,
+            group, following, half, chips, part, [e[1:] for e in extras[n]],
         )
         blocks = blocks + held
         kept.update(zip([e[0] for e in extras[n]], got))
@@ -356,26 +374,23 @@
                 continue
             value = keep[at] + other[at].astype(F32)
             if offset % 2 == 0:
-                value += passing.pop((b, offset, part)).astype(F32)
+                value += passing.pop((b, offset)).astype(F32)
             value = value.astype(BF16)
-            due[min(last, n + (2 if offset % 2 else 3))].append(value)
+            due[deadline(plan, n, offset)].append(value)
             arrived = across_col(value, 2 if offset % 2 else 2 * offset)
             if offset > 1 and offset % 2:
-                passing[b, offset - 1, part] = arrived
+                passing[b, offset - 1] = arrived
             else:
                 term(b, offset, arrived)
 
-    total = parts[0]
-    for offset in range(1, members):
-        total += across_row(parts[offset], offset).astype(F32)
-    first = total.astype(BF16)
     firsts = [first] + [across_row(first, o) for o in range(1, members)]
     early = sorted({0, members // 2 if members > 2 else 0})
     late = [o for o in range(members) if o not in early]
     vmem = pl.BlockSpec(memory_space=pltpu.VMEM)
     carried = pl.pallas_call(
         functools.partial(carry_kernel, members, early, cols),
-        in_specs=[pl.BlockSpec(memory_space=pltpu.SMEM)] + [vmem] * (1 + len(early)),
+        in_specs=[pl.BlockSpec(memory_space=pltpu.SMEM)] + [vmem] * (1 + len(early))
+        + [pl.BlockSpec(memory_space=pl.ANY)],
         out_specs=vmem,
         out_shape=jax.ShapeDtypeStruct((half, width), F32),
         name="carry",
@@ -383,12 +398,19 @@
         cost_estimate=pl.CostEstimate(
             flops=2 * half * width * width, bytes_accessed=width * width, transcendentals=0
         ),
-    )(place, *[firsts[o] for o in early], kept["link"])
+    )(place, *[firsts[o] for o in early], kept["link"], keep)
+    shape = (half, width)
+    edge, res = solve(
+        functools.partial(solve_second_kernel, counts(1), members, late, cols),
+        flops, place,
+        [rhs, *flat(1), carried, *[firsts[o] for o in late], kept["link"], kept["second"]],
+        shape, [BF16, BF16],
+    )
     parts = solve(
-        functools.partial(solve_second_kernel, counts(1), members, late, cols),
-        2 * flops, place, rhs, flat(1),
-        [carried] + [firsts[o] for o in late] + [kept["link"], kept["second"]], members,
+        functools.partial(second_rest_kernel, members, cols),
+        flops, place, [res, kept["second"]], shape, [F32] + [BF16] * (members - 2),
     )
+    parts = list(parts) + [edge]
     arrived = [across_row(parts[offset], offset) for offset in range(1, members)]
     return pl.pallas_call(
         result_kernel,

time: 104 us -> 109 us (1.048)
  waiting for transfers between devices: 34.7 us -> 39.8 us
  starting transfers between devices: 25.8 us -> 23.7 us
  Pallas kernels: 42.7 us -> 44.5 us
    ppermute x14, waiting for transfers between devices: 16.3 us -> 20.4 us  [across_col(): return lax.ppermute(value, 'col', [(i, i ^ offset) for i in range(cols)])]
    ppermute x14, starting transfers between devices: 15.1 us -> 13 us  [across_col(): return lax.ppermute(value, 'col', [(i, i ^ offset) for i in range(cols)])]
    pallas_call x6 -> x8, Pallas kernels: 35.6 us -> 37.2 us  [partial_sums(): pl.pallas_call(functools.partial(partial_kernel, cfg), in_specs=in_specs,...]
    pallas_call x2 -> x3, Pallas kernels: 4.36 us -> 4.56 us  [solve(): pl.pallas_call(kernel, in_specs=[pl.BlockSpec(memory_space=pltpu.SMEM)] +...]
  transfers between devices with their start and end apart: 23 -> 23, of which waited for: 11 -> 12; matrix products, arithmetic and copies ran while one was open for 1% -> 0% of each run, Pallas kernels for 24% -> 16%
where the time goes in v3:
time: 109 us
  Pallas kernels  44.5 us (41%)
  waiting for transfers between devices  39.8 us (37%)
  starting transfers between devices  23.7 us (22%)
    pallas_call x8, Pallas kernels, partial_sums(): pl.pallas_call(functools.partial(partial_kernel, cfg), in_specs=in_specs,...  37.2 us
    ppermute x14, waiting for transfers between devices, across_col(): return lax.ppermute(value, 'col', [(i, i ^ offset) for i in range(cols)])  20.4 us
    ppermute x9, waiting for transfers between devices, across_row(): return lax.ppermute(value, 'row', [(i, i ^ offset) for i in range(members)])  19.3 us
    ppermute x14, starting transfers between devices, across_col(): return lax.ppermute(value, 'col', [(i, i ^ offset) for i in range(cols)])  13 us
    ppermute x9, starting transfers between devices, across_row(): return lax.ppermute(value, 'row', [(i, i ^ offset) for i in range(members)])  10.7 us
    pallas_call x3, Pallas kernels, solve(): pl.pallas_call(kernel, in_specs=[pl.BlockSpec(memory_space=pltpu.SMEM)] +...  4.56 us
  transfers between devices with their start and end apart: 23, of which 12 were waited for; matrix products, arithmetic and copies ran while one was open for 0% of the time, Pallas kernels for 16%

profile of v3, /device:TPU:0, one launch (start us, length us, event | category | flops | bytes accessed | tf_op | source)
XLA Modules:
  0.0 108.7 jit_solution(7440465954383844665)
XLA Ops:
  0.0 8.8 %shard_map.55 = (bf16[1,128,1024]{2,1,0:T(8,128)(2,1)S(1)}, f32[1,128,1024]{2,1,0:T(8,128)S(1)}, bf16[1024,6144]{1,0:T(8,128)(2,1)S(1)}, bf16[256,6144]{1,0:T(8,128)(2,1)}, bf16[256,6144]{1,0:T(8,128)(2,1)S(1)}) custom-call(s32[1]{0:T(128)} %bitcast.refs_0_.place, bf16[1024,6144]{1,0:T(8,128)(2,1)} %refs_1_.15, bf16[2,1024,6144]{2,1,0:T(8,128)(2,1)} %refs_5_.2), custom_call_target="tpu_custom_call" | custom-call | flops 3221225472 | bytes 15728640 | tf_op jit(solution)/shard_map/pallas_call | solution.py:186
  9.4 3.9 %shard_map.56 = (bf16[1,128,1024]{2,1,0:T(8,128)(2,1)S(1)}, f32[1,128,1024]{2,1,0:T(8,128)S(1)}, bf16[256,6144]{1,0:T(8,128)(2,1)S(1)}, bf16[512,6144]{1,0:T(8,128)(2,1)S(1)}) custom-call(s32[1]{0:T(128)} %bitcast.refs_0_.place, bf16[1024,6144]{1,0:T(8,128)(2,1)} %refs_1_.15, bf16[256,6144]{1,0:T(8,128)(2,1)S(1)} %get-tuple-element.42.refs_2_, ...), custom_call_target="tpu_custom_call" | custom-call | flops 3221225472 | bytes 15728640 | tf_op jit(solution)/shard_map/pallas_call | solution.py:186
  13.4 3.9 %shard_map.57 = (bf16[1,128,1024]{2,1,0:T(8,128)(2,1)S(1)}, f32[1,128,1024]{2,1,0:T(8,128)S(1)}, bf16[256,6144]{1,0:T(8,128)(2,1)S(1)}, bf16[512,6144]{1,0:T(8,128)(2,1)S(1)}) custom-call(s32[1]{0:T(128)} %bitcast.refs_0_.place, bf16[1024,6144]{1,0:T(8,128)(2,1)} %refs_1_.15, bf16[256,6144]{1,0:T(8,128)(2,1)S(1)} %get-tuple-element.48.refs_2_, ...), custom_call_target="tpu_custom_call" | custom-call | flops 3221225472 | bytes 15728640 | tf_op jit(solution)/shard_map/pallas_call | solution.py:186
  17.9 2.6 %collective-permute-start.2 = (bf16[128,1024]{1,0:T(8,128)(2,1)S(1)}, bf16[128,1024]{1,0:T(8,128)(2,1)S(1)}, u32[]{:S(2)}, u32[]{:S(2)}) collective-permute-start(bf16[128,1024]{1,0:T(8,128)(2,1)S(1)} %fusion.2.refs_4_), channel_id=1, source_target_pairs={{0,2},{1,3},{2,0},{3,1},{4,6},{5,7},{6,4},{7,5},{8,10},{9,11},{10,... | collective-permute-start | bytes 786440 | tf_op jit(solution)/shard_map/ppermute | solution.py:315
  20.6 6.8 %collective-permute-done.2 = bf16[128,1024]{1,0:T(8,128)(2,1)S(1)} collective-permute-done((bf16[128,1024]{1,0:T(8,128)(2,1)S(1)}, bf16[128,1024]{1,0:T(8,128)(2,1)S(1)}, u32[]{:S(2)}, u32[]{:S(2)}) %collective-permute-start.2) | collective-permute-done | bytes 262176 | tf_op jit(solution)/shard_map/ppermute | solution.py:315
  27.6 3.0 %shard_map.59 = (bf16[1,128,512]{2,1,0:T(8,128)(2,1)S(1)}, f32[1,128,512]{2,1,0:T(8,128)S(1)}, bf16[512,6144]{1,0:T(8,128)(2,1)S(1)}) custom-call(s32[1]{0:T(128)} %bitcast.refs_0_.place, bf16[1024,6144]{1,0:T(8,128)(2,1)} %refs_1_.15, bf16[256,6144]{1,0:T(8,128)(2,1)S(1)} %get-tuple-element.51.refs_2_, bf16[1024,6144]{1,0:T(8,128)(2,1)S(1)} %get-tuple-element.43.refs_3_, ...), custom_call_target="tpu_custom_call" | custom-call | flops 1610612736 | bytes 9437184 | tf_op jit(solution)/shard_map/pallas_call | solution.py:186
  30.6 7.1 %shard_map.60 = (bf16[2,128,1024]{2,1,0:T(8,128)(2,1)S(1)}, f32[2,128,1024]{2,1,0:T(8,128)S(1)}, bf16[256,6144]{1,0:T(8,128)(2,1)S(1)}, bf16[1024,4096]{1,0:T(8,128)(2,1)S(1)}) custom-call(s32[1]{0:T(128)} %bitcast.refs_0_.place, bf16[1024,6144]{1,0:T(8,128)(2,1)} %refs_1_.15, bf16[512,6144]{1,0:T(8,128)(2,1)S(1)} %get-tuple-element.56.refs_2_, ...), custom_call_target="tpu_custom_call" | custom-call | flops 6442450944 | bytes 18874368 | tf_op jit(solution)/shard_map/pallas_call | solution.py:186
  37.8 2.8 %collective-permute-start.3 = (bf16[128,1024]{1,0:T(8,128)(2,1)S(1)}, bf16[128,1024]{1,0:T(8,128)(2,1)S(1)}, u32[]{:S(2)}, u32[]{:S(2)}) collective-permute-start(bf16[128,1024]{1,0:T(8,128)(2,1)S(1)} %fusion.1.refs_4_), channel_id=1, source_target_pairs={{0,4},{1,5},{2,6},{3,7},{4,0},{5,1},{6,2},{7,3},{8,12},{9,13},{10,... | collective-permute-start | bytes 786440 | tf_op jit(solution)/shard_map/ppermute | solution.py:315
  40.6 1.6 %collective-permute-start.5 = (bf16[128,1024]{1,0:T(8,128)(2,1)S(1)}, bf16[128,1024]{1,0:T(8,128)(2,1)S(1)}, u32[]{:S(2)}, u32[]{:S(2)}) collective-permute-start(bf16[128,1024]{1,0:T(8,128)(2,1)S(1)} %fusion.3.refs_5_), channel_id=1, source_target_pairs={{0,2},{1,3},{2,0},{3,1},{4,6},{5,7},{6,4},{7,5},{8,10},{9,11},{10,... | collective-permute-start | bytes 786440 | tf_op jit(solution)/shard_map/ppermute | solution.py:315
  42.8 2.0 %shard_map.58 = (bf16[1,128,512]{2,1,0:T(8,128)(2,1)S(1)}, f32[1,128,512]{2,1,0:T(8,128)S(1)}) custom-call(s32[1]{0:T(128)} %bitcast.refs_0_.place, bf16[1024,6144]{1,0:T(8,128)(2,1)} %refs_1_.15, bf16[256,6144]{1,0:T(8,128)(2,1)S(1)} %get-tuple-element.51.refs_2_, bf16[1024,6144]{1,0:T(8,128)(2,1)S(1)} %get-tuple-element.43.refs_3_), custom_call_target="tpu_custom_call" | custom-call | flops 1610612736 | bytes 9437184 | tf_op jit(solution)/shard_map/pallas_call | solution.py:186
  46.4 6.9 %collective-permute-done.3.refs_0_ = bf16[128,1024]{1,0:T(8,128)(2,1)S(1)} collective-permute-done((bf16[128,1024]{1,0:T(8,128)(2,1)S(1)}, bf16[128,1024]{1,0:T(8,128)(2,1)S(1)}, u32[]{:S(2)}, u32[]{:S(2)}) %collective-permute-start.3) | collective-permute-done | bytes 262176 | tf_op jit(solution)/shard_map/ppermute | solution.py:315
  53.2 1.0 collective-permute-done.5.refs_1_
  54.3 1.5 %shard_map.61 = (f32[128,1024]{1,0:T(8,128)S(1)}, bf16[128,1024]{1,0:T(8,128)(2,1)S(1)}, bf16[128,1024]{1,0:T(8,128)(2,1)S(1)}, bf16[128,1024]{1,0:T(8,128)(2,1)S(1)}) custom-call(s32[1]{0:T(128)} %bitcast.refs_0_.place, bf16[128,2,1024]{2,1,0:T(2,128)(2,1)S(1)} %copy-done, bf16[128,1024]{1,0:T(8,128)(2,1)S(1)} %collective-permute-done.3.refs_0_, ...), custom_call_target="tpu_custom_call" | custom-call | flops 1073741824 | bytes 8388608 | tf_op jit(solution)/shard_map/pallas_call | solution.py:273
  55.8 1.6 %collective-permute-start.9 = (bf16[128,1024]{1,0:T(8,128)(2,1)S(1)}, bf16[128,1024]{1,0:T(8,128)(2,1)S(1)}, u32[]{:S(2)}, u32[]{:S(2)}) collective-permute-start(bf16[128,1024]{1,0:T(8,128)(2,1)S(1)} %get-tuple-element.62), channel_id=1, source_target_pairs={{0,16},{8,24},{16,0},{24,8},{1,17},{9,25},{17,1},{25,9},{2,18},{10... | collective-permute-start | bytes 786440 | tf_op jit(solution)/shard_map/ppermute | solution.py:312
  57.4 1.4 %collective-permute-start.10 = (bf16[128,1024]{1,0:T(8,128)(2,1)S(1)}, bf16[128,1024]{1,0:T(8,128)(2,1)S(1)}, u32[]{:S(2)}, u32[]{:S(2)}) collective-permute-start(bf16[128,1024]{1,0:T(8,128)(2,1)S(1)} %get-tuple-element.63), channel_id=1, source_target_pairs={{0,24},{8,16},{16,8},{24,0},{1,25},{9,17},{17,9},{25,1},{2,26},{10... | collective-permute-start | bytes 786440 | tf_op jit(solution)/shard_map/ppermute | solution.py:312
  59.4 4.6 %shard_map.62 = (bf16[1,128,1024]{2,1,0:T(8,128)(2,1)S(1)}, f32[1,128,1024]{2,1,0:T(8,128)S(1)}, bf16[256,6144]{1,0:T(8,128)(2,1)S(1)}, bf16[1024,4096]{1,0:T(8,128)(2,1)S(1)}) custom-call(s32[1]{0:T(128)} %bitcast.refs_0_.place, bf16[1024,6144]{1,0:T(8,128)(2,1)} %refs_1_.15, bf16[256,6144]{1,0:T(8,128)(2,1)S(1)} %get-tuple-element.66.refs_2_, ...), custom_call_target="tpu_custom_call" | custom-call | flops 3221225472 | bytes 15728640 | tf_op jit(solution)/shard_map/pallas_call | solution.py:186
  64.1 4.2 %collective-permute-done.9 = bf16[128,1024]{1,0:T(8,128)(2,1)S(1)} collective-permute-done((bf16[128,1024]{1,0:T(8,128)(2,1)S(1)}, bf16[128,1024]{1,0:T(8,128)(2,1)S(1)}, u32[]{:S(2)}, u32[]{:S(2)}) %collective-permute-start.9) | collective-permute-done | bytes 262176 | tf_op jit(solution)/shard_map/ppermute | solution.py:312
  68.3 1.2 %collective-permute-done.8 = bf16[128,1024]{1,0:T(8,128)(2,1)S(1)} collective-permute-done((bf16[128,1024]{1,0:T(8,128)(2,1)S(1)}, bf16[128,1024]{1,0:T(8,128)(2,1)S(1)}, u32[]{:S(2)}, u32[]{:S(2)}) %collective-permute-start.8) | collective-permute-done | bytes 262176 | tf_op jit(solution)/shard_map/ppermute | solution.py:312
  69.7 2.5 %collective-permute-start.19 = (bf16[128,1024]{1,0:T(8,128)(2,1)S(1)}, bf16[128,1024]{1,0:T(8,128)(2,1)S(1)}, u32[]{:S(2)}, u32[]{:S(2)}) collective-permute-start(bf16[128,1024]{1,0:T(8,128)(2,1)S(1)} %add_convert_fusion.2.refs_6_.refs_0_.first), channel_id=1, source_target_pairs={{0,24},{8,16},{16,8},{24,0},{1,25},{9,17},{17,9},{25,1},{2,26},{10... | collective-permute-start | bytes 786440 | tf_op jit(solution)/shard_map/ppermute | solution.py:312
  73.2 1.5 %collective-permute-start.13 = (bf16[128,1024]{1,0:T(8,128)(2,1)S(1)}, bf16[128,1024]{1,0:T(8,128)(2,1)S(1)}, u32[]{:S(2)}, u32[]{:S(2)}) collective-permute-start(bf16[128,1024]{1,0:T(8,128)(2,1)S(1)} %fusion.refs_6_), channel_id=1, source_target_pairs={{0,4},{1,5},{2,6},{3,7},{4,0},{5,1},{6,2},{7,3},{8,12},{9,13},{10,... | collective-permute-start | bytes 786440 | tf_op jit(solution)/shard_map/ppermute | solution.py:315
  74.8 3.8 %shard_map.63 = (bf16[1,128,1024]{2,1,0:T(8,128)(2,1)S(1)}, f32[1,128,1024]{2,1,0:T(8,128)S(1)}, bf16[1024,4096]{1,0:T(8,128)(2,1)S(1)}) custom-call(s32[1]{0:T(128)} %bitcast.refs_0_.place, bf16[1024,6144]{1,0:T(8,128)(2,1)} %refs_1_.15, bf16[256,6144]{1,0:T(8,128)(2,1)S(1)} %get-tuple-element.69.refs_2_, bf16[512,6144]{1,0:T(8,128)(2,1)S(1)} %get-tuple-element.57.refs_3_, ...), custom_call_target="tpu_custom_call" | custom-call | flops 3221225472 | bytes 15728640 | tf_op jit(solution)/shard_map/pallas_call | solution.py:186
  78.7 3.3 %collective-permute-done.17.refs_1_ = bf16[128,1024]{1,0:T(8,128)(2,1)S(1)} collective-permute-done((bf16[128,1024]{1,0:T(8,128)(2,1)S(1)}, bf16[128,1024]{1,0:T(8,128)(2,1)S(1)}, u32[]{:S(2)}, u32[]{:S(2)}) %collective-permute-start.17) | collective-permute-done | bytes 262176 | tf_op jit(solution)/shard_map/ppermute | solution.py:312
  82.0 2.0 %collective-permute-start.15 = (bf16[128,1024]{1,0:T(8,128)(2,1)S(1)}, bf16[128,1024]{1,0:T(8,128)(2,1)S(1)}, u32[]{:S(2)}, u32[]{:S(2)}) collective-permute-start(bf16[128,1024]{1,0:T(8,128)(2,1)S(1)} %fusion.5.refs_5_), channel_id=1, source_target_pairs={{0,2},{1,3},{2,0},{3,1},{4,6},{5,7},{6,4},{7,5},{8,10},{9,11},{10,... | collective-permute-start | bytes 786440 | tf_op jit(solution)/shard_map/ppermute | solution.py:315
  84.0 1.5 %carry.1.refs_4_ = f32[128,1024]{1,0:T(8,128)S(1)} custom-call(s32[1]{0:T(128)} %bitcast.refs_0_.place, bf16[128,1024]{1,0:T(8,128)(2,1)S(1)} %add_convert_fusion.2.refs_6_.refs_0_.first, bf16[128,1024]{1,0:T(8,128)(2,1)S(1)} %collective-permute-done.17.refs_1_, bf16[1024,4096]{1,0:T(8,128)(2,1)S(1)} %get-tuple-element.72.refs_2_.refs_7_, ...), custom_call_target="tpu_custom_call" | custom-call | flops 268435456 | bytes 1048576 | tf_op jit(solution)/shard_map/carry/pallas_call | solution.py:390
  85.6 4.7 %collective-permute-done.15.refs_1_ = bf16[128,1024]{1,0:T(8,128)(2,1)S(1)} collective-permute-done((bf16[128,1024]{1,0:T(8,128)(2,1)S(1)}, bf16[128,1024]{1,0:T(8,128)(2,1)S(1)}, u32[]{:S(2)}, u32[]{:S(2)}) %collective-permute-start.15) | collective-permute-done | bytes 262176 | tf_op jit(solution)/shard_map/ppermute | solution.py:315
  90.3 2.1 %shard_map.64 = (bf16[128,1024]{1,0:T(8,128)(2,1)S(1)}, bf16[128,1024]{1,0:T(8,128)(2,1)S(1)}) custom-call(s32[1]{0:T(128)} %bitcast.refs_0_.place, bf16[128,2,1024]{2,1,0:T(2,128)(2,1)S(1)} %copy-done, bf16[128,1024]{1,0:T(8,128)(2,1)S(1)} %collective-permute-done.13.refs_0_, bf16[128,1024]{1,0:T(8,128)(2,1)S(1)} %collective-permute-done.15.refs_1_, ...), custom_call_target="tpu_custom_call" | custom-call | flops 1073741824 | bytes 8388608 | tf_op jit(solution)/shard_map/pallas_call | solution.py:273
  92.3 1.0 shard_map.65
  93.3 1.4 %collective-permute-start.20 = (bf16[128,1024]{1,0:T(8,128)(2,1)S(1)}, bf16[128,1024]{1,0:T(8,128)(2,1)S(1)}, u32[]{:S(2)}, u32[]{:S(2)}) collective-permute-start(bf16[128,1024]{1,0:T(8,128)(2,1)S(1)} %get-tuple-element.76), channel_id=1, source_target_pairs={{0,8},{8,0},{16,24},{24,16},{1,9},{9,1},{17,25},{25,17},{2,10},{10... | collective-permute-start | bytes 786440 | tf_op jit(solution)/shard_map/ppermute | solution.py:312
  94.7 1.7 %collective-permute-start.21 = (bf16[128,1024]{1,0:T(8,128)(2,1)S(1)}, bf16[128,1024]{1,0:T(8,128)(2,1)S(1)}, u32[]{:S(2)}, u32[]{:S(2)}) collective-permute-start(bf16[128,1024]{1,0:T(8,128)(2,1)S(1)} %get-tuple-element.77), channel_id=1, source_target_pairs={{0,16},{8,24},{16,0},{24,8},{1,17},{9,25},{17,1},{25,9},{2,18},{10... | collective-permute-start | bytes 786440 | tf_op jit(solution)/shard_map/ppermute | solution.py:312
  96.9 5.7 %collective-permute-done.20.refs_1_ = bf16[128,1024]{1,0:T(8,128)(2,1)S(1)} collective-permute-done((bf16[128,1024]{1,0:T(8,128)(2,1)S(1)}, bf16[128,1024]{1,0:T(8,128)(2,1)S(1)}, u32[]{:S(2)}, u32[]{:S(2)}) %collective-permute-start.20) | collective-permute-done | bytes 262176 | tf_op jit(solution)/shard_map/ppermute | solution.py:312
  102.6 4.2 %collective-permute-done.21.refs_2_ = bf16[128,1024]{1,0:T(8,128)(2,1)S(1)} collective-permute-done((bf16[128,1024]{1,0:T(8,128)(2,1)S(1)}, bf16[128,1024]{1,0:T(8,128)(2,1)S(1)}, u32[]{:S(2)}, u32[]{:S(2)}) %collective-permute-start.21) | collective-permute-done | bytes 262176 | tf_op jit(solution)/shard_map/ppermute | solution.py:312
  107.5 1.2 %result.1 = bf16[128,2,1024]{2,1,0:T(2,128)(2,1)} custom-call(bf16[128,1024]{1,0:T(8,128)(2,1)S(1)} %add_convert_fusion.2.refs_6_.refs_0_.first, f32[128,1024]{1,0:T(8,128)S(1)} %get-tuple-element.75.refs_0_, bf16[128,1024]{1,0:T(8,128)(2,1)S(1)} %collective-permute-done.20.refs_1_, bf16[128,1024]{1,0:T(8,128)(2,1)S(1)} %collective-permute-done.21.refs_2_, ...), custom_call_target="tpu_custom_call" | custom-call | tf_op jit(solution)/shard_map/result/pallas_call | solution.py:415
  (36 shorter events, 6.8 us)
Async XLA Ops:
  8.8 4.5 %collective-permute-start.1 = (bf16[1,128,1024]{2,1,0:T(8,128)(2,1)S(1)}, bf16[1,128,1024]{2,1,0:T(8,128)(2,1)S(1)}, u32[]{:S(2)}, u32[]{:S(2)}) collective-permute-start(bf16[1,128,1024]{2,1,0:T(8,128)(2,1)S(1)} %get-tuple-element.47), channel_id=1, source_target_pairs={{0,1},{1,0},{2,3},{3,2},{4,5},{5,4},{6,7},{7,6},{8,9},{9,8},{10,11... | collective-permute-start | bytes 786440 | tf_op jit(solution)/shard_map/ppermute | solution.py:315
  17.3 3.2 %collective-permute-start.4 = (bf16[1,128,1024]{2,1,0:T(8,128)(2,1)S(1)}, bf16[1,128,1024]{2,1,0:T(8,128)(2,1)S(1)}, u32[]{:S(2)}, u32[]{:S(2)}) collective-permute-start(bf16[1,128,1024]{2,1,0:T(8,128)(2,1)S(1)} %get-tuple-element.50), channel_id=1, source_target_pairs={{0,1},{1,0},{2,3},{3,2},{4,5},{5,4},{6,7},{7,6},{8,9},{9,8},{10,11... | collective-permute-start | bytes 786440 | tf_op jit(solution)/shard_map/ppermute | solution.py:315
  17.4 3.2 %collective-permute-start = (bf16[1,128,1024]{2,1,0:T(8,128)(2,1)S(1)}, bf16[1,128,1024]{2,1,0:T(8,128)(2,1)S(1)}, u32[]{:S(2)}, u32[]{:S(2)}) collective-permute-start(bf16[1,128,1024]{2,1,0:T(8,128)(2,1)S(1)} %get-tuple-element.45), channel_id=1, source_target_pairs={{0,1},{1,0},{2,3},{3,2},{4,5},{5,4},{6,7},{7,6},{8,9},{9,8},{10,11... | collective-permute-start | bytes 786440 | tf_op jit(solution)/shard_map/ppermute | solution.py:315
  17.9 9.5 %collective-permute-start.2 = (bf16[128,1024]{1,0:T(8,128)(2,1)S(1)}, bf16[128,1024]{1,0:T(8,128)(2,1)S(1)}, u32[]{:S(2)}, u32[]{:S(2)}) collective-permute-start(bf16[128,1024]{1,0:T(8,128)(2,1)S(1)} %fusion.2.refs_4_), channel_id=1, source_target_pairs={{0,2},{1,3},{2,0},{3,1},{4,6},{5,7},{6,4},{7,5},{8,10},{9,11},{10,... | collective-permute-start | bytes 786440 | tf_op jit(solution)/shard_map/ppermute | solution.py:315
  37.7 4.5 %collective-permute-start.11 = (bf16[2,128,1024]{2,1,0:T(8,128)(2,1)S(1)}, bf16[2,128,1024]{2,1,0:T(8,128)(2,1)S(1)}, u32[]{:S(2)}, u32[]{:S(2)}) collective-permute-start(bf16[2,128,1024]{2,1,0:T(8,128)(2,1)S(1)} %get-tuple-element.65), channel_id=1, source_target_pairs={{0,1},{1,0},{2,3},{3,2},{4,5},{5,4},{6,7},{7,6},{8,9},{9,8},{10,11... | collective-permute-start | bytes 1572872 | tf_op jit(solution)/shard_map/ppermute | solution.py:315
  37.8 15.4 %collective-permute-start.3 = (bf16[128,1024]{1,0:T(8,128)(2,1)S(1)}, bf16[128,1024]{1,0:T(8,128)(2,1)S(1)}, u32[]{:S(2)}, u32[]{:S(2)}) collective-permute-start(bf16[128,1024]{1,0:T(8,128)(2,1)S(1)} %fusion.1.refs_4_), channel_id=1, source_target_pairs={{0,4},{1,5},{2,6},{3,7},{4,0},{5,1},{6,2},{7,3},{8,12},{9,13},{10,... | collective-permute-start | bytes 786440 | tf_op jit(solution)/shard_map/ppermute | solution.py:315
  40.6 13.6 %collective-permute-start.5 = (bf16[128,1024]{1,0:T(8,128)(2,1)S(1)}, bf16[128,1024]{1,0:T(8,128)(2,1)S(1)}, u32[]{:S(2)}, u32[]{:S(2)}) collective-permute-start(bf16[128,1024]{1,0:T(8,128)(2,1)S(1)} %fusion.3.refs_5_), channel_id=1, source_target_pairs={{0,2},{1,3},{2,0},{3,1},{4,6},{5,7},{6,4},{7,5},{8,10},{9,11},{10,... | collective-permute-start | bytes 786440 | tf_op jit(solution)/shard_map/ppermute | solution.py:315
  42.3 12.0 %copy-start = (bf16[128,2,1024]{2,1,0:T(2,128)(2,1)S(1)}, bf16[128,2,1024]{2,1,0:T(2,128)(2,1)}, u32[]{:S(2)}) copy-start(bf16[128,2,1024]{2,1,0:T(2,128)(2,1)} %rhs.3) | copy-start | bytes 1572868
  42.3 17.0 %collective-permute-start.12 = (bf16[128,1024]{1,0:T(8,128)(2,1)S(1)}, bf16[128,1024]{1,0:T(8,128)(2,1)S(1)}, u32[]{:S(2)}, u32[]{:S(2)}) collective-permute-start(bf16[128,1024]{1,0:T(8,128)(2,1)S(1)} %fusion.4.refs_5_), channel_id=1, source_target_pairs={{0,2},{1,3},{2,0},{3,1},{4,6},{5,7},{6,4},{7,5},{8,10},{9,11},{10,... | collective-permute-start | bytes 786440 | tf_op jit(solution)/shard_map/ppermute | solution.py:315
  44.8 1.4 %collective-permute-start.6 = (bf16[1,128,512]{2,1,0:T(8,128)(2,1)S(1)}, bf16[1,128,512]{2,1,0:T(8,128)(2,1)S(1)}, u32[]{:S(2)}, u32[]{:S(2)}) collective-permute-start(bf16[1,128,512]{2,1,0:T(8,128)(2,1)S(1)} %get-tuple-element.54), channel_id=1, source_target_pairs={{0,1},{1,0},{2,3},{3,2},{4,5},{5,4},{6,7},{7,6},{8,9},{9,8},{10,11... | collective-permute-start | bytes 393224 | tf_op jit(solution)/shard_map/ppermute | solution.py:315
  44.8 1.5 %collective-permute-start.7 = (bf16[1,128,512]{2,1,0:T(8,128)(2,1)S(1)}, bf16[1,128,512]{2,1,0:T(8,128)(2,1)S(1)}, u32[]{:S(2)}, u32[]{:S(2)}) collective-permute-start(bf16[1,128,512]{2,1,0:T(8,128)(2,1)S(1)} %get-tuple-element.55), channel_id=1, source_target_pairs={{0,1},{1,0},{2,3},{3,2},{4,5},{5,4},{6,7},{7,6},{8,9},{9,8},{10,11... | collective-permute-start | bytes 393224 | tf_op jit(solution)/shard_map/ppermute | solution.py:315
  55.8 12.5 %collective-permute-start.9 = (bf16[128,1024]{1,0:T(8,128)(2,1)S(1)}, bf16[128,1024]{1,0:T(8,128)(2,1)S(1)}, u32[]{:S(2)}, u32[]{:S(2)}) collective-permute-start(bf16[128,1024]{1,0:T(8,128)(2,1)S(1)} %get-tuple-element.62), channel_id=1, source_target_pairs={{0,16},{8,24},{16,0},{24,8},{1,17},{9,25},{17,1},{25,9},{2,18},{10... | collective-permute-start | bytes 786440 | tf_op jit(solution)/shard_map/ppermute | solution.py:312
  57.4 10.9 %collective-permute-start.10 = (bf16[128,1024]{1,0:T(8,128)(2,1)S(1)}, bf16[128,1024]{1,0:T(8,128)(2,1)S(1)}, u32[]{:S(2)}, u32[]{:S(2)}) collective-permute-start(bf16[128,1024]{1,0:T(8,128)(2,1)S(1)} %get-tuple-element.63), channel_id=1, source_target_pairs={{0,24},{8,16},{16,8},{24,0},{1,25},{9,17},{17,9},{25,1},{2,26},{10... | collective-permute-start | bytes 786440 | tf_op jit(solution)/shard_map/ppermute | solution.py:312
  58.8 10.7 %collective-permute-start.8 = (bf16[128,1024]{1,0:T(8,128)(2,1)S(1)}, bf16[128,1024]{1,0:T(8,128)(2,1)S(1)}, u32[]{:S(2)}, u32[]{:S(2)}) collective-permute-start(bf16[128,1024]{1,0:T(8,128)(2,1)S(1)} %get-tuple-element.61.refs_7_), channel_id=1, source_target_pairs={{0,8},{8,0},{16,24},{24,16},{1,9},{9,1},{17,25},{25,17},{2,10},{10... | collective-permute-start | bytes 786440 | tf_op jit(solution)/shard_map/ppermute | solution.py:312
  64.0 10.7 %collective-permute-start.14 = (bf16[1,128,1024]{2,1,0:T(8,128)(2,1)S(1)}, bf16[1,128,1024]{2,1,0:T(8,128)(2,1)S(1)}, u32[]{:S(2)}, u32[]{:S(2)}) collective-permute-start(bf16[1,128,1024]{2,1,0:T(8,128)(2,1)S(1)} %get-tuple-element.68), channel_id=1, source_target_pairs={{0,1},{1,0},{2,3},{3,2},{4,5},{5,4},{6,7},{7,6},{8,9},{9,8},{10,11... | collective-permute-start | bytes 786440 | tf_op jit(solution)/shard_map/ppermute | solution.py:315
  69.7 15.9 %collective-permute-start.19 = (bf16[128,1024]{1,0:T(8,128)(2,1)S(1)}, bf16[128,1024]{1,0:T(8,128)(2,1)S(1)}, u32[]{:S(2)}, u32[]{:S(2)}) collective-permute-start(bf16[128,1024]{1,0:T(8,128)(2,1)S(1)} %add_convert_fusion.2.refs_6_.refs_0_.first), channel_id=1, source_target_pairs={{0,24},{8,16},{16,8},{24,0},{1,25},{9,17},{17,9},{25,1},{2,26},{10... | collective-permute-start | bytes 786440 | tf_op jit(solution)/shard_map/ppermute | solution.py:312
  72.1 13.4 %collective-permute-start.18 = (bf16[128,1024]{1,0:T(8,128)(2,1)S(1)}, bf16[128,1024]{1,0:T(8,128)(2,1)S(1)}, u32[]{:S(2)}, u32[]{:S(2)}) collective-permute-start(bf16[128,1024]{1,0:T(8,128)(2,1)S(1)} %add_convert_fusion.2.refs_6_.refs_0_.first), channel_id=1, source_target_pairs={{0,8},{8,0},{16,24},{24,16},{1,9},{9,1},{17,25},{25,17},{2,10},{10... | collective-permute-start | bytes 786440 | tf_op jit(solution)/shard_map/ppermute | solution.py:312
  72.6 9.3 %collective-permute-start.17 = (bf16[128,1024]{1,0:T(8,128)(2,1)S(1)}, bf16[128,1024]{1,0:T(8,128)(2,1)S(1)}, u32[]{:S(2)}, u32[]{:S(2)}) collective-permute-start(bf16[128,1024]{1,0:T(8,128)(2,1)S(1)} %add_convert_fusion.2.refs_6_.refs_0_.first), channel_id=1, source_target_pairs={{0,16},{8,24},{16,0},{24,8},{1,17},{9,25},{17,1},{25,9},{2,18},{10... | collective-permute-start | bytes 786440 | tf_op jit(solution)/shard_map/ppermute | solution.py:312
  73.2 12.3 %collective-permute-start.13 = (bf16[128,1024]{1,0:T(8,128)(2,1)S(1)}, bf16[128,1024]{1,0:T(8,128)(2,1)S(1)}, u32[]{:S(2)}, u32[]{:S(2)}) collective-permute-start(bf16[128,1024]{1,0:T(8,128)(2,1)S(1)} %fusion.refs_6_), channel_id=1, source_target_pairs={{0,4},{1,5},{2,6},{3,7},{4,0},{5,1},{6,2},{7,3},{8,12},{9,13},{10,... | collective-permute-start | bytes 786440 | tf_op jit(solution)/shard_map/ppermute | solution.py:315
  78.6 6.9 %collective-permute-start.16 = (bf16[1,128,1024]{2,1,0:T(8,128)(2,1)S(1)}, bf16[1,128,1024]{2,1,0:T(8,128)(2,1)S(1)}, u32[]{:S(2)}, u32[]{:S(2)}) collective-permute-start(bf16[1,128,1024]{2,1,0:T(8,128)(2,1)S(1)} %get-tuple-element.71), channel_id=1, source_target_pairs={{0,1},{1,0},{2,3},{3,2},{4,5},{5,4},{6,7},{7,6},{8,9},{9,8},{10,11... | collective-permute-start | bytes 786440 | tf_op jit(solution)/shard_map/ppermute | solution.py:315
  82.0 8.3 %collective-permute-start.15 = (bf16[128,1024]{1,0:T(8,128)(2,1)S(1)}, bf16[128,1024]{1,0:T(8,128)(2,1)S(1)}, u32[]{:S(2)}, u32[]{:S(2)}) collective-permute-start(bf16[128,1024]{1,0:T(8,128)(2,1)S(1)} %fusion.5.refs_5_), channel_id=1, source_target_pairs={{0,2},{1,3},{2,0},{3,1},{4,6},{5,7},{6,4},{7,5},{8,10},{9,11},{10,... | collective-permute-start | bytes 786440 | tf_op jit(solution)/shard_map/ppermute | solution.py:315
  93.3 9.2 %collective-permute-start.20 = (bf16[128,1024]{1,0:T(8,128)(2,1)S(1)}, bf16[128,1024]{1,0:T(8,128)(2,1)S(1)}, u32[]{:S(2)}, u32[]{:S(2)}) collective-permute-start(bf16[128,1024]{1,0:T(8,128)(2,1)S(1)} %get-tuple-element.76), channel_id=1, source_target_pairs={{0,8},{8,0},{16,24},{24,16},{1,9},{9,1},{17,25},{25,17},{2,10},{10... | collective-permute-start | bytes 786440 | tf_op jit(solution)/shard_map/ppermute | solution.py:312
  94.7 12.0 %collective-permute-start.21 = (bf16[128,1024]{1,0:T(8,128)(2,1)S(1)}, bf16[128,1024]{1,0:T(8,128)(2,1)S(1)}, u32[]{:S(2)}, u32[]{:S(2)}) collective-permute-start(bf16[128,1024]{1,0:T(8,128)(2,1)S(1)} %get-tuple-element.77), channel_id=1, source_target_pairs={{0,16},{8,24},{16,0},{24,8},{1,17},{9,25},{17,1},{25,9},{2,18},{10... | collective-permute-start | bytes 786440 | tf_op jit(solution)/shard_map/ppermute | solution.py:312
  96.5 11.0 %collective-permute-start.22 = (bf16[128,1024]{1,0:T(8,128)(2,1)S(1)}, bf16[128,1024]{1,0:T(8,128)(2,1)S(1)}, u32[]{:S(2)}, u32[]{:S(2)}) collective-permute-start(bf16[128,1024]{1,0:T(8,128)(2,1)S(1)} %get-tuple-element.78), channel_id=1, source_target_pairs={{0,24},{8,16},{16,8},{24,0},{1,25},{9,17},{17,9},{25,1},{2,26},{10... | collective-permute-start | bytes 786440 | tf_op jit(solution)/shard_map/ppermute | solution.py:312

commit v4 on v3

--- a/solution.py
+++ b/solution.py
@@ -41,10 +41,10 @@
     send, keep = refs.pop(0), refs.pop(0)
     if load_p:
         held = [refs.pop(0)]
+    upcoming = refs.pop(0) if following else None
+    fetched = [refs.pop(0) for _ in extras]
     if load_x:
         x = refs.pop(0)
-    upcoming = refs.pop(0) if following else None
-    fetched = [refs.pop(0) for _ in extras]
     acc, sems = refs
     depth = solved.shape[1]
     piece = depth // PIECES
@@ -169,14 +169,13 @@
     ]
     if load_p:
         shapes.append(jax.ShapeDtypeStruct((span[2], depth), panel.dtype))
-    if load_x:
-        shapes.append(jax.ShapeDtypeStruct((rows, depth), solved.dtype))
     if following:
         shapes.append(jax.ShapeDtypeStruct((2 * len(following) * half, depth), solved.dtype))
     shapes += [
         jax.ShapeDtypeStruct((size, array.shape[-1]), array.dtype) for array, _, _, size in extras
     ]
-    scratch = [pltpu.VMEM((rows, tile), F32)]
+    scratch = [pltpu.VMEM((rows, depth), solved.dtype)] if load_x else []
+    scratch.append(pltpu.VMEM((rows, tile), F32))
     copies = PIECES * (2 * count + 1) + panels[0].shape[-2] // tile + 2 * len(following) + PIECES * len(extras)
     scratch.append(pltpu.SemaphoreType.DMA((copies,)))
     cfg = (
@@ -199,8 +198,6 @@
     out = list(out)
     send, keep = out.pop(0), out.pop(0)
     held = [out.pop(0)] if load_p else []
-    if load_x:
-        x = out.pop(0)
     return send, keep, held, out.pop(0) if following else x, out
 
 
@@ -254,17 +251,9 @@
     carried = early[...]
     if offsets:
         carried += carry(firsts, link, at, offsets)
-    out, res = outs
     value = (residual(1, rhs, parts, counts) - carried).astype(BF16)
-    res[...] = value
-    d = jnp.dot(value, inverse[:, at[members - 1]], preferred_element_type=F32)
-    out[...] = d.astype(out.dtype)
-
-
-def second_rest_kernel(members, cols, place, res, inverse, *outs):
-    at = blocks_of(place[0] // cols, members, res.shape[1])
-    for offset in range(members - 2, -1, -1):
-        d = jnp.dot(res[...], inverse[:, at[offset]], preferred_element_type=F32)
+    for offset in range(members - 1, -1, -1):
+        d = jnp.dot(value, inverse[:, at[offset]], preferred_element_type=F32)
         outs[offset][...] = d.astype(outs[offset].dtype)
 
 
@@ -292,8 +281,7 @@
 
 
 def plan_of(chips):
-    plan = [(0, [o], (0, 1)) for o in range(chips - 1, 0, -1)]
-    plan += [(0, [0], (0, 2)), (0, [0], (1, 2))] if plan else [(0, [0], (0, 1))]
+    plan = [(0, [o], (0, 1)) for o in range(chips - 1, -1, -1)]
     plan += [(1, [o + 1, o], (0, 1)) for o in range(chips - 2, 0, -2)]
     return plan + [(1, [o], (0, 1)) for o in ([1, 0] if chips > 1 else [0])]
 
@@ -321,8 +309,8 @@
     ahead = [n for n, (b, _, _) in enumerate(plan) if b == 0]
     extras[len(ahead) if last > len(ahead) + 1 else 0].append(("inverse", inverse, 0, 0, width))
     piece = width // 2
-    extras[max(0, ahead[-1] - 3)].append(("low", panel, 1, 0, piece))
-    extras[max(0, ahead[-1] - 2)].append(("high", panel, 1, piece, piece))
+    extras[max(0, ahead[-1] - 2)].append(("low", panel, 1, 0, piece))
+    extras[max(0, ahead[-1] - 1)].append(("high", panel, 1, piece, piece))
     extras[last - 1].append(("link", link, None, 0, width))
     extras[last].append(("second", inverse, 1, 0, width))
 
@@ -384,7 +372,7 @@
                 term(b, offset, arrived)
 
     firsts = [first] + [across_row(first, o) for o in range(1, members)]
-    early = sorted({0, members // 2 if members > 2 else 0})
+    early = list(range(max(1, members - 1)))
     late = [o for o in range(members) if o not in early]
     vmem = pl.BlockSpec(memory_space=pltpu.VMEM)
     carried = pl.pallas_call(
@@ -399,18 +387,12 @@
             flops=2 * half * width * width, bytes_accessed=width * width, transcendentals=0
         ),
     )(place, *[firsts[o] for o in early], kept["link"], keep)
-    shape = (half, width)
-    edge, res = solve(
+    parts = solve(
         functools.partial(solve_second_kernel, counts(1), members, late, cols),
-        flops, place,
+        2 * flops, place,
         [rhs, *flat(1), carried, *[firsts[o] for o in late], kept["link"], kept["second"]],
-        shape, [BF16, BF16],
+        (half, width), [F32] + [BF16] * (members - 1),
     )
-    parts = solve(
-        functools.partial(second_rest_kernel, members, cols),
-        flops, place, [res, kept["second"]], shape, [F32] + [BF16] * (members - 2),
-    )
-    parts = list(parts) + [edge]
     arrived = [across_row(parts[offset], offset) for offset in range(1, members)]
     return pl.pallas_call(
         result_kernel,

time: 109 us -> 98.8 us (0.906)
  waiting for transfers between devices: 39.8 us -> 34.7 us
  Pallas kernels: 44.5 us -> 41.1 us
  starting transfers between devices: 23.7 us -> 22.1 us
    ppermute x14 -> x13, waiting for transfers between devices: 20.4 us -> 12.6 us  [across_col(): return lax.ppermute(value, 'col', [(i, i ^ offset) for i in range(cols)])]
    pallas_call x8 -> x7, Pallas kernels: 37.2 us -> 34 us  [partial_sums(): pl.pallas_call(functools.partial(partial_kernel, cfg), in_specs=in_specs,...]
    ppermute x9, waiting for transfers between devices: 19.3 us -> 22.1 us  [across_row(): return lax.ppermute(value, 'row', [(i, i ^ offset) for i in range(members)])]
    ppermute x14 -> x13, starting transfers between devices: 13 us -> 11.5 us  [across_col(): return lax.ppermute(value, 'col', [(i, i ^ offset) for i in range(cols)])]
    pallas_call x3 -> x2, Pallas kernels: 4.56 us -> 3.7 us  [solve(): pl.pallas_call(kernel, in_specs=[pl.BlockSpec(memory_space=pltpu.SMEM)] +...]
  transfers between devices with their start and end apart: 23 -> 22, of which waited for: 12 -> 8; matrix products, arithmetic and copies ran while one was open for 0% -> 0% of each run, Pallas kernels for 16% -> 24%
where the time goes in v4:
time: 98.8 us; the launch traced here: 98.7 us
  Pallas kernels  41.1 us (42%)
  waiting for transfers between devices  34.7 us (35%)
  starting transfers between devices  22.1 us (22%)
    pallas_call x7, Pallas kernels, partial_sums(): pl.pallas_call(functools.partial(partial_kernel, cfg), in_specs=in_specs,...  34 us
    ppermute x9, waiting for transfers between devices, across_row(): return lax.ppermute(value, 'row', [(i, i ^ offset) for i in range(members)])  22.1 us
    ppermute x13, waiting for transfers between devices, across_col(): return lax.ppermute(value, 'col', [(i, i ^ offset) for i in range(cols)])  12.6 us
    ppermute x13, starting transfers between devices, across_col(): return lax.ppermute(value, 'col', [(i, i ^ offset) for i in range(cols)])  11.5 us
    ppermute x9, starting transfers between devices, across_row(): return lax.ppermute(value, 'row', [(i, i ^ offset) for i in range(members)])  10.7 us
    pallas_call x2, Pallas kernels, solve(): pl.pallas_call(kernel, in_specs=[pl.BlockSpec(memory_space=pltpu.SMEM)] +...  3.7 us
    pallas_call x1, Pallas kernels, local(): pl.pallas_call(functools.partial(carry_kernel, members, early, cols), in_...  2.18 us
  transfers between devices with their start and end apart: 22, of which 8 were waited for; matrix products, arithmetic and copies ran while one was open for 0% of the time, Pallas kernels for 24%

profile of v4, /device:TPU:0, one launch (start us, length us, event | category | flops | bytes accessed | tf_op | source)
XLA Modules:
  0.0 98.7 jit_solution(15437596173101009572)
XLA Ops:
  0.0 7.2 %shard_map.55 = (bf16[1,128,1024]{2,1,0:T(8,128)(2,1)S(1)}, f32[1,128,1024]{2,1,0:T(8,128)S(1)}, bf16[1024,6144]{1,0:T(8,128)(2,1)S(1)}, bf16[256,6144]{1,0:T(8,128)(2,1)S(1)}) custom-call(s32[1]{0:T(128)} %bitcast.refs_0_.place, bf16[1024,6144]{1,0:T(8,128)(2,1)} %refs_1_.13, bf16[2,1024,6144]{2,1,0:T(8,128)(2,1)} %refs_5_.1), custom_call_target="tpu_custom_call" | custom-call | flops 3221225472 | bytes 15728640 | tf_op jit(solution)/shard_map/pallas_call | solution.py:185
  7.2 0.6 collective-permute-start.1
  7.7 3.9 %shard_map.56 = (bf16[1,128,1024]{2,1,0:T(8,128)(2,1)S(1)}, f32[1,128,1024]{2,1,0:T(8,128)S(1)}, bf16[256,6144]{1,0:T(8,128)(2,1)S(1)}, bf16[512,6144]{1,0:T(8,128)(2,1)S(1)}) custom-call(s32[1]{0:T(128)} %bitcast.refs_0_.place, bf16[1024,6144]{1,0:T(8,128)(2,1)} %refs_1_.13, bf16[256,6144]{1,0:T(8,128)(2,1)S(1)} %get-tuple-element.39.refs_2_, ...), custom_call_target="tpu_custom_call" | custom-call | flops 3221225472 | bytes 15728640 | tf_op jit(solution)/shard_map/pallas_call | solution.py:185
  11.8 3.1 %collective-permute-start.2 = (bf16[128,1024]{1,0:T(8,128)(2,1)S(1)}, bf16[128,1024]{1,0:T(8,128)(2,1)S(1)}, u32[]{:S(2)}, u32[]{:S(2)}) collective-permute-start(bf16[128,1024]{1,0:T(8,128)(2,1)S(1)} %fusion.2.refs_4_), channel_id=1, source_target_pairs={{0,2},{1,3},{2,0},{3,1},{4,6},{5,7},{6,4},{7,5},{8,10},{9,11},{10,... | collective-permute-start | bytes 786440 | tf_op jit(solution)/shard_map/ppermute | solution.py:303
  15.0 3.9 %shard_map.57 = (bf16[1,128,1024]{2,1,0:T(8,128)(2,1)S(1)}, f32[1,128,1024]{2,1,0:T(8,128)S(1)}, bf16[256,6144]{1,0:T(8,128)(2,1)S(1)}, bf16[512,6144]{1,0:T(8,128)(2,1)S(1)}) custom-call(s32[1]{0:T(128)} %bitcast.refs_0_.place, bf16[1024,6144]{1,0:T(8,128)(2,1)} %refs_1_.13, bf16[256,6144]{1,0:T(8,128)(2,1)S(1)} %get-tuple-element.45.refs_2_, ...), custom_call_target="tpu_custom_call" | custom-call | flops 3221225472 | bytes 15728640 | tf_op jit(solution)/shard_map/pallas_call | solution.py:185
  19.0 3.6 %shard_map.58 = (bf16[1,128,1024]{2,1,0:T(8,128)(2,1)S(1)}, f32[1,128,1024]{2,1,0:T(8,128)S(1)}, bf16[512,6144]{1,0:T(8,128)(2,1)S(1)}) custom-call(s32[1]{0:T(128)} %bitcast.refs_0_.place, bf16[1024,6144]{1,0:T(8,128)(2,1)} %refs_1_.13, bf16[256,6144]{1,0:T(8,128)(2,1)S(1)} %get-tuple-element.48.refs_2_, bf16[1024,6144]{1,0:T(8,128)(2,1)S(1)} %get-tuple-element.40.refs_3_), custom_call_target="tpu_custom_call" | custom-call | flops 3221225472 | bytes 15728640 | tf_op jit(solution)/shard_map/pallas_call | solution.py:185
  22.8 7.1 %shard_map.59 = (bf16[2,128,1024]{2,1,0:T(8,128)(2,1)S(1)}, f32[2,128,1024]{2,1,0:T(8,128)S(1)}, bf16[256,6144]{1,0:T(8,128)(2,1)S(1)}, bf16[1024,4096]{1,0:T(8,128)(2,1)S(1)}) custom-call(s32[1]{0:T(128)} %bitcast.refs_0_.place, bf16[1024,6144]{1,0:T(8,128)(2,1)} %refs_1_.13, bf16[512,6144]{1,0:T(8,128)(2,1)S(1)} %get-tuple-element.51.refs_2_, ...), custom_call_target="tpu_custom_call" | custom-call | flops 6442450944 | bytes 18874368 | tf_op jit(solution)/shard_map/pallas_call | solution.py:185
  30.0 0.6 collective-permute-start.10
  30.6 2.6 %collective-permute-start.3 = (bf16[128,1024]{1,0:T(8,128)(2,1)S(1)}, bf16[128,1024]{1,0:T(8,128)(2,1)S(1)}, u32[]{:S(2)}, u32[]{:S(2)}) collective-permute-start(bf16[128,1024]{1,0:T(8,128)(2,1)S(1)} %fusion.1.refs_5_), channel_id=1, source_target_pairs={{0,4},{1,5},{2,6},{3,7},{4,0},{5,1},{6,2},{7,3},{8,12},{9,13},{10,... | collective-permute-start | bytes 786440 | tf_op jit(solution)/shard_map/ppermute | solution.py:303
  33.7 1.6 %collective-permute-start.11 = (bf16[128,1024]{1,0:T(8,128)(2,1)S(1)}, bf16[128,1024]{1,0:T(8,128)(2,1)S(1)}, u32[]{:S(2)}, u32[]{:S(2)}) collective-permute-start(bf16[128,1024]{1,0:T(8,128)(2,1)S(1)} %fusion.4.refs_5_), channel_id=1, source_target_pairs={{0,2},{1,3},{2,0},{3,1},{4,6},{5,7},{6,4},{7,5},{8,10},{9,11},{10,... | collective-permute-start | bytes 786440 | tf_op jit(solution)/shard_map/ppermute | solution.py:303
  35.3 10.3 %collective-permute-done.3.refs_0_ = bf16[128,1024]{1,0:T(8,128)(2,1)S(1)} collective-permute-done((bf16[128,1024]{1,0:T(8,128)(2,1)S(1)}, bf16[128,1024]{1,0:T(8,128)(2,1)S(1)}, u32[]{:S(2)}, u32[]{:S(2)}) %collective-permute-start.3) | collective-permute-done | bytes 262176 | tf_op jit(solution)/shard_map/ppermute | solution.py:303
  45.7 2.2 %collective-permute-done.5.refs_1_ = bf16[128,1024]{1,0:T(8,128)(2,1)S(1)} collective-permute-done((bf16[128,1024]{1,0:T(8,128)(2,1)S(1)}, bf16[128,1024]{1,0:T(8,128)(2,1)S(1)}, u32[]{:S(2)}, u32[]{:S(2)}) %collective-permute-start.5) | collective-permute-done | bytes 262176 | tf_op jit(solution)/shard_map/ppermute | solution.py:303
  47.9 1.5 %shard_map.60 = (f32[128,1024]{1,0:T(8,128)S(1)}, bf16[128,1024]{1,0:T(8,128)(2,1)S(1)}, bf16[128,1024]{1,0:T(8,128)(2,1)S(1)}, bf16[128,1024]{1,0:T(8,128)(2,1)S(1)}) custom-call(s32[1]{0:T(128)} %bitcast.refs_0_.place, bf16[128,2,1024]{2,1,0:T(2,128)(2,1)S(1)} %copy-done, bf16[128,1024]{1,0:T(8,128)(2,1)S(1)} %collective-permute-done.3.refs_0_, ...), custom_call_target="tpu_custom_call" | custom-call | flops 1073741824 | bytes 8388608 | tf_op jit(solution)/shard_map/pallas_call | solution.py:262
  49.4 2.5 %collective-permute-start.9 = (bf16[128,1024]{1,0:T(8,128)(2,1)S(1)}, bf16[128,1024]{1,0:T(8,128)(2,1)S(1)}, u32[]{:S(2)}, u32[]{:S(2)}) collective-permute-start(bf16[128,1024]{1,0:T(8,128)(2,1)S(1)} %get-tuple-element.58), channel_id=1, source_target_pairs={{0,24},{8,16},{16,8},{24,0},{1,25},{9,17},{17,9},{25,1},{2,26},{10... | collective-permute-start | bytes 786440 | tf_op jit(solution)/shard_map/ppermute | solution.py:300
  51.9 0.5 collective-permute-start.8
  52.4 0.5 collective-permute-start.7
  53.1 4.6 %shard_map.61 = (bf16[1,128,1024]{2,1,0:T(8,128)(2,1)S(1)}, f32[1,128,1024]{2,1,0:T(8,128)S(1)}, bf16[256,6144]{1,0:T(8,128)(2,1)S(1)}, bf16[1024,4096]{1,0:T(8,128)(2,1)S(1)}) custom-call(s32[1]{0:T(128)} %bitcast.refs_0_.place, bf16[1024,6144]{1,0:T(8,128)(2,1)} %refs_1_.13, bf16[256,6144]{1,0:T(8,128)(2,1)S(1)} %get-tuple-element.61.refs_2_, ...), custom_call_target="tpu_custom_call" | custom-call | flops 3221225472 | bytes 15728640 | tf_op jit(solution)/shard_map/pallas_call | solution.py:185
  57.7 1.9 %collective-permute-done.9 = bf16[128,1024]{1,0:T(8,128)(2,1)S(1)} collective-permute-done((bf16[128,1024]{1,0:T(8,128)(2,1)S(1)}, bf16[128,1024]{1,0:T(8,128)(2,1)S(1)}, u32[]{:S(2)}, u32[]{:S(2)}) %collective-permute-start.9) | collective-permute-done | bytes 262176 | tf_op jit(solution)/shard_map/ppermute | solution.py:300
  59.6 3.1 %collective-permute-done.8 = bf16[128,1024]{1,0:T(8,128)(2,1)S(1)} collective-permute-done((bf16[128,1024]{1,0:T(8,128)(2,1)S(1)}, bf16[128,1024]{1,0:T(8,128)(2,1)S(1)}, u32[]{:S(2)}, u32[]{:S(2)}) %collective-permute-start.8) | collective-permute-done | bytes 262176 | tf_op jit(solution)/shard_map/ppermute | solution.py:300
  62.9 1.6 %collective-permute-start.16 = (bf16[128,1024]{1,0:T(8,128)(2,1)S(1)}, bf16[128,1024]{1,0:T(8,128)(2,1)S(1)}, u32[]{:S(2)}, u32[]{:S(2)}) collective-permute-start(bf16[128,1024]{1,0:T(8,128)(2,1)S(1)} %add_convert_fusion.2.refs_6_.refs_0_.first), channel_id=1, source_target_pairs={{0,8},{8,0},{16,24},{24,16},{1,9},{9,1},{17,25},{25,17},{2,10},{10... | collective-permute-start | bytes 786440 | tf_op jit(solution)/shard_map/ppermute | solution.py:300
  64.5 0.7 collective-permute-start.17
  65.2 1.3 %collective-permute-start.18 = (bf16[128,1024]{1,0:T(8,128)(2,1)S(1)}, bf16[128,1024]{1,0:T(8,128)(2,1)S(1)}, u32[]{:S(2)}, u32[]{:S(2)}) collective-permute-start(bf16[128,1024]{1,0:T(8,128)(2,1)S(1)} %add_convert_fusion.2.refs_6_.refs_0_.first), channel_id=1, source_target_pairs={{0,24},{8,16},{16,8},{24,0},{1,25},{9,17},{17,9},{25,1},{2,26},{10... | collective-permute-start | bytes 786440 | tf_op jit(solution)/shard_map/ppermute | solution.py:300
  66.5 2.2 %collective-permute-start.14 = (bf16[128,1024]{1,0:T(8,128)(2,1)S(1)}, bf16[128,1024]{1,0:T(8,128)(2,1)S(1)}, u32[]{:S(2)}, u32[]{:S(2)}) collective-permute-start(bf16[128,1024]{1,0:T(8,128)(2,1)S(1)} %fusion.5.refs_5_), channel_id=1, source_target_pairs={{0,2},{1,3},{2,0},{3,1},{4,6},{5,7},{6,4},{7,5},{8,10},{9,11},{10,... | collective-permute-start | bytes 786440 | tf_op jit(solution)/shard_map/ppermute | solution.py:303
  68.7 3.6 %shard_map.62 = (bf16[1,128,1024]{2,1,0:T(8,128)(2,1)S(1)}, f32[1,128,1024]{2,1,0:T(8,128)S(1)}, bf16[1024,4096]{1,0:T(8,128)(2,1)S(1)}) custom-call(s32[1]{0:T(128)} %bitcast.refs_0_.place, bf16[1024,6144]{1,0:T(8,128)(2,1)} %refs_1_.13, bf16[256,6144]{1,0:T(8,128)(2,1)S(1)} %get-tuple-element.64.refs_2_, bf16[512,6144]{1,0:T(8,128)(2,1)S(1)} %get-tuple-element.52.refs_3_, ...), custom_call_target="tpu_custom_call" | custom-call | flops 3221225472 | bytes 15728640 | tf_op jit(solution)/shard_map/pallas_call | solution.py:185
  72.4 5.5 %collective-permute-done.17.refs_2_ = bf16[128,1024]{1,0:T(8,128)(2,1)S(1)} collective-permute-done((bf16[128,1024]{1,0:T(8,128)(2,1)S(1)}, bf16[128,1024]{1,0:T(8,128)(2,1)S(1)}, u32[]{:S(2)}, u32[]{:S(2)}) %collective-permute-start.17) | collective-permute-done | bytes 262176 | tf_op jit(solution)/shard_map/ppermute | solution.py:300
  77.9 2.2 %carry.1.refs_4_ = f32[128,1024]{1,0:T(8,128)S(1)} custom-call(s32[1]{0:T(128)} %bitcast.refs_0_.place, bf16[128,1024]{1,0:T(8,128)(2,1)S(1)} %add_convert_fusion.2.refs_6_.refs_0_.first, bf16[128,1024]{1,0:T(8,128)(2,1)S(1)} %collective-permute-done.16.refs_1_, bf16[128,1024]{1,0:T(8,128)(2,1)S(1)} %collective-permute-done.17.refs_2_, ...), custom_call_target="tpu_custom_call" | custom-call | flops 268435456 | bytes 1048576 | tf_op jit(solution)/shard_map/carry/pallas_call | solution.py:378
  80.2 2.2 %shard_map.63 = (f32[128,1024]{1,0:T(8,128)S(1)}, bf16[128,1024]{1,0:T(8,128)(2,1)S(1)}, bf16[128,1024]{1,0:T(8,128)(2,1)S(1)}, bf16[128,1024]{1,0:T(8,128)(2,1)S(1)}) custom-call(s32[1]{0:T(128)} %bitcast.refs_0_.place, bf16[128,2,1024]{2,1,0:T(2,128)(2,1)S(1)} %copy-done, bf16[128,1024]{1,0:T(8,128)(2,1)S(1)} %collective-permute-done.12.refs_0_, ...), custom_call_target="tpu_custom_call" | custom-call | flops 2147483648 | bytes 16777216 | tf_op jit(solution)/shard_map/pallas_call | solution.py:262
  82.4 1.7 %collective-permute-start.19 = (bf16[128,1024]{1,0:T(8,128)(2,1)S(1)}, bf16[128,1024]{1,0:T(8,128)(2,1)S(1)}, u32[]{:S(2)}, u32[]{:S(2)}) collective-permute-start(bf16[128,1024]{1,0:T(8,128)(2,1)S(1)} %get-tuple-element.70), channel_id=1, source_target_pairs={{0,8},{8,0},{16,24},{24,16},{1,9},{9,1},{17,25},{25,17},{2,10},{10... | collective-permute-start | bytes 786440 | tf_op jit(solution)/shard_map/ppermute | solution.py:300
  84.5 1.4 %collective-permute-start.21 = (bf16[128,1024]{1,0:T(8,128)(2,1)S(1)}, bf16[128,1024]{1,0:T(8,128)(2,1)S(1)}, u32[]{:S(2)}, u32[]{:S(2)}) collective-permute-start(bf16[128,1024]{1,0:T(8,128)(2,1)S(1)} %get-tuple-element.72), channel_id=1, source_target_pairs={{0,24},{8,16},{16,8},{24,0},{1,25},{9,17},{17,9},{25,1},{2,26},{10... | collective-permute-start | bytes 786440 | tf_op jit(solution)/shard_map/ppermute | solution.py:300
  85.9 5.7 %collective-permute-done.19.refs_1_ = bf16[128,1024]{1,0:T(8,128)(2,1)S(1)} collective-permute-done((bf16[128,1024]{1,0:T(8,128)(2,1)S(1)}, bf16[128,1024]{1,0:T(8,128)(2,1)S(1)}, u32[]{:S(2)}, u32[]{:S(2)}) %collective-permute-start.19) | collective-permute-done | bytes 262176 | tf_op jit(solution)/shard_map/ppermute | solution.py:300
  91.6 5.8 %collective-permute-done.20.refs_2_ = bf16[128,1024]{1,0:T(8,128)(2,1)S(1)} collective-permute-done((bf16[128,1024]{1,0:T(8,128)(2,1)S(1)}, bf16[128,1024]{1,0:T(8,128)(2,1)S(1)}, u32[]{:S(2)}, u32[]{:S(2)}) %collective-permute-start.20) | collective-permute-done | bytes 262176 | tf_op jit(solution)/shard_map/ppermute | solution.py:300
  97.5 1.2 %result.1 = bf16[128,2,1024]{2,1,0:T(2,128)(2,1)} custom-call(bf16[128,1024]{1,0:T(8,128)(2,1)S(1)} %add_convert_fusion.2.refs_6_.refs_0_.first, f32[128,1024]{1,0:T(8,128)S(1)} %get-tuple-element.69.refs_0_, bf16[128,1024]{1,0:T(8,128)(2,1)S(1)} %collective-permute-done.19.refs_1_, bf16[128,1024]{1,0:T(8,128)(2,1)S(1)} %collective-permute-done.20.refs_2_, ...), custom_call_target="tpu_custom_call" | custom-call | tf_op jit(solution)/shard_map/result/pallas_call | solution.py:397
  (32 shorter events, 2.0 us)
Async XLA Ops:
  7.2 4.6 %collective-permute-start.1 = (bf16[1,128,1024]{2,1,0:T(8,128)(2,1)S(1)}, bf16[1,128,1024]{2,1,0:T(8,128)(2,1)S(1)}, u32[]{:S(2)}, u32[]{:S(2)}) collective-permute-start(bf16[1,128,1024]{2,1,0:T(8,128)(2,1)S(1)} %get-tuple-element.44), channel_id=1, source_target_pairs={{0,1},{1,0},{2,3},{3,2},{4,5},{5,4},{6,7},{7,6},{8,9},{9,8},{10,11... | collective-permute-start | bytes 786440 | tf_op jit(solution)/shard_map/ppermute | solution.py:303
  11.7 11.0 %collective-permute-start = (bf16[1,128,1024]{2,1,0:T(8,128)(2,1)S(1)}, bf16[1,128,1024]{2,1,0:T(8,128)(2,1)S(1)}, u32[]{:S(2)}, u32[]{:S(2)}) collective-permute-start(bf16[1,128,1024]{2,1,0:T(8,128)(2,1)S(1)} %get-tuple-element.42), channel_id=1, source_target_pairs={{0,1},{1,0},{2,3},{3,2},{4,5},{5,4},{6,7},{7,6},{8,9},{9,8},{10,11... | collective-permute-start | bytes 786440 | tf_op jit(solution)/shard_map/ppermute | solution.py:303
  11.8 10.9 %collective-permute-start.2 = (bf16[128,1024]{1,0:T(8,128)(2,1)S(1)}, bf16[128,1024]{1,0:T(8,128)(2,1)S(1)}, u32[]{:S(2)}, u32[]{:S(2)}) collective-permute-start(bf16[128,1024]{1,0:T(8,128)(2,1)S(1)} %fusion.2.refs_4_), channel_id=1, source_target_pairs={{0,2},{1,3},{2,0},{3,1},{4,6},{5,7},{6,4},{7,5},{8,10},{9,11},{10,... | collective-permute-start | bytes 786440 | tf_op jit(solution)/shard_map/ppermute | solution.py:303
  18.9 3.7 %collective-permute-start.4 = (bf16[1,128,1024]{2,1,0:T(8,128)(2,1)S(1)}, bf16[1,128,1024]{2,1,0:T(8,128)(2,1)S(1)}, u32[]{:S(2)}, u32[]{:S(2)}) collective-permute-start(bf16[1,128,1024]{2,1,0:T(8,128)(2,1)S(1)} %get-tuple-element.47), channel_id=1, source_target_pairs={{0,1},{1,0},{2,3},{3,2},{4,5},{5,4},{6,7},{7,6},{8,9},{9,8},{10,11... | collective-permute-start | bytes 786440 | tf_op jit(solution)/shard_map/ppermute | solution.py:303
  22.8 25.1 %copy-start = (bf16[128,2,1024]{2,1,0:T(2,128)(2,1)S(1)}, bf16[128,2,1024]{2,1,0:T(2,128)(2,1)}, u32[]{:S(2)}) copy-start(bf16[128,2,1024]{2,1,0:T(2,128)(2,1)} %rhs.3) | copy-start | bytes 1572868
  30.0 3.7 %collective-permute-start.10 = (bf16[2,128,1024]{2,1,0:T(8,128)(2,1)S(1)}, bf16[2,128,1024]{2,1,0:T(8,128)(2,1)S(1)}, u32[]{:S(2)}, u32[]{:S(2)}) collective-permute-start(bf16[2,128,1024]{2,1,0:T(8,128)(2,1)S(1)} %get-tuple-element.60), channel_id=1, source_target_pairs={{0,1},{1,0},{2,3},{3,2},{4,5},{5,4},{6,7},{7,6},{8,9},{9,8},{10,11... | collective-permute-start | bytes 1572872 | tf_op jit(solution)/shard_map/ppermute | solution.py:303
  30.5 4.8 %collective-permute-start.6 = (bf16[1,128,1024]{2,1,0:T(8,128)(2,1)S(1)}, bf16[1,128,1024]{2,1,0:T(8,128)(2,1)S(1)}, u32[]{:S(2)}, u32[]{:S(2)}) collective-permute-start(bf16[1,128,1024]{2,1,0:T(8,128)(2,1)S(1)} %get-tuple-element.50), channel_id=1, source_target_pairs={{0,1},{1,0},{2,3},{3,2},{4,5},{5,4},{6,7},{7,6},{8,9},{9,8},{10,11... | collective-permute-start | bytes 786440 | tf_op jit(solution)/shard_map/ppermute | solution.py:303
  30.6 15.1 %collective-permute-start.3 = (bf16[128,1024]{1,0:T(8,128)(2,1)S(1)}, bf16[128,1024]{1,0:T(8,128)(2,1)S(1)}, u32[]{:S(2)}, u32[]{:S(2)}) collective-permute-start(bf16[128,1024]{1,0:T(8,128)(2,1)S(1)} %fusion.1.refs_5_), channel_id=1, source_target_pairs={{0,4},{1,5},{2,6},{3,7},{4,0},{5,1},{6,2},{7,3},{8,12},{9,13},{10,... | collective-permute-start | bytes 786440 | tf_op jit(solution)/shard_map/ppermute | solution.py:303
  33.2 14.7 %collective-permute-start.5 = (bf16[128,1024]{1,0:T(8,128)(2,1)S(1)}, bf16[128,1024]{1,0:T(8,128)(2,1)S(1)}, u32[]{:S(2)}, u32[]{:S(2)}) collective-permute-start(bf16[128,1024]{1,0:T(8,128)(2,1)S(1)} %fusion.3.refs_6_), channel_id=1, source_target_pairs={{0,2},{1,3},{2,0},{3,1},{4,6},{5,7},{6,4},{7,5},{8,10},{9,11},{10,... | collective-permute-start | bytes 786440 | tf_op jit(solution)/shard_map/ppermute | solution.py:303
  33.7 19.2 %collective-permute-start.11 = (bf16[128,1024]{1,0:T(8,128)(2,1)S(1)}, bf16[128,1024]{1,0:T(8,128)(2,1)S(1)}, u32[]{:S(2)}, u32[]{:S(2)}) collective-permute-start(bf16[128,1024]{1,0:T(8,128)(2,1)S(1)} %fusion.4.refs_5_), channel_id=1, source_target_pairs={{0,2},{1,3},{2,0},{3,1},{4,6},{5,7},{6,4},{7,5},{8,10},{9,11},{10,... | collective-permute-start | bytes 786440 | tf_op jit(solution)/shard_map/ppermute | solution.py:303
  49.4 10.2 %collective-permute-start.9 = (bf16[128,1024]{1,0:T(8,128)(2,1)S(1)}, bf16[128,1024]{1,0:T(8,128)(2,1)S(1)}, u32[]{:S(2)}, u32[]{:S(2)}) collective-permute-start(bf16[128,1024]{1,0:T(8,128)(2,1)S(1)} %get-tuple-element.58), channel_id=1, source_target_pairs={{0,24},{8,16},{16,8},{24,0},{1,25},{9,17},{17,9},{25,1},{2,26},{10... | collective-permute-start | bytes 786440 | tf_op jit(solution)/shard_map/ppermute | solution.py:300
  51.9 10.8 %collective-permute-start.8 = (bf16[128,1024]{1,0:T(8,128)(2,1)S(1)}, bf16[128,1024]{1,0:T(8,128)(2,1)S(1)}, u32[]{:S(2)}, u32[]{:S(2)}) collective-permute-start(bf16[128,1024]{1,0:T(8,128)(2,1)S(1)} %get-tuple-element.57), channel_id=1, source_target_pairs={{0,16},{8,24},{16,0},{24,8},{1,17},{9,25},{17,1},{25,9},{2,18},{10... | collective-permute-start | bytes 786440 | tf_op jit(solution)/shard_map/ppermute | solution.py:300
  52.4 10.3 %collective-permute-start.7 = (bf16[128,1024]{1,0:T(8,128)(2,1)S(1)}, bf16[128,1024]{1,0:T(8,128)(2,1)S(1)}, u32[]{:S(2)}, u32[]{:S(2)}) collective-permute-start(bf16[128,1024]{1,0:T(8,128)(2,1)S(1)} %get-tuple-element.56.refs_7_), channel_id=1, source_target_pairs={{0,8},{8,0},{16,24},{24,16},{1,9},{9,1},{17,25},{25,17},{2,10},{10... | collective-permute-start | bytes 786440 | tf_op jit(solution)/shard_map/ppermute | solution.py:300
  57.6 8.8 %collective-permute-start.13 = (bf16[1,128,1024]{2,1,0:T(8,128)(2,1)S(1)}, bf16[1,128,1024]{2,1,0:T(8,128)(2,1)S(1)}, u32[]{:S(2)}, u32[]{:S(2)}) collective-permute-start(bf16[1,128,1024]{2,1,0:T(8,128)(2,1)S(1)} %get-tuple-element.63), channel_id=1, source_target_pairs={{0,1},{1,0},{2,3},{3,2},{4,5},{5,4},{6,7},{7,6},{8,9},{9,8},{10,11... | collective-permute-start | bytes 786440 | tf_op jit(solution)/shard_map/ppermute | solution.py:303
  62.9 9.4 %collective-permute-start.16 = (bf16[128,1024]{1,0:T(8,128)(2,1)S(1)}, bf16[128,1024]{1,0:T(8,128)(2,1)S(1)}, u32[]{:S(2)}, u32[]{:S(2)}) collective-permute-start(bf16[128,1024]{1,0:T(8,128)(2,1)S(1)} %add_convert_fusion.2.refs_6_.refs_0_.first), channel_id=1, source_target_pairs={{0,8},{8,0},{16,24},{24,16},{1,9},{9,1},{17,25},{25,17},{2,10},{10... | collective-permute-start | bytes 786440 | tf_op jit(solution)/shard_map/ppermute | solution.py:300
  64.5 13.5 %collective-permute-start.17 = (bf16[128,1024]{1,0:T(8,128)(2,1)S(1)}, bf16[128,1024]{1,0:T(8,128)(2,1)S(1)}, u32[]{:S(2)}, u32[]{:S(2)}) collective-permute-start(bf16[128,1024]{1,0:T(8,128)(2,1)S(1)} %add_convert_fusion.2.refs_6_.refs_0_.first), channel_id=1, source_target_pairs={{0,16},{8,24},{16,0},{24,8},{1,17},{9,25},{17,1},{25,9},{2,18},{10... | collective-permute-start | bytes 786440 | tf_op jit(solution)/shard_map/ppermute | solution.py:300
  65.2 14.9 %collective-permute-start.18 = (bf16[128,1024]{1,0:T(8,128)(2,1)S(1)}, bf16[128,1024]{1,0:T(8,128)(2,1)S(1)}, u32[]{:S(2)}, u32[]{:S(2)}) collective-permute-start(bf16[128,1024]{1,0:T(8,128)(2,1)S(1)} %add_convert_fusion.2.refs_6_.refs_0_.first), channel_id=1, source_target_pairs={{0,24},{8,16},{16,8},{24,0},{1,25},{9,17},{17,9},{25,1},{2,26},{10... | collective-permute-start | bytes 786440 | tf_op jit(solution)/shard_map/ppermute | solution.py:300
  66.5 13.7 %collective-permute-start.12 = (bf16[128,1024]{1,0:T(8,128)(2,1)S(1)}, bf16[128,1024]{1,0:T(8,128)(2,1)S(1)}, u32[]{:S(2)}, u32[]{:S(2)}) collective-permute-start(bf16[128,1024]{1,0:T(8,128)(2,1)S(1)} %fusion.refs_6_), channel_id=1, source_target_pairs={{0,4},{1,5},{2,6},{3,7},{4,0},{5,1},{6,2},{7,3},{8,12},{9,13},{10,... | collective-permute-start | bytes 786440 | tf_op jit(solution)/shard_map/ppermute | solution.py:303
  66.5 13.6 %collective-permute-start.14 = (bf16[128,1024]{1,0:T(8,128)(2,1)S(1)}, bf16[128,1024]{1,0:T(8,128)(2,1)S(1)}, u32[]{:S(2)}, u32[]{:S(2)}) collective-permute-start(bf16[128,1024]{1,0:T(8,128)(2,1)S(1)} %fusion.5.refs_5_), channel_id=1, source_target_pairs={{0,2},{1,3},{2,0},{3,1},{4,6},{5,7},{6,4},{7,5},{8,10},{9,11},{10,... | collective-permute-start | bytes 786440 | tf_op jit(solution)/shard_map/ppermute | solution.py:303
  72.3 7.8 %collective-permute-start.15 = (bf16[1,128,1024]{2,1,0:T(8,128)(2,1)S(1)}, bf16[1,128,1024]{2,1,0:T(8,128)(2,1)S(1)}, u32[]{:S(2)}, u32[]{:S(2)}) collective-permute-start(bf16[1,128,1024]{2,1,0:T(8,128)(2,1)S(1)} %get-tuple-element.66), channel_id=1, source_target_pairs={{0,1},{1,0},{2,3},{3,2},{4,5},{5,4},{6,7},{7,6},{8,9},{9,8},{10,11... | collective-permute-start | bytes 786440 | tf_op jit(solution)/shard_map/ppermute | solution.py:303
  82.4 9.2 %collective-permute-start.19 = (bf16[128,1024]{1,0:T(8,128)(2,1)S(1)}, bf16[128,1024]{1,0:T(8,128)(2,1)S(1)}, u32[]{:S(2)}, u32[]{:S(2)}) collective-permute-start(bf16[128,1024]{1,0:T(8,128)(2,1)S(1)} %get-tuple-element.70), channel_id=1, source_target_pairs={{0,8},{8,0},{16,24},{24,16},{1,9},{9,1},{17,25},{25,17},{2,10},{10... | collective-permute-start | bytes 786440 | tf_op jit(solution)/shard_map/ppermute | solution.py:300
  84.0 13.4 %collective-permute-start.20 = (bf16[128,1024]{1,0:T(8,128)(2,1)S(1)}, bf16[128,1024]{1,0:T(8,128)(2,1)S(1)}, u32[]{:S(2)}, u32[]{:S(2)}) collective-permute-start(bf16[128,1024]{1,0:T(8,128)(2,1)S(1)} %get-tuple-element.71), channel_id=1, source_target_pairs={{0,16},{8,24},{16,0},{24,8},{1,17},{9,25},{17,1},{25,9},{2,18},{10... | collective-permute-start | bytes 786440 | tf_op jit(solution)/shard_map/ppermute | solution.py:300
  84.5 13.0 %collective-permute-start.21 = (bf16[128,1024]{1,0:T(8,128)(2,1)S(1)}, bf16[128,1024]{1,0:T(8,128)(2,1)S(1)}, u32[]{:S(2)}, u32[]{:S(2)}) collective-permute-start(bf16[128,1024]{1,0:T(8,128)(2,1)S(1)} %get-tuple-element.72), channel_id=1, source_target_pairs={{0,24},{8,16},{16,8},{24,0},{1,25},{9,17},{17,9},{25,1},{2,26},{10... | collective-permute-start | bytes 786440 | tf_op jit(solution)/shard_map/ppermute | solution.py:300

commit v5 on v4

--- a/solution.py
+++ b/solution.py
@@ -9,7 +9,7 @@
 
 
 F32, BF16 = jnp.float32, jnp.bfloat16
-AHEAD = 3
+AHEAD = 8
 PIECES = 4
 LIMIT = 6 << 20
 
@@ -281,14 +281,14 @@
 
 
 def plan_of(chips):
-    plan = [(0, [o], (0, 1)) for o in range(chips - 1, -1, -1)]
+    order = [chips - 1] + [o + step for o in range(chips - 3, 0, -2) for step in (0, 1)]
+    plan = [(0, [o], (0, 1)) for o in order + ([0] if chips > 1 else [])]
     plan += [(1, [o + 1, o], (0, 1)) for o in range(chips - 2, 0, -2)]
     return plan + [(1, [o], (0, 1)) for o in ([1, 0] if chips > 1 else [0])]
 
 
-def deadline(plan, n, offset):
-    odd, last = offset % 2, len(plan) - 1
-    return min(last, n + (1 if plan[n][0] else 2 if odd else 3))
+def deadline(plan, n):
+    return min(len(plan) - 1, n + (1 if plan[n][0] else 2))
 
 
 def local(members, chips, rhs, solved, panel, inverse, link):
@@ -364,7 +364,7 @@
             if offset % 2 == 0:
                 value += passing.pop((b, offset)).astype(F32)
             value = value.astype(BF16)
-            due[deadline(plan, n, offset)].append(value)
+            due[deadline(plan, n) if b == 0 or offset % 2 else last].append(value)
             arrived = across_col(value, 2 if offset % 2 else 2 * offset)
             if offset > 1 and offset % 2:
                 passing[b, offset - 1] = arrived

time: 98.8 us -> 95.4 us (0.966)
  waiting for transfers between devices: 34.7 us -> 26.2 us
  starting transfers between devices: 22.1 us -> 27.4 us
    ppermute x9, waiting for transfers between devices: 22.1 us -> 14.7 us  [across_row(): return lax.ppermute(value, 'row', [(i, i ^ offset) for i in range(members)])]
    ppermute x13, starting transfers between devices: 11.5 us -> 16.8 us  [across_col(): return lax.ppermute(value, 'col', [(i, i ^ offset) for i in range(cols)])]
    ppermute x13, waiting for transfers between devices: 12.6 us -> 11.5 us  [across_col(): return lax.ppermute(value, 'col', [(i, i ^ offset) for i in range(cols)])]
  transfers between devices with their start and end apart: 22 -> 22, of which waited for: 8 -> 8; matrix products, arithmetic and copies ran while one was open for 0% -> 0% of each run, Pallas kernels for 24% -> 25%
where the time goes in v5:
time: 95.4 us; the launch traced here: 95.3 us
  Pallas kernels  40.9 us (43%)
  starting transfers between devices  27.4 us (29%)
  waiting for transfers between devices  26.2 us (27%)
    pallas_call x7, Pallas kernels, partial_sums(): pl.pallas_call(functools.partial(partial_kernel, cfg), in_specs=in_specs,...  33.8 us
    ppermute x13, starting transfers between devices, across_col(): return lax.ppermute(value, 'col', [(i, i ^ offset) for i in range(cols)])  16.8 us
    ppermute x9, waiting for transfers between devices, across_row(): return lax.ppermute(value, 'row', [(i, i ^ offset) for i in range(members)])  14.7 us
    ppermute x13, waiting for transfers between devices, across_col(): return lax.ppermute(value, 'col', [(i, i ^ offset) for i in range(cols)])  11.5 us
    ppermute x9, starting transfers between devices, across_row(): return lax.ppermute(value, 'row', [(i, i ^ offset) for i in range(members)])  10.7 us
    pallas_call x2, Pallas kernels, solve(): pl.pallas_call(kernel, in_specs=[pl.BlockSpec(memory_space=pltpu.SMEM)] +...  3.65 us
    pallas_call x1, Pallas kernels, local(): pl.pallas_call(functools.partial(carry_kernel, members, early, cols), in_...  2.18 us
  transfers between devices with their start and end apart: 22, of which 8 were waited for; matrix products, arithmetic and copies ran while one was open for 0% of the time, Pallas kernels for 25%

profile of v5, /device:TPU:0, one launch (start us, length us, event | category | flops | bytes accessed | tf_op | source)
XLA Modules:
  0.0 95.3 jit_solution(10605383572279699261)
XLA Ops:
  0.0 7.0 %shard_map.55 = (bf16[1,128,1024]{2,1,0:T(8,128)(2,1)S(1)}, f32[1,128,1024]{2,1,0:T(8,128)S(1)}, bf16[1024,6144]{1,0:T(8,128)(2,1)S(1)}, bf16[256,6144]{1,0:T(8,128)(2,1)S(1)}) custom-call(s32[1]{0:T(128)} %bitcast.refs_0_.place, bf16[1024,6144]{1,0:T(8,128)(2,1)} %refs_1_.13, bf16[2,1024,6144]{2,1,0:T(8,128)(2,1)} %refs_5_.1), custom_call_target="tpu_custom_call" | custom-call | flops 3221225472 | bytes 15728640 | tf_op jit(solution)/shard_map/pallas_call | solution.py:185
  7.0 0.6 collective-permute-start.2
  7.6 3.9 %shard_map.56 = (bf16[1,128,1024]{2,1,0:T(8,128)(2,1)S(1)}, f32[1,128,1024]{2,1,0:T(8,128)S(1)}, bf16[256,6144]{1,0:T(8,128)(2,1)S(1)}, bf16[512,6144]{1,0:T(8,128)(2,1)S(1)}) custom-call(s32[1]{0:T(128)} %bitcast.refs_0_.place, bf16[1024,6144]{1,0:T(8,128)(2,1)} %refs_1_.13, bf16[256,6144]{1,0:T(8,128)(2,1)S(1)} %get-tuple-element.39.refs_2_, ...), custom_call_target="tpu_custom_call" | custom-call | flops 3221225472 | bytes 15728640 | tf_op jit(solution)/shard_map/pallas_call | solution.py:185
  11.7 3.1 %collective-permute-start.4 = (bf16[128,1024]{1,0:T(8,128)(2,1)S(1)}, bf16[128,1024]{1,0:T(8,128)(2,1)S(1)}, u32[]{:S(2)}, u32[]{:S(2)}) collective-permute-start(bf16[128,1024]{1,0:T(8,128)(2,1)S(1)} %fusion.3.refs_4_), channel_id=1, source_target_pairs={{0,2},{1,3},{2,0},{3,1},{4,6},{5,7},{6,4},{7,5},{8,10},{9,11},{10,... | collective-permute-start | bytes 786440 | tf_op jit(solution)/shard_map/ppermute | solution.py:303
  14.8 3.9 %shard_map.57 = (bf16[1,128,1024]{2,1,0:T(8,128)(2,1)S(1)}, f32[1,128,1024]{2,1,0:T(8,128)S(1)}, bf16[256,6144]{1,0:T(8,128)(2,1)S(1)}, bf16[512,6144]{1,0:T(8,128)(2,1)S(1)}) custom-call(s32[1]{0:T(128)} %bitcast.refs_0_.place, bf16[1024,6144]{1,0:T(8,128)(2,1)} %refs_1_.13, bf16[256,6144]{1,0:T(8,128)(2,1)S(1)} %get-tuple-element.43.refs_2_, ...), custom_call_target="tpu_custom_call" | custom-call | flops 3221225472 | bytes 15728640 | tf_op jit(solution)/shard_map/pallas_call | solution.py:185
  18.9 3.6 %shard_map.58 = (bf16[1,128,1024]{2,1,0:T(8,128)(2,1)S(1)}, f32[1,128,1024]{2,1,0:T(8,128)S(1)}, bf16[512,6144]{1,0:T(8,128)(2,1)S(1)}) custom-call(s32[1]{0:T(128)} %bitcast.refs_0_.place, bf16[1024,6144]{1,0:T(8,128)(2,1)} %refs_1_.13, bf16[256,6144]{1,0:T(8,128)(2,1)S(1)} %get-tuple-element.48.refs_2_, bf16[1024,6144]{1,0:T(8,128)(2,1)S(1)} %get-tuple-element.40.refs_3_, ...), custom_call_target="tpu_custom_call" | custom-call | flops 3221225472 | bytes 15728640 | tf_op jit(solution)/shard_map/pallas_call | solution.py:185
  22.7 7.1 %shard_map.59 = (bf16[2,128,1024]{2,1,0:T(8,128)(2,1)S(1)}, f32[2,128,1024]{2,1,0:T(8,128)S(1)}, bf16[256,6144]{1,0:T(8,128)(2,1)S(1)}, bf16[1024,4096]{1,0:T(8,128)(2,1)S(1)}) custom-call(s32[1]{0:T(128)} %bitcast.refs_0_.place, bf16[1024,6144]{1,0:T(8,128)(2,1)} %refs_1_.13, bf16[512,6144]{1,0:T(8,128)(2,1)S(1)} %get-tuple-element.51.refs_2_, ...), custom_call_target="tpu_custom_call" | custom-call | flops 6442450944 | bytes 18874368 | tf_op jit(solution)/shard_map/pallas_call | solution.py:185
  29.8 0.6 collective-permute-start.10
  30.6 2.8 %collective-permute-start.5 = (bf16[128,1024]{1,0:T(8,128)(2,1)S(1)}, bf16[128,1024]{1,0:T(8,128)(2,1)S(1)}, u32[]{:S(2)}, u32[]{:S(2)}) collective-permute-start(bf16[128,1024]{1,0:T(8,128)(2,1)S(1)} %fusion.1.refs_5_), channel_id=1, source_target_pairs={{0,4},{1,5},{2,6},{3,7},{4,0},{5,1},{6,2},{7,3},{8,12},{9,13},{10,... | collective-permute-start | bytes 786440 | tf_op jit(solution)/shard_map/ppermute | solution.py:303
  33.4 10.9 %collective-permute-done.1.refs_0_ = bf16[128,1024]{1,0:T(8,128)(2,1)S(1)} collective-permute-done((bf16[128,1024]{1,0:T(8,128)(2,1)S(1)}, bf16[128,1024]{1,0:T(8,128)(2,1)S(1)}, u32[]{:S(2)}, u32[]{:S(2)}) %collective-permute-start.1) | collective-permute-done | bytes 262176 | tf_op jit(solution)/shard_map/ppermute | solution.py:303
  44.3 1.5 %shard_map.60 = (f32[128,1024]{1,0:T(8,128)S(1)}, bf16[128,1024]{1,0:T(8,128)(2,1)S(1)}, bf16[128,1024]{1,0:T(8,128)(2,1)S(1)}, bf16[128,1024]{1,0:T(8,128)(2,1)S(1)}) custom-call(s32[1]{0:T(128)} %bitcast.refs_0_.place, bf16[128,2,1024]{2,1,0:T(2,128)(2,1)S(1)} %copy-done, bf16[128,1024]{1,0:T(8,128)(2,1)S(1)} %collective-permute-done.1.refs_0_, ...), custom_call_target="tpu_custom_call" | custom-call | flops 1073741824 | bytes 8388608 | tf_op jit(solution)/shard_map/pallas_call | solution.py:262
  45.7 2.5 %collective-permute-start.9 = (bf16[128,1024]{1,0:T(8,128)(2,1)S(1)}, bf16[128,1024]{1,0:T(8,128)(2,1)S(1)}, u32[]{:S(2)}, u32[]{:S(2)}) collective-permute-start(bf16[128,1024]{1,0:T(8,128)(2,1)S(1)} %get-tuple-element.58), channel_id=1, source_target_pairs={{0,24},{8,16},{16,8},{24,0},{1,25},{9,17},{17,9},{25,1},{2,26},{10... | collective-permute-start | bytes 786440 | tf_op jit(solution)/shard_map/ppermute | solution.py:300
  48.3 0.5 collective-permute-start.8
  48.8 0.5 collective-permute-start.7
  49.4 2.7 %collective-permute-start.11 = (bf16[128,1024]{1,0:T(8,128)(2,1)S(1)}, bf16[128,1024]{1,0:T(8,128)(2,1)S(1)}, u32[]{:S(2)}, u32[]{:S(2)}) collective-permute-start(bf16[128,1024]{1,0:T(8,128)(2,1)S(1)} %fusion.4.refs_5_), channel_id=1, source_target_pairs={{0,2},{1,3},{2,0},{3,1},{4,6},{5,7},{6,4},{7,5},{8,10},{9,11},{10,... | collective-permute-start | bytes 786440 | tf_op jit(solution)/shard_map/ppermute | solution.py:303
  52.0 4.6 %shard_map.61 = (bf16[1,128,1024]{2,1,0:T(8,128)(2,1)S(1)}, f32[1,128,1024]{2,1,0:T(8,128)S(1)}, bf16[256,6144]{1,0:T(8,128)(2,1)S(1)}, bf16[1024,4096]{1,0:T(8,128)(2,1)S(1)}) custom-call(s32[1]{0:T(128)} %bitcast.refs_0_.place, bf16[1024,6144]{1,0:T(8,128)(2,1)} %refs_1_.13, bf16[256,6144]{1,0:T(8,128)(2,1)S(1)} %get-tuple-element.61.refs_2_, ...), custom_call_target="tpu_custom_call" | custom-call | flops 3221225472 | bytes 15728640 | tf_op jit(solution)/shard_map/pallas_call | solution.py:185
  56.7 3.1 %collective-permute-done.8 = bf16[128,1024]{1,0:T(8,128)(2,1)S(1)} collective-permute-done((bf16[128,1024]{1,0:T(8,128)(2,1)S(1)}, bf16[128,1024]{1,0:T(8,128)(2,1)S(1)}, u32[]{:S(2)}, u32[]{:S(2)}) %collective-permute-start.8) | collective-permute-done | bytes 262176 | tf_op jit(solution)/shard_map/ppermute | solution.py:300
  60.0 1.6 %collective-permute-start.16 = (bf16[128,1024]{1,0:T(8,128)(2,1)S(1)}, bf16[128,1024]{1,0:T(8,128)(2,1)S(1)}, u32[]{:S(2)}, u32[]{:S(2)}) collective-permute-start(bf16[128,1024]{1,0:T(8,128)(2,1)S(1)} %add_convert_fusion.2.refs_7_.refs_0_.first), channel_id=1, source_target_pairs={{0,8},{8,0},{16,24},{24,16},{1,9},{9,1},{17,25},{25,17},{2,10},{10... | collective-permute-start | bytes 786440 | tf_op jit(solution)/shard_map/ppermute | solution.py:300
  61.6 0.7 collective-permute-start.17
  62.3 1.3 %collective-permute-start.18 = (bf16[128,1024]{1,0:T(8,128)(2,1)S(1)}, bf16[128,1024]{1,0:T(8,128)(2,1)S(1)}, u32[]{:S(2)}, u32[]{:S(2)}) collective-permute-start(bf16[128,1024]{1,0:T(8,128)(2,1)S(1)} %add_convert_fusion.2.refs_7_.refs_0_.first), channel_id=1, source_target_pairs={{0,24},{8,16},{16,8},{24,0},{1,25},{9,17},{17,9},{25,1},{2,26},{10... | collective-permute-start | bytes 786440 | tf_op jit(solution)/shard_map/ppermute | solution.py:300
  63.7 1.7 %collective-permute-start.12 = (bf16[128,1024]{1,0:T(8,128)(2,1)S(1)}, bf16[128,1024]{1,0:T(8,128)(2,1)S(1)}, u32[]{:S(2)}, u32[]{:S(2)}) collective-permute-start(bf16[128,1024]{1,0:T(8,128)(2,1)S(1)} %fusion.refs_5_), channel_id=1, source_target_pairs={{0,4},{1,5},{2,6},{3,7},{4,0},{5,1},{6,2},{7,3},{8,12},{9,13},{10,... | collective-permute-start | bytes 786440 | tf_op jit(solution)/shard_map/ppermute | solution.py:303
  65.4 4.9 %collective-permute-start.14 = (bf16[128,1024]{1,0:T(8,128)(2,1)S(1)}, bf16[128,1024]{1,0:T(8,128)(2,1)S(1)}, u32[]{:S(2)}, u32[]{:S(2)}) collective-permute-start(bf16[128,1024]{1,0:T(8,128)(2,1)S(1)} %fusion.5.refs_6_), channel_id=1, source_target_pairs={{0,2},{1,3},{2,0},{3,1},{4,6},{5,7},{6,4},{7,5},{8,10},{9,11},{10,... | collective-permute-start | bytes 786440 | tf_op jit(solution)/shard_map/ppermute | solution.py:303
  70.3 3.6 %shard_map.62 = (bf16[1,128,1024]{2,1,0:T(8,128)(2,1)S(1)}, f32[1,128,1024]{2,1,0:T(8,128)S(1)}, bf16[1024,4096]{1,0:T(8,128)(2,1)S(1)}) custom-call(s32[1]{0:T(128)} %bitcast.refs_0_.place, bf16[1024,6144]{1,0:T(8,128)(2,1)} %refs_1_.13, bf16[256,6144]{1,0:T(8,128)(2,1)S(1)} %get-tuple-element.64.refs_2_, bf16[512,6144]{1,0:T(8,128)(2,1)S(1)} %get-tuple-element.52.refs_3_, ...), custom_call_target="tpu_custom_call" | custom-call | flops 3221225472 | bytes 15728640 | tf_op jit(solution)/shard_map/pallas_call | solution.py:185
  74.0 1.0 %collective-permute-done.17.refs_2_ = bf16[128,1024]{1,0:T(8,128)(2,1)S(1)} collective-permute-done((bf16[128,1024]{1,0:T(8,128)(2,1)S(1)}, bf16[128,1024]{1,0:T(8,128)(2,1)S(1)}, u32[]{:S(2)}, u32[]{:S(2)}) %collective-permute-start.17) | collective-permute-done | bytes 262176 | tf_op jit(solution)/shard_map/ppermute | solution.py:300
  75.0 2.2 %carry.1.refs_4_ = f32[128,1024]{1,0:T(8,128)S(1)} custom-call(s32[1]{0:T(128)} %bitcast.refs_0_.place, bf16[128,1024]{1,0:T(8,128)(2,1)S(1)} %add_convert_fusion.2.refs_7_.refs_0_.first, bf16[128,1024]{1,0:T(8,128)(2,1)S(1)} %collective-permute-done.16.refs_1_, bf16[128,1024]{1,0:T(8,128)(2,1)S(1)} %collective-permute-done.17.refs_2_, ...), custom_call_target="tpu_custom_call" | custom-call | flops 268435456 | bytes 1048576 | tf_op jit(solution)/shard_map/carry/pallas_call | solution.py:378
  77.2 0.4 collective-permute-done.12.refs_0_
  77.9 2.2 %shard_map.63 = (f32[128,1024]{1,0:T(8,128)S(1)}, bf16[128,1024]{1,0:T(8,128)(2,1)S(1)}, bf16[128,1024]{1,0:T(8,128)(2,1)S(1)}, bf16[128,1024]{1,0:T(8,128)(2,1)S(1)}) custom-call(s32[1]{0:T(128)} %bitcast.refs_0_.place, bf16[128,2,1024]{2,1,0:T(2,128)(2,1)S(1)} %copy-done, bf16[128,1024]{1,0:T(8,128)(2,1)S(1)} %collective-permute-done.12.refs_0_, ...), custom_call_target="tpu_custom_call" | custom-call | flops 2147483648 | bytes 16777216 | tf_op jit(solution)/shard_map/pallas_call | solution.py:262
  80.1 1.6 %collective-permute-start.19 = (bf16[128,1024]{1,0:T(8,128)(2,1)S(1)}, bf16[128,1024]{1,0:T(8,128)(2,1)S(1)}, u32[]{:S(2)}, u32[]{:S(2)}) collective-permute-start(bf16[128,1024]{1,0:T(8,128)(2,1)S(1)} %get-tuple-element.70), channel_id=1, source_target_pairs={{0,8},{8,0},{16,24},{24,16},{1,9},{9,1},{17,25},{25,17},{2,10},{10... | collective-permute-start | bytes 786440 | tf_op jit(solution)/shard_map/ppermute | solution.py:300
  82.0 1.6 %collective-permute-start.21 = (bf16[128,1024]{1,0:T(8,128)(2,1)S(1)}, bf16[128,1024]{1,0:T(8,128)(2,1)S(1)}, u32[]{:S(2)}, u32[]{:S(2)}) collective-permute-start(bf16[128,1024]{1,0:T(8,128)(2,1)S(1)} %get-tuple-element.72), channel_id=1, source_target_pairs={{0,24},{8,16},{16,8},{24,0},{1,25},{9,17},{17,9},{25,1},{2,26},{10... | collective-permute-start | bytes 786440 | tf_op jit(solution)/shard_map/ppermute | solution.py:300
  83.6 5.7 %collective-permute-done.19.refs_1_ = bf16[128,1024]{1,0:T(8,128)(2,1)S(1)} collective-permute-done((bf16[128,1024]{1,0:T(8,128)(2,1)S(1)}, bf16[128,1024]{1,0:T(8,128)(2,1)S(1)}, u32[]{:S(2)}, u32[]{:S(2)}) %collective-permute-start.19) | collective-permute-done | bytes 262176 | tf_op jit(solution)/shard_map/ppermute | solution.py:300
  89.3 4.8 %collective-permute-done.20.refs_2_ = bf16[128,1024]{1,0:T(8,128)(2,1)S(1)} collective-permute-done((bf16[128,1024]{1,0:T(8,128)(2,1)S(1)}, bf16[128,1024]{1,0:T(8,128)(2,1)S(1)}, u32[]{:S(2)}, u32[]{:S(2)}) %collective-permute-start.20) | collective-permute-done | bytes 262176 | tf_op jit(solution)/shard_map/ppermute | solution.py:300
  94.1 1.2 %result.1 = bf16[128,2,1024]{2,1,0:T(2,128)(2,1)} custom-call(bf16[128,1024]{1,0:T(8,128)(2,1)S(1)} %add_convert_fusion.2.refs_7_.refs_0_.first, f32[128,1024]{1,0:T(8,128)S(1)} %get-tuple-element.69.refs_0_, bf16[128,1024]{1,0:T(8,128)(2,1)S(1)} %collective-permute-done.19.refs_1_, bf16[128,1024]{1,0:T(8,128)(2,1)S(1)} %collective-permute-done.20.refs_2_, ...), custom_call_target="tpu_custom_call" | custom-call | tf_op jit(solution)/shard_map/result/pallas_call | solution.py:397
  (32 shorter events, 1.8 us)
Async XLA Ops:
  7.0 4.6 %collective-permute-start.2 = (bf16[1,128,1024]{2,1,0:T(8,128)(2,1)S(1)}, bf16[1,128,1024]{2,1,0:T(8,128)(2,1)S(1)}, u32[]{:S(2)}, u32[]{:S(2)}) collective-permute-start(bf16[1,128,1024]{2,1,0:T(8,128)(2,1)S(1)} %get-tuple-element.45), channel_id=1, source_target_pairs={{0,1},{1,0},{2,3},{3,2},{4,5},{5,4},{6,7},{7,6},{8,9},{9,8},{10,11... | collective-permute-start | bytes 786440 | tf_op jit(solution)/shard_map/ppermute | solution.py:303
  11.5 7.3 %collective-permute-start = (bf16[1,128,1024]{2,1,0:T(8,128)(2,1)S(1)}, bf16[1,128,1024]{2,1,0:T(8,128)(2,1)S(1)}, u32[]{:S(2)}, u32[]{:S(2)}) collective-permute-start(bf16[1,128,1024]{2,1,0:T(8,128)(2,1)S(1)} %get-tuple-element.42), channel_id=1, source_target_pairs={{0,1},{1,0},{2,3},{3,2},{4,5},{5,4},{6,7},{7,6},{8,9},{9,8},{10,11... | collective-permute-start | bytes 786440 | tf_op jit(solution)/shard_map/ppermute | solution.py:303
  11.7 10.9 %collective-permute-start.4 = (bf16[128,1024]{1,0:T(8,128)(2,1)S(1)}, bf16[128,1024]{1,0:T(8,128)(2,1)S(1)}, u32[]{:S(2)}, u32[]{:S(2)}) collective-permute-start(bf16[128,1024]{1,0:T(8,128)(2,1)S(1)} %fusion.3.refs_4_), channel_id=1, source_target_pairs={{0,2},{1,3},{2,0},{3,1},{4,6},{5,7},{6,4},{7,5},{8,10},{9,11},{10,... | collective-permute-start | bytes 786440 | tf_op jit(solution)/shard_map/ppermute | solution.py:303
  18.7 3.8 %collective-permute-start.3 = (bf16[1,128,1024]{2,1,0:T(8,128)(2,1)S(1)}, bf16[1,128,1024]{2,1,0:T(8,128)(2,1)S(1)}, u32[]{:S(2)}, u32[]{:S(2)}) collective-permute-start(bf16[1,128,1024]{2,1,0:T(8,128)(2,1)S(1)} %get-tuple-element.47), channel_id=1, source_target_pairs={{0,1},{1,0},{2,3},{3,2},{4,5},{5,4},{6,7},{7,6},{8,9},{9,8},{10,11... | collective-permute-start | bytes 786440 | tf_op jit(solution)/shard_map/ppermute | solution.py:303
  22.6 21.6 %copy-start = (bf16[128,2,1024]{2,1,0:T(2,128)(2,1)S(1)}, bf16[128,2,1024]{2,1,0:T(2,128)(2,1)}, u32[]{:S(2)}) copy-start(bf16[128,2,1024]{2,1,0:T(2,128)(2,1)} %rhs.3) | copy-start | bytes 1572868
  29.8 19.5 %collective-permute-start.10 = (bf16[2,128,1024]{2,1,0:T(8,128)(2,1)S(1)}, bf16[2,128,1024]{2,1,0:T(8,128)(2,1)S(1)}, u32[]{:S(2)}, u32[]{:S(2)}) collective-permute-start(bf16[2,128,1024]{2,1,0:T(8,128)(2,1)S(1)} %get-tuple-element.60), channel_id=1, source_target_pairs={{0,1},{1,0},{2,3},{3,2},{4,5},{5,4},{6,7},{7,6},{8,9},{9,8},{10,11... | collective-permute-start | bytes 1572872 | tf_op jit(solution)/shard_map/ppermute | solution.py:303
  30.3 13.9 %collective-permute-start.1 = (bf16[128,1024]{1,0:T(8,128)(2,1)S(1)}, bf16[128,1024]{1,0:T(8,128)(2,1)S(1)}, u32[]{:S(2)}, u32[]{:S(2)}) collective-permute-start(bf16[128,1024]{1,0:T(8,128)(2,1)S(1)} %fusion.2.refs_4_), channel_id=1, source_target_pairs={{0,2},{1,3},{2,0},{3,1},{4,6},{5,7},{6,4},{7,5},{8,10},{9,11},{10,... | collective-permute-start | bytes 786440 | tf_op jit(solution)/shard_map/ppermute | solution.py:303
  30.4 13.8 %collective-permute-start.6 = (bf16[1,128,1024]{2,1,0:T(8,128)(2,1)S(1)}, bf16[1,128,1024]{2,1,0:T(8,128)(2,1)S(1)}, u32[]{:S(2)}, u32[]{:S(2)}) collective-permute-start(bf16[1,128,1024]{2,1,0:T(8,128)(2,1)S(1)} %get-tuple-element.50), channel_id=1, source_target_pairs={{0,1},{1,0},{2,3},{3,2},{4,5},{5,4},{6,7},{7,6},{8,9},{9,8},{10,11... | collective-permute-start | bytes 786440 | tf_op jit(solution)/shard_map/ppermute | solution.py:303
  30.6 13.7 %collective-permute-start.5 = (bf16[128,1024]{1,0:T(8,128)(2,1)S(1)}, bf16[128,1024]{1,0:T(8,128)(2,1)S(1)}, u32[]{:S(2)}, u32[]{:S(2)}) collective-permute-start(bf16[128,1024]{1,0:T(8,128)(2,1)S(1)} %fusion.1.refs_5_), channel_id=1, source_target_pairs={{0,4},{1,5},{2,6},{3,7},{4,0},{5,1},{6,2},{7,3},{8,12},{9,13},{10,... | collective-permute-start | bytes 786440 | tf_op jit(solution)/shard_map/ppermute | solution.py:303
  45.7 10.9 %collective-permute-start.9 = (bf16[128,1024]{1,0:T(8,128)(2,1)S(1)}, bf16[128,1024]{1,0:T(8,128)(2,1)S(1)}, u32[]{:S(2)}, u32[]{:S(2)}) collective-permute-start(bf16[128,1024]{1,0:T(8,128)(2,1)S(1)} %get-tuple-element.58), channel_id=1, source_target_pairs={{0,24},{8,16},{16,8},{24,0},{1,25},{9,17},{17,9},{25,1},{2,26},{10... | collective-permute-start | bytes 786440 | tf_op jit(solution)/shard_map/ppermute | solution.py:300
  48.3 11.5 %collective-permute-start.8 = (bf16[128,1024]{1,0:T(8,128)(2,1)S(1)}, bf16[128,1024]{1,0:T(8,128)(2,1)S(1)}, u32[]{:S(2)}, u32[]{:S(2)}) collective-permute-start(bf16[128,1024]{1,0:T(8,128)(2,1)S(1)} %get-tuple-element.57), channel_id=1, source_target_pairs={{0,16},{8,24},{16,0},{24,8},{1,17},{9,25},{17,1},{25,9},{2,18},{10... | collective-permute-start | bytes 786440 | tf_op jit(solution)/shard_map/ppermute | solution.py:300
  48.8 11.1 %collective-permute-start.7 = (bf16[128,1024]{1,0:T(8,128)(2,1)S(1)}, bf16[128,1024]{1,0:T(8,128)(2,1)S(1)}, u32[]{:S(2)}, u32[]{:S(2)}) collective-permute-start(bf16[128,1024]{1,0:T(8,128)(2,1)S(1)} %get-tuple-element.56.refs_6_), channel_id=1, source_target_pairs={{0,8},{8,0},{16,24},{24,16},{1,9},{9,1},{17,25},{25,17},{2,10},{10... | collective-permute-start | bytes 786440 | tf_op jit(solution)/shard_map/ppermute | solution.py:300
  49.4 14.2 %collective-permute-start.11 = (bf16[128,1024]{1,0:T(8,128)(2,1)S(1)}, bf16[128,1024]{1,0:T(8,128)(2,1)S(1)}, u32[]{:S(2)}, u32[]{:S(2)}) collective-permute-start(bf16[128,1024]{1,0:T(8,128)(2,1)S(1)} %fusion.4.refs_5_), channel_id=1, source_target_pairs={{0,2},{1,3},{2,0},{3,1},{4,6},{5,7},{6,4},{7,5},{8,10},{9,11},{10,... | collective-permute-start | bytes 786440 | tf_op jit(solution)/shard_map/ppermute | solution.py:303
  56.6 8.8 %collective-permute-start.13 = (bf16[1,128,1024]{2,1,0:T(8,128)(2,1)S(1)}, bf16[1,128,1024]{2,1,0:T(8,128)(2,1)S(1)}, u32[]{:S(2)}, u32[]{:S(2)}) collective-permute-start(bf16[1,128,1024]{2,1,0:T(8,128)(2,1)S(1)} %get-tuple-element.63), channel_id=1, source_target_pairs={{0,1},{1,0},{2,3},{3,2},{4,5},{5,4},{6,7},{7,6},{8,9},{9,8},{10,11... | collective-permute-start | bytes 786440 | tf_op jit(solution)/shard_map/ppermute | solution.py:303
  60.0 13.9 %collective-permute-start.16 = (bf16[128,1024]{1,0:T(8,128)(2,1)S(1)}, bf16[128,1024]{1,0:T(8,128)(2,1)S(1)}, u32[]{:S(2)}, u32[]{:S(2)}) collective-permute-start(bf16[128,1024]{1,0:T(8,128)(2,1)S(1)} %add_convert_fusion.2.refs_7_.refs_0_.first), channel_id=1, source_target_pairs={{0,8},{8,0},{16,24},{24,16},{1,9},{9,1},{17,25},{25,17},{2,10},{10... | collective-permute-start | bytes 786440 | tf_op jit(solution)/shard_map/ppermute | solution.py:300
  61.6 13.5 %collective-permute-start.17 = (bf16[128,1024]{1,0:T(8,128)(2,1)S(1)}, bf16[128,1024]{1,0:T(8,128)(2,1)S(1)}, u32[]{:S(2)}, u32[]{:S(2)}) collective-permute-start(bf16[128,1024]{1,0:T(8,128)(2,1)S(1)} %add_convert_fusion.2.refs_7_.refs_0_.first), channel_id=1, source_target_pairs={{0,16},{8,24},{16,0},{24,8},{1,17},{9,25},{17,1},{25,9},{2,18},{10... | collective-permute-start | bytes 786440 | tf_op jit(solution)/shard_map/ppermute | solution.py:300
  62.3 14.9 %collective-permute-start.18 = (bf16[128,1024]{1,0:T(8,128)(2,1)S(1)}, bf16[128,1024]{1,0:T(8,128)(2,1)S(1)}, u32[]{:S(2)}, u32[]{:S(2)}) collective-permute-start(bf16[128,1024]{1,0:T(8,128)(2,1)S(1)} %add_convert_fusion.2.refs_7_.refs_0_.first), channel_id=1, source_target_pairs={{0,24},{8,16},{16,8},{24,0},{1,25},{9,17},{17,9},{25,1},{2,26},{10... | collective-permute-start | bytes 786440 | tf_op jit(solution)/shard_map/ppermute | solution.py:300
  63.7 14.0 %collective-permute-start.12 = (bf16[128,1024]{1,0:T(8,128)(2,1)S(1)}, bf16[128,1024]{1,0:T(8,128)(2,1)S(1)}, u32[]{:S(2)}, u32[]{:S(2)}) collective-permute-start(bf16[128,1024]{1,0:T(8,128)(2,1)S(1)} %fusion.refs_5_), channel_id=1, source_target_pairs={{0,4},{1,5},{2,6},{3,7},{4,0},{5,1},{6,2},{7,3},{8,12},{9,13},{10,... | collective-permute-start | bytes 786440 | tf_op jit(solution)/shard_map/ppermute | solution.py:303
  65.4 12.4 %collective-permute-start.14 = (bf16[128,1024]{1,0:T(8,128)(2,1)S(1)}, bf16[128,1024]{1,0:T(8,128)(2,1)S(1)}, u32[]{:S(2)}, u32[]{:S(2)}) collective-permute-start(bf16[128,1024]{1,0:T(8,128)(2,1)S(1)} %fusion.5.refs_6_), channel_id=1, source_target_pairs={{0,2},{1,3},{2,0},{3,1},{4,6},{5,7},{6,4},{7,5},{8,10},{9,11},{10,... | collective-permute-start | bytes 786440 | tf_op jit(solution)/shard_map/ppermute | solution.py:303
  73.9 3.9 %collective-permute-start.15 = (bf16[1,128,1024]{2,1,0:T(8,128)(2,1)S(1)}, bf16[1,128,1024]{2,1,0:T(8,128)(2,1)S(1)}, u32[]{:S(2)}, u32[]{:S(2)}) collective-permute-start(bf16[1,128,1024]{2,1,0:T(8,128)(2,1)S(1)} %get-tuple-element.66), channel_id=1, source_target_pairs={{0,1},{1,0},{2,3},{3,2},{4,5},{5,4},{6,7},{7,6},{8,9},{9,8},{10,11... | collective-permute-start | bytes 786440 | tf_op jit(solution)/shard_map/ppermute | solution.py:303
  80.1 9.2 %collective-permute-start.19 = (bf16[128,1024]{1,0:T(8,128)(2,1)S(1)}, bf16[128,1024]{1,0:T(8,128)(2,1)S(1)}, u32[]{:S(2)}, u32[]{:S(2)}) collective-permute-start(bf16[128,1024]{1,0:T(8,128)(2,1)S(1)} %get-tuple-element.70), channel_id=1, source_target_pairs={{0,8},{8,0},{16,24},{24,16},{1,9},{9,1},{17,25},{25,17},{2,10},{10... | collective-permute-start | bytes 786440 | tf_op jit(solution)/shard_map/ppermute | solution.py:300
  81.6 12.4 %collective-permute-start.20 = (bf16[128,1024]{1,0:T(8,128)(2,1)S(1)}, bf16[128,1024]{1,0:T(8,128)(2,1)S(1)}, u32[]{:S(2)}, u32[]{:S(2)}) collective-permute-start(bf16[128,1024]{1,0:T(8,128)(2,1)S(1)} %get-tuple-element.71), channel_id=1, source_target_pairs={{0,16},{8,24},{16,0},{24,8},{1,17},{9,25},{17,1},{25,9},{2,18},{10... | collective-permute-start | bytes 786440 | tf_op jit(solution)/shard_map/ppermute | solution.py:300
  82.0 12.1 %collective-permute-start.21 = (bf16[128,1024]{1,0:T(8,128)(2,1)S(1)}, bf16[128,1024]{1,0:T(8,128)(2,1)S(1)}, u32[]{:S(2)}, u32[]{:S(2)}) collective-permute-start(bf16[128,1024]{1,0:T(8,128)(2,1)S(1)} %get-tuple-element.72), channel_id=1, source_target_pairs={{0,24},{8,16},{16,8},{24,0},{1,25},{9,17},{17,9},{25,1},{2,26},{10... | collective-permute-start | bytes 786440 | tf_op jit(solution)/shard_map/ppermute | solution.py:300
